TPU v7x, 128 devices: a whole 4x4x4 slice. The times are simulated.
128 devices in a mesh: coil: 8 (over x, z_lo), slab: 16 (over y, z_hi, core).
Axes of the slice: x: 4, y: 4, z: 4 (z_hi: 2, z_lo: 2; z = z_hi * 2 + z_lo), core: 2. Of those that a mesh axis runs over, the one named last changes fastest.
Arguments:
- coil_maps: float32 [8, 2, 16, 256, 128], P('coil', None, 'slab'), may hold values from -1.5 to 1.5
- kspace: float32 [8, 2, 16, 256, 128], P('coil', None, 'slab'), may hold values from -6 to 6
- sample_mask: int32 [256, 128], replicated, may hold values 0 or 1
- iterate: float32 [2, 16, 256, 128], P(None, 'slab', 'coil'), may hold values from -6 to 6
- probe_bits: int32 [2, 16, 256, 128], P(None, 'slab', 'coil'), may hold values from 0 to 1
- loss_gradient: float32 [2, 16, 256, 128], P(None, 'slab', 'coil'), may hold values from -6 to 6
- adjoint: float32 [2, 16, 256, 128], P(None, 'slab', 'coil'), may hold values from -6 to 6
- kernel_first: bfloat16 [24, 2, 3, 3, 3], replicated, may hold values from -0.875 to 0.875
- kernel_second: bfloat16 [24, 24, 3, 3, 3], replicated, may hold values from -0.25 to 0.25
- kernel_last: bfloat16 [2, 24, 3, 3, 3], replicated, may hold values from -0.25 to 0.25
Outputs:
- new_iterate: float32 [2, 16, 256, 128], P(None, 'slab', 'coil')
- probe_pullback: float32 [2, 16, 256, 128], P(None, 'slab', 'coil')
- adjoint_next: float32 [2, 16, 256, 128], P(None, 'slab', 'coil')
Inputs may be any that keep to these rules, and one draw needn't show every extreme that they name: `sample_mask`: 1 marks a sampled phase-encode line. `probe_bits`: the probe's sign is 2 p - 1.
All inputs are finite; a program needn't handle non-finite values.
Results may differ from a plain program's by a relative error of at most 0.0055.
Values may be sent and summed in bfloat16 or wider, within the bound.
No kernel may reach another device: no remote copies, remote signals or barrier semaphores. Data moves between devices by JAX's collectives and lax.ppermute only.
A program may use at most 128 MiB of HBM per device.

v0:
```python
import math

import jax
import jax.numpy as jnp
from jax import lax
from jax.sharding import PartitionSpec as P

step_size = 0.8
kernel_layout = ("NCDHW", "OIDHW", "NCDHW")


def with_halo(cells, sides, width):
    for axis, dim in sides:
        count = lax.axis_size(axis)
        ends = count - 1
        head = lax.slice_in_dim(cells, 0, width, axis=dim)
        tail = lax.slice_in_dim(cells, cells.shape[dim] - width, cells.shape[dim], axis=dim)
        cells = jnp.concatenate(
            [
                lax.ppermute(tail, axis, [(i, (i + 1) % count) for i in range(ends)]),
                cells,
                lax.ppermute(head, axis, [((i + 1) % count, i) for i in range(ends)]),
            ],
            axis=dim,
        )
    return cells


def fourier_table(length, inverse):
    counter = jnp.arange(length, dtype=jnp.int32)
    phase_index = counter[:, None] * counter[None, :] % length
    angles = phase_index.astype(jnp.float32) * (2.0 * math.pi / length)
    norm_scale = 1.0 / math.sqrt(length)
    sine_sign = 1.0 if inverse else -1.0
    return (jnp.cos(angles) * norm_scale, sine_sign * jnp.sin(angles) * norm_scale)


def spectrum(real_part, imag_part, tables):
    height_cos, height_sin, depth_cos, depth_sin = tables
    highest = lax.Precision.HIGHEST
    along_real = jnp.einsum("...z,zw->...w", real_part, depth_cos, precision=highest) - jnp.einsum(
        "...z,zw->...w", imag_part, depth_sin, precision=highest
    )
    along_imag = jnp.einsum("...z,zw->...w", real_part, depth_sin, precision=highest) + jnp.einsum(
        "...z,zw->...w", imag_part, depth_cos, precision=highest
    )
    final_real = jnp.einsum(
        "yv,...vz->...yz", height_cos, along_real, precision=highest
    ) - jnp.einsum("yv,...vz->...yz", height_sin, along_imag, precision=highest)
    final_imag = jnp.einsum(
        "yv,...vz->...yz", height_sin, along_real, precision=highest
    ) + jnp.einsum("yv,...vz->...yz", height_cos, along_imag, precision=highest)
    return (final_real, final_imag)


def coil_partial(field, coil_maps, kspace, mask_weight, forward_tables, inverse_tables, with_data):
    field_real = field[:, 0]
    field_imag = field[:, 1]
    running = jnp.zeros(field.shape, jnp.float32)
    map_real = coil_maps[0, 0]
    map_imag = coil_maps[0, 1]
    coil_real = map_real * field_real - map_imag * field_imag
    coil_imag = map_real * field_imag + map_imag * field_real
    freq_real, freq_imag = spectrum(coil_real, coil_imag, forward_tables)
    freq_real = mask_weight * freq_real
    freq_imag = mask_weight * freq_imag
    if with_data:
        freq_real = freq_real - mask_weight * kspace[0, 0]
        freq_imag = freq_imag - mask_weight * kspace[0, 1]
    back_real, back_imag = spectrum(freq_real, freq_imag, inverse_tables)
    running = running + jnp.stack(
        [map_real * back_real + map_imag * back_imag, map_real * back_imag - map_imag * back_real],
        axis=1,
    )
    return running


def convolve_local(haloed, kernel):
    return lax.conv_general_dilated(
        haloed,
        kernel,
        (1, 1, 1),
        ((0, 0), (0, 0), (1, 1)),
        dimension_numbers=kernel_layout,
        preferred_element_type=jnp.float32,
    )


def transposed(kernel):
    return jnp.swapaxes(jnp.flip(kernel, (2, 3, 4)), 0, 1)


def silu_slope(preact):
    sigmoid_value = jax.nn.sigmoid(preact)
    return sigmoid_value * (1.0 + preact * (1.0 - sigmoid_value))


def feature_border(values):
    return with_halo(values, (("coil", 3), ("slab", 2)), 1)


def border_apart(values):
    return with_halo(values, (("coil", 3), ("slab", 2)), 1)


def on_device(
    coil_maps,
    kspace,
    sample_mask,
    iterate,
    probe_bits,
    loss_gradient,
    adjoint,
    kernel_first,
    kernel_second,
    kernel_last,
):
    height = sample_mask.shape[0]
    depth = sample_mask.shape[1]
    forward_tables = fourier_table(height, False) + fourier_table(depth, False)
    inverse_tables = fourier_table(height, True) + fourier_table(depth, True)
    mask_weight = sample_mask.astype(jnp.float32)
    row_count = iterate.shape[2]
    gathered = lax.all_gather(iterate.astype(jnp.bfloat16), "coil", axis=2, tiled=True).astype(
        iterate.dtype
    )
    partial_sum = coil_partial(
        gathered[None], coil_maps, kspace, mask_weight, forward_tables, inverse_tables, True
    )[0]
    summed = lax.psum(partial_sum, "coil")
    my_share = lax.dynamic_slice_in_dim(summed, lax.axis_index("coil") * row_count, row_count, 2)
    relaxed = iterate - step_size * my_share
    activation = relaxed.astype(jnp.bfloat16)[None]
    preacts = []
    for kernel in (kernel_first, kernel_second):
        preact = convolve_local(feature_border(activation), kernel)
        preacts.append(preact)
        activation = jax.nn.silu(preact).astype(jnp.bfloat16)
    new_iterate = relaxed + convolve_local(feature_border(activation), kernel_last)[0]

    def pullback(cotangent, border):
        grad_field = convolve_local(border(cotangent.astype(jnp.bfloat16)), transposed(kernel_last))
        for kernel, preact in ((kernel_second, preacts[1]), (kernel_first, preacts[0])):
            grad_field = (grad_field * silu_slope(preact)).astype(jnp.bfloat16)
            grad_field = convolve_local(border(grad_field), transposed(kernel))
        return cotangent + grad_field

    sign_field = (2 * probe_bits - 1).astype(jnp.float32)
    pulled = jnp.concatenate(
        [pullback(sign_field[None], border_apart), pullback(adjoint[None], border_apart)]
    )
    spread = lax.all_gather(pulled.astype(jnp.bfloat16), "coil", axis=3, tiled=True).astype(
        pulled.dtype
    )
    back_partial = coil_partial(
        spread, coil_maps, kspace, mask_weight, forward_tables, inverse_tables, False
    )
    back_summed = lax.psum(back_partial.astype(jnp.bfloat16), "coil").astype(jnp.float32)
    back_share = lax.dynamic_slice_in_dim(
        back_summed, lax.axis_index("coil") * row_count, row_count, 3
    )
    result = pulled - step_size * back_share
    return (new_iterate, result[0], loss_gradient + result[1])


def solution(mesh):
    in_specs = (
        P("coil", None, "slab", None, None),
        P("coil", None, "slab", None, None),
        P(),
        P(None, "slab", "coil", None),
        P(None, "slab", "coil", None),
        P(None, "slab", "coil", None),
        P(None, "slab", "coil", None),
        P(),
        P(),
        P(),
    )
    out_specs = (
        P(None, "slab", "coil", None),
        P(None, "slab", "coil", None),
        P(None, "slab", "coil", None),
    )
    return jax.shard_map(
        on_device, mesh=mesh, in_specs=in_specs, out_specs=out_specs, check_vma=False
    )
```

profile of v0, /device:TPU:0, one launch (start us, length us, event | category | flops | bytes accessed | tf_op | source)
XLA Modules:
  0.0 676.6 jit_solution(4032366645207725723)
XLA Ops:
  7.2 1.7 slice_bitcast_fusion.23
  10.0 28.3 %all_gather.6 = bf16[2,1,256,128]{3,0,1,2:T(2,128)(2,1)S(1)} all-gather(bf16[2,1,32,128]{3,0,1,2:T(2,128)(2,1)S(1)} %copy.525), channel_id=1, replica_groups=mesh['coil'=8,'slab'=16] {'coil'}, dimensions={2}, use_global_device_ids=true | all-gather | bytes 147456 | tf_op jit(solution)/shard_map/all_gather | solution.py:124
  49.7 1.6 fusion.152
  53.2 1.4 fusion.130
  55.4 3.8 collective-permute-start.24
  60.6 4.5 collective-permute-start.12
  68.6 3.0 collective-permute-start.26
  71.6 59.6 %all-reduce.3.cloned.1.call-done = f32[2,1,256,128]{2,3,0,1:T(8,128)} async-done(((f32[2,1,256,128]{2,3,0,1:T(8,128)}), f32[2,1,256,128]{2,3,0,1:T(8,128)}) %all-reduce.3.cloned.1.call-update) | async-done | bytes 262160 | tf_op jit(solution)/shard_map/psum | solution.py:130
  133.7 4.5 collective-permute-start
  138.6 1.5 collective-permute-done
  141.5 3.0 collective-permute-start.2
  147.6 5.8 multiply_convert_fusion.5
  156.5 4.9 collective-permute-start.4
  162.0 4.1 collective-permute-start.14
  167.5 7.1 %collective-permute-start.6 = (bf16[1,24,1,34,128]{4,1,3,2,0:T(8,128)(2,1)S(1)}, bf16[1,24,1,34,128]{4,1,3,2,0:T(8,128)(2,1)S(1)}, u32[]{:S(2)}, u32[]{:S(2)}) collective-permute-start(bf16[1,24,1,34,128]{4,1,3,2,0:T(8,128)(2,1)S(1)} %pad_maximum_fusion.7), channel_id=1, source_target_pairs={{0,1},{1,2},{2,3},{3,4},{4,5},{5,6},{6,7},{7,8},{8,9},{9,10},{10,1... | collective-permute-start | bytes 626696 | tf_op jit(solution)/shard_map/ppermute | solution.py:20
  178.1 2.7 copy.381
  180.8 2.1 pad.2
  182.9 8.5 %copy.383 = bf16[24,3,34,1,8,17]{0,4,5,2,1,3:T(8,128)(2,1)} copy(bf16[24,3,34,1,8,17]{2,0,5,4,1,3:T(8,128)(2,1)S(1)} %bitcast.429) | data formatting | bytes 1331712 | tf_op jit(solution)/shard_map/conv_general_dilated | solution.py:79
  192.6 8.0 %multiply_convert_fusion.4 = (bf16[1,32,8,17,24]{4,2,3,1,0:T(8,128)(2,1)S(1)}, f32[1,32,8,17,24]{4,2,3,1,0:T(8,128)}) fusion(pred[8,17]{0,1:T(8,128)(4,1)S(1)} %copy-done.40, bf16[24,24,3,3,3]{1,0,4,3,2:T(8,128)(2,1)S(1)} %copy-done, bf16[24,3,34,1,7,2]{0,4,5,2,1,3:T(8,128)(2,1)S(1)} %slice.166, bf16[24,3,34,1,8,17]{0,4,5,2,1,3:T(8,128)(2,1)} %copy.383), kind=kOutput, calls=%fused_computation.39 | convolution fusion | flops 138223872 | bytes 1392328 | tf_op jit(solution)/shard_map/conv_general_dilated | solution.py:79
  202.5 6.6 multiply_convert_fusion.1
  210.7 2.2 copy.428
  212.9 6.5 multiply_convert_fusion.3
  220.4 2.0 copy.402
  226.9 4.8 collective-permute-start.8
  235.3 5.4 collective-permute-start.28
  243.7 5.4 collective-permute-start.16
  250.5 4.6 collective-permute-start.30
  257.2 9.2 %collective-permute-start.10 = (bf16[1,24,1,34,128]{4,1,3,2,0:T(8,128)(2,1)}, bf16[1,24,1,34,128]{4,1,3,2,0:T(8,128)(2,1)}, u32[]{:S(2)}, u32[]{:S(2)}) collective-permute-start(bf16[1,24,1,34,128]{4,1,3,2,0:T(8,128)(2,1)} %pad_maximum_fusion.8), channel_id=1, source_target_pairs={{0,1},{1,2},{2,3},{3,4},{4,5},{5,6},{6,7},{7,8},{8,9},{9,10},{10,1... | collective-permute-start | bytes 626696 | tf_op jit(solution)/shard_map/ppermute | solution.py:20
  268.5 5.9 collective-permute-start.18
  274.4 2.9 copy.433
  277.3 2.1 pad.14
  279.5 8.5 %copy.435 = bf16[24,3,34,1,8,17]{0,4,5,2,1,3:T(8,128)(2,1)} copy(bf16[24,3,34,1,8,17]{2,0,5,4,1,3:T(8,128)(2,1)S(1)} %bitcast.430) | data formatting | bytes 1331712 | tf_op jit(solution)/shard_map/conv_general_dilated | solution.py:79
  289.2 8.1 %multiply_convert_fusion = bf16[1,32,8,17,24]{4,2,3,1,0:T(8,128)(2,1)S(1)} fusion(bf16[24,24,3,3,3]{1,0,4,3,2:T(8,128)(2,1)S(1)} %copy-done, bf16[24,3,34,1,7,2]{0,4,5,2,1,3:T(8,128)(2,1)S(1)} %slice.198, bf16[24,3,34,1,8,17]{0,4,5,2,1,3:T(8,128)(2,1)} %copy.435, pred[8,17]{0,1:T(8,128)(4,1)S(1)} %copy-done.40, f32[1,32,8,17,24]{4,2,3,1,0:T(8,128)} %get-tuple-element.53), kind=kOutput, calls=%fused_computation.34 | convolution fusion | flops 138746112 | bytes 1392328 | tf_op jit(solution)/shard_map/conv_general_dilated | solution.py:79
  300.2 2.7 copy.407
  302.9 2.1 pad.8
  305.1 8.9 %copy.409 = bf16[24,3,34,1,8,17]{0,4,5,2,1,3:T(8,128)(2,1)} copy(bf16[24,3,34,1,8,17]{2,0,5,4,1,3:T(8,128)(2,1)S(1)} %bitcast.431) | data formatting | bytes 1331712 | tf_op jit(solution)/shard_map/conv_general_dilated | solution.py:79
  315.1 8.1 %multiply_convert_fusion.2 = bf16[1,32,8,17,24]{4,2,3,1,0:T(8,128)(2,1)S(1)} fusion(bf16[24,24,3,3,3]{1,0,4,3,2:T(8,128)(2,1)S(1)} %copy-done, bf16[24,3,34,1,7,2]{0,4,5,2,1,3:T(8,128)(2,1)S(1)} %slice.182, bf16[24,3,34,1,8,17]{0,4,5,2,1,3:T(8,128)(2,1)} %copy.409, pred[8,17]{0,1:T(8,128)(4,1)} %constant.113, f32[1,32,8,17,24]{4,2,3,1,0:T(8,128)} %get-tuple-element.53), kind=kOutput, calls=%fused_computation.36 | convolution fusion | flops 138746112 | bytes 1392328 | tf_op jit(solution)/shard_map/conv_general_dilated | solution.py:79
  326.4 4.8 collective-permute-start.32
  333.7 5.4 collective-permute-start.20
  341.2 5.0 collective-permute-start.34
  347.3 2.7 copy.390
  350.0 2.1 pad.4
  352.2 8.5 %copy.392 = bf16[24,3,34,1,8,17]{0,4,5,2,1,3:T(8,128)(2,1)} copy(bf16[24,3,34,1,8,17]{2,0,5,4,1,3:T(8,128)(2,1)S(1)} %bitcast.432) | data formatting | bytes 1331712 | tf_op jit(solution)/shard_map/conv_general_dilated | solution.py:79
  360.7 2.0 slice.172
  364.5 5.1 collective-permute-start.22
  370.8 2.7 copy.442
  373.5 2.1 pad.16
  375.7 8.5 %copy.444 = bf16[24,3,34,1,8,17]{0,4,5,2,1,3:T(8,128)(2,1)} copy(bf16[24,3,34,1,8,17]{2,0,5,4,1,3:T(8,128)(2,1)S(1)} %bitcast.433) | data formatting | bytes 1331712 | tf_op jit(solution)/shard_map/conv_general_dilated | solution.py:79
  385.3 70.1 %fusion.76 = f32[1,32,8,17,2]{2,4,3,1,0:T(2,128)S(1)} fusion(bf16[24,2,3,3,3]{0,1,4,3,2:T(2,128)(2,1)S(1)} %copy-done.37, bf16[24,3,34,1,7,2]{0,4,5,2,1,3:T(8,128)(2,1)S(1)} %slice.204, bf16[24,3,34,1,8,17]{0,4,5,2,1,3:T(8,128)(2,1)} %copy.444, pred[8,17]{0,1:T(8,128)(4,1)S(1)} %copy-done.41), kind=kOutput, calls=%fused_computation.90 | convolution fusion | flops 13521664 | bytes 771944 | tf_op jit(solution)/shard_map/conv_general_dilated | solution.py:79
  455.9 3.1 copy.416
  459.1 2.1 pad.10
  461.2 8.5 %copy.418 = bf16[24,3,34,1,8,17]{0,4,5,2,1,3:T(8,128)(2,1)} copy(bf16[24,3,34,1,8,17]{2,0,5,4,1,3:T(8,128)(2,1)S(1)} %bitcast.428) | data formatting | bytes 1331712 | tf_op jit(solution)/shard_map/conv_general_dilated | solution.py:79
  470.9 70.0 %fusion.73 = f32[1,32,8,17,2]{2,4,3,1,0:T(2,128)S(1)} fusion(bf16[24,2,3,3,3]{0,1,4,3,2:T(2,128)(2,1)S(1)} %copy-done.37, bf16[24,3,34,1,7,2]{0,4,5,2,1,3:T(8,128)(2,1)S(1)} %slice.188, bf16[24,3,34,1,8,17]{0,4,5,2,1,3:T(8,128)(2,1)} %copy.418, pred[8,17]{0,1:T(8,128)(4,1)S(1)} %copy-done.41), kind=kOutput, calls=%fused_computation.89 | convolution fusion | flops 13521664 | bytes 771944 | tf_op jit(solution)/shard_map/conv_general_dilated | solution.py:79
  541.3 28.6 %all_gather.7 = bf16[2,2,1,256,128]{4,1,2,0,3:T(2,128)(2,1)S(1)} all-gather(bf16[2,2,1,32,128]{4,1,2,0,3:T(2,128)(2,1)S(1)} %copy.449), channel_id=1, replica_groups=mesh['coil'=8,'slab'=16] {'coil'}, dimensions={3}, use_global_device_ids=true | all-gather | bytes 294912 | tf_op jit(solution)/shard_map/all_gather | solution.py:152
  572.4 1.5 fusion.105
  573.9 1.5 fusion.98
  576.0 1.5 fusion.59
  579.0 1.5 fusion.56
  581.2 1.7 fusion.95
  582.8 1.6 fusion.102
  585.2 1.6 fusion.52
  586.9 1.4 fusion.126
  589.1 70.2 %fusion.70 = f32[1,32,8,17,2]{2,4,3,1,0:T(2,128)S(1)} fusion(bf16[2,24,3,3,3]{1,0,4,3,2:T(2,128)(2,1)S(1)} %copy-done.39, bf16[24,3,34,1,7,2]{0,4,5,2,1,3:T(8,128)(2,1)S(1)} %copy-done.18, bf16[24,3,34,1,8,17]{0,4,5,2,1,3:T(8,128)(2,1)} %copy.392, pred[8,17]{0,1:T(8,128)(4,1)S(1)} %copy-done.41), kind=kOutput, calls=%fused_computation.88 | convolution fusion | flops 13521664 | bytes 771944 | tf_op jit(solution)/shard_map/conv_general_dilated | solution.py:79
  660.4 7.0 %all-reduce.5.cloned.1.call-done = bf16[2,2,1,256,128]{4,3,1,2,0:T(8,128)(2,1)} async-done(((bf16[2,2,1,256,128]{4,3,1,2,0:T(8,128)(2,1)}), bf16[2,2,1,256,128]{4,3,1,2,0:T(8,128)(2,1)}) %all-reduce.5.cloned.1.call-update) | async-done | bytes 262160 | tf_op jit(solution)/shard_map/psum | solution.py:158
  (301 shorter events, 86.9 us)
Async XLA Ops:
  7.2 185.4 %copy-start = (bf16[24,24,3,3,3]{1,0,4,3,2:T(8,128)(2,1)S(1)}, bf16[24,24,3,3,3]{1,0,4,3,2:T(8,128)(2,1)}, u32[]{:S(2)}) copy-start(bf16[24,24,3,3,3]{1,0,4,3,2:T(8,128)(2,1)} %param.18) | copy-start | bytes 93316
  7.2 124.1 %all-reduce.3.cloned.1.call-start = ((), (), s32[]{:S(2)}) async-start(), calls=%async_computation | async-start | bytes 524288 | tf_op jit(solution)/shard_map/psum | solution.py:130
  49.7 10.9 %copy-start.27 = (s32[2,1,32,128]{3,2,1,0:T(8,128)S(1)}, s32[2,1,32,128]{3,2,1,0:T(8,128)}, u32[]{:S(2)}) copy-start(s32[2,1,32,128]{3,2,1,0:T(8,128)} %param.14) | copy-start | bytes 98308
  49.7 16.7 %copy-start.22 = (f32[2,1,32,128]{3,2,1,0:T(8,128)S(1)}, f32[2,1,32,128]{3,2,1,0:T(8,128)}, u32[]{:S(2)}) copy-start(f32[2,1,32,128]{3,2,1,0:T(8,128)} %param.13) | copy-start | bytes 98308
  54.5 93.1 %copy-start.36 = (bf16[24,2,3,3,3]{0,1,4,3,2:T(2,128)(2,1)S(1)}, bf16[24,2,3,3,3]{0,1,4,3,2:T(2,128)(2,1)}, u32[]{:S(2)}) copy-start(bf16[24,2,3,3,3]{0,1,4,3,2:T(2,128)(2,1)} %param.17) | copy-start | bytes 7780
  54.6 93.0 %copy-start.40 = (pred[8,17]{0,1:T(8,128)(4,1)S(1)}, pred[8,17]{0,1:T(8,128)(4,1)}, u32[]{:S(2)}) copy-start(pred[8,17]{0,1:T(8,128)(4,1)} %constant.113) | copy-start | bytes 412
  55.3 612.1 %all-reduce.5.cloned.1.call-start = ((), (), s32[]{:S(2)}) async-start(), calls=%async_computation.1 | async-start | bytes 524288 | tf_op jit(solution)/shard_map/psum | solution.py:158
  55.4 11.8 %collective-permute-start.24 = (bf16[1,2,1,1,128]{4,3,1,2,0:T(2,128)(2,1)S(1)}, bf16[1,2,1,1,128]{4,3,1,2,0:T(2,128)(2,1)S(1)}, u32[]{:S(2)}, u32[]{:S(2)}) collective-permute-start(bf16[1,2,1,1,128]{4,3,1,2,0:T(2,128)(2,1)S(1)} %get-tuple-element.51), channel_id=1, source_target_pairs={{0,16},{16,32},{32,48},{48,64},{64,80},{80,96},{96,112},{1,17},{17... | collective-permute-start | bytes 1544 | tf_op jit(solution)/shard_map/ppermute | solution.py:20
  59.2 8.0 %collective-permute-start.25 = (bf16[1,2,1,1,128]{4,3,1,2,0:T(2,128)(2,1)S(1)}, bf16[1,2,1,1,128]{4,3,1,2,0:T(2,128)(2,1)S(1)}, u32[]{:S(2)}, u32[]{:S(2)}) collective-permute-start(bf16[1,2,1,1,128]{4,3,1,2,0:T(2,128)(2,1)S(1)} %get-tuple-element.50), channel_id=1, source_target_pairs={{16,0},{32,16},{48,32},{64,48},{80,64},{96,80},{112,96},{17,1},{33... | collective-permute-start | bytes 1544 | tf_op jit(solution)/shard_map/ppermute | solution.py:22
  60.6 11.1 %collective-permute-start.12 = (bf16[1,2,1,1,128]{4,3,1,2,0:T(2,128)(2,1)S(1)}, bf16[1,2,1,1,128]{4,3,1,2,0:T(2,128)(2,1)S(1)}, u32[]{:S(2)}, u32[]{:S(2)}) collective-permute-start(bf16[1,2,1,1,128]{4,3,1,2,0:T(2,128)(2,1)S(1)} %get-tuple-element.49), channel_id=1, source_target_pairs={{0,16},{16,32},{32,48},{48,64},{64,80},{80,96},{96,112},{1,17},{17... | collective-permute-start | bytes 1544 | tf_op jit(solution)/shard_map/ppermute | solution.py:20
  65.1 79.5 %collective-permute-start.13 = (bf16[1,2,1,1,128]{4,3,1,2,0:T(2,128)(2,1)S(1)}, bf16[1,2,1,1,128]{4,3,1,2,0:T(2,128)(2,1)S(1)}, u32[]{:S(2)}, u32[]{:S(2)}) collective-permute-start(bf16[1,2,1,1,128]{4,3,1,2,0:T(2,128)(2,1)S(1)} %get-tuple-element.48), channel_id=1, source_target_pairs={{16,0},{32,16},{48,32},{64,48},{80,64},{96,80},{112,96},{17,1},{33... | collective-permute-start | bytes 1544 | tf_op jit(solution)/shard_map/ppermute | solution.py:22
  66.5 86.9 %copy-start.12 = (f32[2,1,32,128]{2,3,0,1:T(8,128)}, f32[2,1,32,128]{2,3,0,1:T(8,128)S(1)}, u32[]{:S(2)}) copy-start(f32[2,1,32,128]{2,3,0,1:T(8,128)S(1)} %copy.368) | copy-start | bytes 98308
  67.3 100.2 %collective-permute-start.27 = (bf16[1,2,1,34,128]{4,1,3,2,0:T(2,128)(2,1)S(1)}, bf16[1,2,1,34,128]{4,1,3,2,0:T(2,128)(2,1)S(1)}, u32[]{:S(2)}, u32[]{:S(2)}) collective-permute-start(bf16[1,2,1,34,128]{4,1,3,2,0:T(2,128)(2,1)S(1)} %constant_dynamic-update-slice_fusion.2), channel_id=1, source_target_pairs={{1,0},{2,1},{3,2},{4,3},{5,4},{6,5},{7,6},{8,7},{9,8},{10,9},{11,1... | collective-permute-start | bytes 52232 | tf_op jit(solution)/shard_map/ppermute | solution.py:22
  68.6 106.0 %collective-permute-start.26 = (bf16[1,2,1,34,128]{4,1,3,2,0:T(2,128)(2,1)S(1)}, bf16[1,2,1,34,128]{4,1,3,2,0:T(2,128)(2,1)S(1)}, u32[]{:S(2)}, u32[]{:S(2)}) collective-permute-start(bf16[1,2,1,34,128]{4,1,3,2,0:T(2,128)(2,1)S(1)} %constant_dynamic-update-slice_fusion.2), channel_id=1, source_target_pairs={{0,1},{1,2},{2,3},{3,4},{4,5},{5,6},{6,7},{7,8},{8,9},{9,10},{10,1... | collective-permute-start | bytes 52232 | tf_op jit(solution)/shard_map/ppermute | solution.py:20
  132.4 6.2 collective-permute-start.1
  133.7 6.4 collective-permute-start
  140.2 5.7 collective-permute-start.3
  141.5 4.4 collective-permute-start.2
  144.6 31.7 %collective-permute-start.15 = (bf16[1,2,1,34,128]{4,1,3,2,0:T(2,128)(2,1)S(1)}, bf16[1,2,1,34,128]{4,1,3,2,0:T(2,128)(2,1)S(1)}, u32[]{:S(2)}, u32[]{:S(2)}) collective-permute-start(bf16[1,2,1,34,128]{4,1,3,2,0:T(2,128)(2,1)S(1)} %constant_dynamic-update-slice_fusion), channel_id=1, source_target_pairs={{1,0},{2,1},{3,2},{4,3},{5,4},{6,5},{7,6},{8,7},{9,8},{10,9},{11,1... | collective-permute-start | bytes 52232 | tf_op jit(solution)/shard_map/ppermute | solution.py:22
  154.9 7.1 %collective-permute-start.5 = (bf16[1,24,1,1,128]{4,1,3,2,0:T(8,128)(2,1)S(1)}, bf16[1,24,1,1,128]{4,1,3,2,0:T(8,128)(2,1)S(1)}, u32[]{:S(2)}, u32[]{:S(2)}) collective-permute-start(bf16[1,24,1,1,128]{4,1,3,2,0:T(8,128)(2,1)S(1)} %slice_bitcast_fusion.20), channel_id=1, source_target_pairs={{16,0},{32,16},{48,32},{64,48},{80,64},{96,80},{112,96},{17,1},{33... | collective-permute-start | bytes 18440 | tf_op jit(solution)/shard_map/ppermute | solution.py:22
  156.5 9.7 %collective-permute-start.4 = (bf16[1,24,1,1,128]{4,1,0,3,2:T(8,128)(2,1)S(1)}, bf16[1,24,1,1,128]{4,1,0,3,2:T(8,128)(2,1)S(1)}, u32[]{:S(2)}, u32[]{:S(2)}) collective-permute-start(bf16[1,24,1,1,128]{4,1,0,3,2:T(8,128)(2,1)S(1)} %slice_bitcast_fusion.21), channel_id=1, source_target_pairs={{0,16},{16,32},{32,48},{48,64},{64,80},{80,96},{96,112},{1,17},{17... | collective-permute-start | bytes 18440 | tf_op jit(solution)/shard_map/ppermute | solution.py:20
  162.0 14.3 %collective-permute-start.14 = (bf16[1,2,1,34,128]{4,1,3,2,0:T(2,128)(2,1)S(1)}, bf16[1,2,1,34,128]{4,1,3,2,0:T(2,128)(2,1)S(1)}, u32[]{:S(2)}, u32[]{:S(2)}) collective-permute-start(bf16[1,2,1,34,128]{4,1,3,2,0:T(2,128)(2,1)S(1)} %constant_dynamic-update-slice_fusion), channel_id=1, source_target_pairs={{0,1},{1,2},{2,3},{3,4},{4,5},{5,6},{6,7},{7,8},{8,9},{9,10},{10,1... | collective-permute-start | bytes 52232 | tf_op jit(solution)/shard_map/ppermute | solution.py:20
  166.2 11.8 %collective-permute-start.7 = (bf16[1,24,1,34,128]{4,1,3,2,0:T(8,128)(2,1)S(1)}, bf16[1,24,1,34,128]{4,1,3,2,0:T(8,128)(2,1)S(1)}, u32[]{:S(2)}, u32[]{:S(2)}) collective-permute-start(bf16[1,24,1,34,128]{4,1,3,2,0:T(8,128)(2,1)S(1)} %pad_maximum_fusion.7), channel_id=1, source_target_pairs={{1,0},{2,1},{3,2},{4,3},{5,4},{6,5},{7,6},{8,7},{9,8},{10,9},{11,1... | collective-permute-start | bytes 626696 | tf_op jit(solution)/shard_map/ppermute | solution.py:22
  167.5 10.5 %collective-permute-start.6 = (bf16[1,24,1,34,128]{4,1,3,2,0:T(8,128)(2,1)S(1)}, bf16[1,24,1,34,128]{4,1,3,2,0:T(8,128)(2,1)S(1)}, u32[]{:S(2)}, u32[]{:S(2)}) collective-permute-start(bf16[1,24,1,34,128]{4,1,3,2,0:T(8,128)(2,1)S(1)} %pad_maximum_fusion.7), channel_id=1, source_target_pairs={{0,1},{1,2},{2,3},{3,4},{4,5},{5,6},{6,7},{7,8},{8,9},{9,10},{10,1... | collective-permute-start | bytes 626696 | tf_op jit(solution)/shard_map/ppermute | solution.py:20
  223.3 27.2 %collective-permute-start.9 = (bf16[1,24,1,1,128]{4,1,3,2,0:T(8,128)(2,1)}, bf16[1,24,1,1,128]{4,1,3,2,0:T(8,128)(2,1)S(1)}, u32[]{:S(2)}, u32[]{:S(2)}) collective-permute-start(bf16[1,24,1,1,128]{4,1,3,2,0:T(8,128)(2,1)} %slice_bitcast_fusion.18), channel_id=1, source_target_pairs={{16,0},{32,16},{48,32},{64,48},{80,64},{96,80},{112,96},{17,1},{33... | collective-permute-start | bytes 18440 | tf_op jit(solution)/shard_map/ppermute | solution.py:22
  226.9 28.3 %collective-permute-start.8 = (bf16[1,24,1,1,128]{4,1,0,3,2:T(8,128)(2,1)S(1)}, bf16[1,24,1,1,128]{4,1,0,3,2:T(8,128)(2,1)S(1)}, u32[]{:S(2)}, u32[]{:S(2)}) collective-permute-start(bf16[1,24,1,1,128]{4,1,0,3,2:T(8,128)(2,1)S(1)} %slice_bitcast_fusion.19), channel_id=1, source_target_pairs={{0,16},{16,32},{32,48},{48,64},{64,80},{80,96},{96,112},{1,17},{17... | collective-permute-start | bytes 18440 | tf_op jit(solution)/shard_map/ppermute | solution.py:20
  232.8 10.9 %collective-permute-start.29 = (bf16[1,24,1,1,128]{4,1,3,2,0:T(8,128)(2,1)S(1)}, bf16[1,24,1,1,128]{4,1,3,2,0:T(8,128)(2,1)S(1)}, u32[]{:S(2)}, u32[]{:S(2)}) collective-permute-start(bf16[1,24,1,1,128]{4,1,3,2,0:T(8,128)(2,1)S(1)} %slice_bitcast_fusion.12), channel_id=1, source_target_pairs={{16,0},{32,16},{48,32},{64,48},{80,64},{96,80},{112,96},{17,1},{33... | collective-permute-start | bytes 18440 | tf_op jit(solution)/shard_map/ppermute | solution.py:22
  234.2 21.0 %copy-start.2 = (bf16[1,24,1,32,128]{4,1,3,2,0:T(8,128)(2,1)S(1)}, bf16[1,24,1,32,128]{4,1,3,2,0:T(8,128)(2,1)}, u32[]{:S(2)}) copy-start(bf16[1,24,1,32,128]{4,1,3,2,0:T(8,128)(2,1)} %copy.389) | copy-start | bytes 589828
  235.3 13.9 %collective-permute-start.28 = (bf16[1,24,1,1,128]{4,1,0,3,2:T(8,128)(2,1)S(1)}, bf16[1,24,1,1,128]{4,1,0,3,2:T(8,128)(2,1)S(1)}, u32[]{:S(2)}, u32[]{:S(2)}) collective-permute-start(bf16[1,24,1,1,128]{4,1,0,3,2:T(8,128)(2,1)S(1)} %slice_bitcast_fusion.13), channel_id=1, source_target_pairs={{0,16},{16,32},{32,48},{48,64},{64,80},{80,96},{96,112},{1,17},{17... | collective-permute-start | bytes 18440 | tf_op jit(solution)/shard_map/ppermute | solution.py:20
  241.0 16.2 %collective-permute-start.17 = (bf16[1,24,1,1,128]{4,1,3,2,0:T(8,128)(2,1)S(1)}, bf16[1,24,1,1,128]{4,1,3,2,0:T(8,128)(2,1)S(1)}, u32[]{:S(2)}, u32[]{:S(2)}) collective-permute-start(bf16[1,24,1,1,128]{4,1,3,2,0:T(8,128)(2,1)S(1)} %slice_bitcast_fusion.16), channel_id=1, source_target_pairs={{16,0},{32,16},{48,32},{64,48},{80,64},{96,80},{112,96},{17,1},{33... | collective-permute-start | bytes 18440 | tf_op jit(solution)/shard_map/ppermute | solution.py:22
  243.7 30.6 %copy-start.4 = (bf16[1,24,1,32,128]{4,1,3,2,0:T(8,128)(2,1)}, bf16[1,24,1,32,128]{4,1,3,2,0:T(8,128)(2,1)S(1)}, u32[]{:S(2)}) copy-start(bf16[1,24,1,32,128]{4,1,3,2,0:T(8,128)(2,1)S(1)} %copy.406) | copy-start | bytes 589828
  243.7 22.7 %collective-permute-start.16 = (bf16[1,24,1,1,128]{4,1,0,3,2:T(8,128)(2,1)S(1)}, bf16[1,24,1,1,128]{4,1,0,3,2:T(8,128)(2,1)S(1)}, u32[]{:S(2)}, u32[]{:S(2)}) collective-permute-start(bf16[1,24,1,1,128]{4,1,0,3,2:T(8,128)(2,1)S(1)} %slice_bitcast_fusion.17), channel_id=1, source_target_pairs={{0,16},{16,32},{32,48},{48,64},{64,80},{80,96},{96,112},{1,17},{17... | collective-permute-start | bytes 18440 | tf_op jit(solution)/shard_map/ppermute | solution.py:20
  249.2 19.2 %collective-permute-start.31 = (bf16[1,24,1,34,128]{4,1,3,2,0:T(8,128)(2,1)S(1)}, bf16[1,24,1,34,128]{4,1,3,2,0:T(8,128)(2,1)S(1)}, u32[]{:S(2)}, u32[]{:S(2)}) collective-permute-start(bf16[1,24,1,34,128]{4,1,3,2,0:T(8,128)(2,1)S(1)} %pad_maximum_fusion.11), channel_id=1, source_target_pairs={{1,0},{2,1},{3,2},{4,3},{5,4},{6,5},{7,6},{8,7},{9,8},{10,9},{11,1... | collective-permute-start | bytes 626696 | tf_op jit(solution)/shard_map/ppermute | solution.py:22
  250.5 23.8 %collective-permute-start.30 = (bf16[1,24,1,34,128]{4,1,3,2,0:T(8,128)(2,1)S(1)}, bf16[1,24,1,34,128]{4,1,3,2,0:T(8,128)(2,1)S(1)}, u32[]{:S(2)}, u32[]{:S(2)}) collective-permute-start(bf16[1,24,1,34,128]{4,1,3,2,0:T(8,128)(2,1)S(1)} %pad_maximum_fusion.11), channel_id=1, source_target_pairs={{0,1},{1,2},{2,3},{3,4},{4,5},{5,6},{6,7},{7,8},{8,9},{9,10},{10,1... | collective-permute-start | bytes 626696 | tf_op jit(solution)/shard_map/ppermute | solution.py:20
  255.2 22.1 %copy-start.30 = (bf16[1,24,1,1,128]{4,1,0,3,2:T(8,128)(2,1)}, bf16[1,24,1,1,128]{4,1,0,3,2:T(8,128)(2,1)S(1)}, u32[]{:S(2)}) copy-start(bf16[1,24,1,1,128]{4,1,0,3,2:T(8,128)(2,1)S(1)} %collective-permute-done.8) | copy-start | bytes 18436
  255.9 85.3 %collective-permute-start.11 = (bf16[1,24,1,34,128]{4,1,3,2,0:T(8,128)(2,1)}, bf16[1,24,1,34,128]{4,1,3,2,0:T(8,128)(2,1)}, u32[]{:S(2)}, u32[]{:S(2)}) collective-permute-start(bf16[1,24,1,34,128]{4,1,3,2,0:T(8,128)(2,1)} %pad_maximum_fusion.8), channel_id=1, source_target_pairs={{1,0},{2,1},{3,2},{4,3},{5,4},{6,5},{7,6},{8,7},{9,8},{10,9},{11,1... | collective-permute-start | bytes 626696 | tf_op jit(solution)/shard_map/ppermute | solution.py:22
  257.2 20.1 %copy-start.32 = (bf16[1,24,1,1,128]{4,1,3,2,0:T(8,128)(2,1)}, bf16[1,24,1,1,128]{4,1,3,2,0:T(8,128)(2,1)S(1)}, u32[]{:S(2)}) copy-start(bf16[1,24,1,1,128]{4,1,3,2,0:T(8,128)(2,1)S(1)} %collective-permute-done.17) | copy-start | bytes 18436
  257.2 89.0 %collective-permute-start.10 = (bf16[1,24,1,34,128]{4,1,3,2,0:T(8,128)(2,1)}, bf16[1,24,1,34,128]{4,1,3,2,0:T(8,128)(2,1)}, u32[]{:S(2)}, u32[]{:S(2)}) collective-permute-start(bf16[1,24,1,34,128]{4,1,3,2,0:T(8,128)(2,1)} %pad_maximum_fusion.8), channel_id=1, source_target_pairs={{0,1},{1,2},{2,3},{3,4},{4,5},{5,6},{6,7},{7,8},{8,9},{9,10},{10,1... | collective-permute-start | bytes 626696 | tf_op jit(solution)/shard_map/ppermute | solution.py:20
  266.4 10.9 %copy-start.34 = (bf16[1,24,1,1,128]{4,1,0,3,2:T(8,128)(2,1)}, bf16[1,24,1,1,128]{4,1,0,3,2:T(8,128)(2,1)S(1)}, u32[]{:S(2)}) copy-start(bf16[1,24,1,1,128]{4,1,0,3,2:T(8,128)(2,1)S(1)} %collective-permute-done.16) | copy-start | bytes 18436
  267.2 31.9 %collective-permute-start.19 = (bf16[1,24,1,34,128]{4,1,3,2,0:T(8,128)(2,1)}, bf16[1,24,1,34,128]{4,1,3,2,0:T(8,128)(2,1)}, u32[]{:S(2)}, u32[]{:S(2)}) collective-permute-start(bf16[1,24,1,34,128]{4,1,3,2,0:T(8,128)(2,1)} %pad_maximum_fusion.9), channel_id=1, source_target_pairs={{1,0},{2,1},{3,2},{4,3},{5,4},{6,5},{7,6},{8,7},{9,8},{10,9},{11,1... | collective-permute-start | bytes 626696 | tf_op jit(solution)/shard_map/ppermute | solution.py:22
  268.5 30.6 %collective-permute-start.18 = (bf16[1,24,1,34,128]{4,1,3,2,0:T(8,128)(2,1)}, bf16[1,24,1,34,128]{4,1,3,2,0:T(8,128)(2,1)}, u32[]{:S(2)}, u32[]{:S(2)}) collective-permute-start(bf16[1,24,1,34,128]{4,1,3,2,0:T(8,128)(2,1)} %pad_maximum_fusion.9), channel_id=1, source_target_pairs={{0,1},{1,2},{2,3},{3,4},{4,5},{5,6},{6,7},{7,8},{8,9},{9,10},{10,1... | collective-permute-start | bytes 626696 | tf_op jit(solution)/shard_map/ppermute | solution.py:20
  289.1 10.0 %copy-start.5 = (bf16[1,24,1,32,128]{4,1,3,2,0:T(8,128)(2,1)S(1)}, bf16[1,24,1,32,128]{4,1,3,2,0:T(8,128)(2,1)}, u32[]{:S(2)}) copy-start(bf16[1,24,1,32,128]{4,1,3,2,0:T(8,128)(2,1)} %copy-done.4) | copy-start | bytes 589828
  289.1 10.0 %copy-start.33 = (bf16[1,24,1,1,128]{4,1,3,2,0:T(8,128)(2,1)S(1)}, bf16[1,24,1,1,128]{4,1,3,2,0:T(8,128)(2,1)}, u32[]{:S(2)}) copy-start(bf16[1,24,1,1,128]{4,1,3,2,0:T(8,128)(2,1)} %copy-done.32) | copy-start | bytes 18436
  289.2 10.0 %copy-start.35 = (bf16[1,24,1,1,128]{4,1,0,3,2:T(8,128)(2,1)S(1)}, bf16[1,24,1,1,128]{4,1,0,3,2:T(8,128)(2,1)}, u32[]{:S(2)}) copy-start(bf16[1,24,1,1,128]{4,1,0,3,2:T(8,128)(2,1)} %copy-done.34) | copy-start | bytes 18436
  324.7 9.0 %collective-permute-start.33 = (bf16[1,24,1,1,128]{4,1,3,2,0:T(8,128)(2,1)S(1)}, bf16[1,24,1,1,128]{4,1,3,2,0:T(8,128)(2,1)S(1)}, u32[]{:S(2)}, u32[]{:S(2)}) collective-permute-start(bf16[1,24,1,1,128]{4,1,3,2,0:T(8,128)(2,1)S(1)} %slice_bitcast_fusion.10), channel_id=1, source_target_pairs={{16,0},{32,16},{48,32},{64,48},{80,64},{96,80},{112,96},{17,1},{33... | collective-permute-start | bytes 18440 | tf_op jit(solution)/shard_map/ppermute | solution.py:22
  326.0 20.2 %copy-start.3 = (bf16[1,24,1,32,128]{4,1,3,2,0:T(8,128)(2,1)S(1)}, bf16[1,24,1,32,128]{4,1,3,2,0:T(8,128)(2,1)}, u32[]{:S(2)}) copy-start(bf16[1,24,1,32,128]{4,1,3,2,0:T(8,128)(2,1)} %copy.389) | copy-start | bytes 589828
  326.0 20.2 %copy-start.31 = (bf16[1,24,1,1,128]{4,1,0,3,2:T(8,128)(2,1)S(1)}, bf16[1,24,1,1,128]{4,1,0,3,2:T(8,128)(2,1)}, u32[]{:S(2)}) copy-start(bf16[1,24,1,1,128]{4,1,0,3,2:T(8,128)(2,1)} %copy-done.30) | copy-start | bytes 18436
  326.4 12.8 %collective-permute-start.32 = (bf16[1,24,1,1,128]{4,1,0,3,2:T(8,128)(2,1)S(1)}, bf16[1,24,1,1,128]{4,1,0,3,2:T(8,128)(2,1)S(1)}, u32[]{:S(2)}, u32[]{:S(2)}) collective-permute-start(bf16[1,24,1,1,128]{4,1,0,3,2:T(8,128)(2,1)S(1)} %slice_bitcast_fusion.11), channel_id=1, source_target_pairs={{0,16},{16,32},{32,48},{48,64},{64,80},{80,96},{96,112},{1,17},{17... | collective-permute-start | bytes 18440 | tf_op jit(solution)/shard_map/ppermute | solution.py:20
  331.5 31.6 %collective-permute-start.21 = (bf16[1,24,1,1,128]{4,1,3,2,0:T(8,128)(2,1)S(1)}, bf16[1,24,1,1,128]{4,1,3,2,0:T(8,128)(2,1)S(1)}, u32[]{:S(2)}, u32[]{:S(2)}) collective-permute-start(bf16[1,24,1,1,128]{4,1,3,2,0:T(8,128)(2,1)S(1)} %slice_bitcast_fusion.14), channel_id=1, source_target_pairs={{16,0},{32,16},{48,32},{64,48},{80,64},{96,80},{112,96},{17,1},{33... | collective-permute-start | bytes 18440 | tf_op jit(solution)/shard_map/ppermute | solution.py:22
  333.7 16.3 %copy-start.6 = (bf16[1,24,1,32,128]{4,1,3,2,0:T(8,128)(2,1)}, bf16[1,24,1,32,128]{4,1,3,2,0:T(8,128)(2,1)S(1)}, u32[]{:S(2)}) copy-start(bf16[1,24,1,32,128]{4,1,3,2,0:T(8,128)(2,1)S(1)} %copy.441) | copy-start | bytes 589828
  333.7 29.4 %collective-permute-start.20 = (bf16[1,24,1,1,128]{4,1,0,3,2:T(8,128)(2,1)S(1)}, bf16[1,24,1,1,128]{4,1,0,3,2:T(8,128)(2,1)S(1)}, u32[]{:S(2)}, u32[]{:S(2)}) collective-permute-start(bf16[1,24,1,1,128]{4,1,0,3,2:T(8,128)(2,1)S(1)} %slice_bitcast_fusion.15), channel_id=1, source_target_pairs={{0,16},{16,32},{32,48},{48,64},{64,80},{80,96},{96,112},{1,17},{17... | collective-permute-start | bytes 18440 | tf_op jit(solution)/shard_map/ppermute | solution.py:20
  339.9 29.7 %collective-permute-start.35 = (bf16[1,24,1,34,128]{4,1,3,2,0:T(8,128)(2,1)}, bf16[1,24,1,34,128]{4,1,3,2,0:T(8,128)(2,1)}, u32[]{:S(2)}, u32[]{:S(2)}) collective-permute-start(bf16[1,24,1,34,128]{4,1,3,2,0:T(8,128)(2,1)} %pad_maximum_fusion.12), channel_id=1, source_target_pairs={{1,0},{2,1},{3,2},{4,3},{5,4},{6,5},{7,6},{8,7},{9,8},{10,9},{11,1... | collective-permute-start | bytes 626696 | tf_op jit(solution)/shard_map/ppermute | solution.py:22
  341.2 28.4 %collective-permute-start.34 = (bf16[1,24,1,34,128]{4,1,3,2,0:T(8,128)(2,1)}, bf16[1,24,1,34,128]{4,1,3,2,0:T(8,128)(2,1)}, u32[]{:S(2)}, u32[]{:S(2)}) collective-permute-start(bf16[1,24,1,34,128]{4,1,3,2,0:T(8,128)(2,1)} %pad_maximum_fusion.12), channel_id=1, source_target_pairs={{0,1},{1,2},{2,3},{3,4},{4,5},{5,6},{6,7},{7,8},{8,9},{9,10},{10,1... | collective-permute-start | bytes 626696 | tf_op jit(solution)/shard_map/ppermute | solution.py:20
  363.2 92.6 %collective-permute-start.23 = (bf16[1,24,1,34,128]{4,1,3,2,0:T(8,128)(2,1)S(1)}, bf16[1,24,1,34,128]{4,1,3,2,0:T(8,128)(2,1)S(1)}, u32[]{:S(2)}, u32[]{:S(2)}) collective-permute-start(bf16[1,24,1,34,128]{4,1,3,2,0:T(8,128)(2,1)S(1)} %pad_maximum_fusion.10), channel_id=1, source_target_pairs={{1,0},{2,1},{3,2},{4,3},{5,4},{6,5},{7,6},{8,7},{9,8},{10,9},{11,1... | collective-permute-start | bytes 626696 | tf_op jit(solution)/shard_map/ppermute | solution.py:22
  364.5 91.3 %collective-permute-start.22 = (bf16[1,24,1,34,128]{4,1,3,2,0:T(8,128)(2,1)S(1)}, bf16[1,24,1,34,128]{4,1,3,2,0:T(8,128)(2,1)S(1)}, u32[]{:S(2)}, u32[]{:S(2)}) collective-permute-start(bf16[1,24,1,34,128]{4,1,3,2,0:T(8,128)(2,1)S(1)} %pad_maximum_fusion.10), channel_id=1, source_target_pairs={{0,1},{1,2},{2,3},{3,4},{4,5},{5,6},{6,7},{7,8},{8,9},{9,10},{10,1... | collective-permute-start | bytes 626696 | tf_op jit(solution)/shard_map/ppermute | solution.py:20
  385.3 70.5 %copy-start.9 = (bf16[1,24,1,32,128]{4,1,3,2,0:T(8,128)(2,1)S(1)}, bf16[1,24,1,32,128]{4,1,3,2,0:T(8,128)(2,1)}, u32[]{:S(2)}) copy-start(bf16[1,24,1,32,128]{4,1,3,2,0:T(8,128)(2,1)} %copy-done.8) | copy-start | bytes 589828
  470.8 70.3 %copy-start.26 = (f32[2,1,32,128]{3,2,1,0:T(8,128)S(1)}, f32[2,1,32,128]{3,2,1,0:T(8,128)}, u32[]{:S(2)}) copy-start(f32[2,1,32,128]{3,2,1,0:T(8,128)} %param.16) | copy-start | bytes 98308
  470.9 70.3 %copy-start.28 = (s32[2,1,32,128]{3,2,1,0:T(8,128)S(1)}, s32[2,1,32,128]{3,2,1,0:T(8,128)}, u32[]{:S(2)}) copy-start(s32[2,1,32,128]{3,2,1,0:T(8,128)} %param.14) | copy-start | bytes 98308
  540.8 29.4 %copy-start.16 = (f32[256,128]{1,0:T(8,128)S(1)}, f32[256,128]{1,0:T(8,128)}, u32[]{:S(2)}) copy-start(f32[256,128]{1,0:T(8,128)} %get-tuple-element.38) | copy-start | bytes 393220
  540.8 29.4 %copy-start.17 = (f32[256,128]{1,0:T(8,128)S(1)}, f32[256,128]{1,0:T(8,128)}, u32[]{:S(2)}) copy-start(f32[256,128]{1,0:T(8,128)} %get-tuple-element.39) | copy-start | bytes 393220
  589.1 70.5 %copy-start.13 = (f32[2,1,32,128]{2,3,0,1:T(8,128)S(1)}, f32[2,1,32,128]{2,3,0,1:T(8,128)}, u32[]{:S(2)}) copy-start(f32[2,1,32,128]{2,3,0,1:T(8,128)} %copy-done.12) | copy-start | bytes 98308
  589.1 70.5 %copy-start.19 = (f32[2,1,256,128]{2,3,0,1:T(8,128)S(1)}, f32[2,1,256,128]{2,3,0,1:T(8,128)}, u32[]{:S(2)}) copy-start(f32[2,1,256,128]{2,3,0,1:T(8,128)} %all-reduce.3.cloned.1.call-done) | copy-start | bytes 786436
  589.1 79.6 %copy-start.29 = (f32[2,1,32,128]{3,2,1,0:T(8,128)S(1)}, f32[2,1,32,128]{3,2,1,0:T(8,128)}, u32[]{:S(2)}) copy-start(f32[2,1,32,128]{3,2,1,0:T(8,128)} %param.15) | copy-start | bytes 98308
  589.1 80.3 %copy-start.1 = (bf16[24,24,3,3,3]{1,0,4,3,2:T(8,128)(2,1)S(1)}, bf16[24,24,3,3,3]{1,0,4,3,2:T(8,128)(2,1)}, u32[]{:S(2)}) copy-start(bf16[24,24,3,3,3]{1,0,4,3,2:T(8,128)(2,1)} %param.18) | copy-start | bytes 93316
  (16 other events, 93.6 us)
Sparse Core Ops, SparseCore 0:
  55.4 75.7 all-reduce.2
  589.2 78.1 all-reduce.4
where the time goes:
time: 687 us; the launch traced here: 677 us
  matrix products  286 us (42%)
  local copies, waits for them, and re-layouts  123 us (18%)
  starting transfers between devices  114 us (17%)
  waiting for transfers between devices  68.4 us (10%)
  blocking collectives  56.9 us (8%)
  between operations  16.3 us (2%)
  other arithmetic  11.2 us (2%)
    conv_general_dilated x9, matrix products, convolve_local(): lax.conv_general_dilated(haloed, kernel, (1, 1, 1), ((0, 0), (0, 0), (1,...  253 us
    ppermute x18, starting transfers between devices, with_halo(): lax.ppermute(tail, axis, [(i, (i + 1) % count) for i in range(ends)])  90.8 us
    conv_general_dilated x24, local copies, waits for them, and re-layouts, convolve_local(): lax.conv_general_dilated(haloed, kernel, (1, 1, 1), ((0, 0), (0, 0), (1,...  63.4 us
    psum x1, waiting for transfers between devices, on_device(): summed = lax.psum(partial_sum, 'coil')  59.6 us
    concatenate x17, local copies, waits for them, and re-layouts, with_halo(): jnp.concatenate([lax.ppermute(tail, axis, [(i, (i + 1) % count) for i in...  30.3 us
    all_gather x1, blocking collectives, on_device(): lax.all_gather(pulled.astype(jnp.bfloat16), 'coil', axis=3, tiled=True)  28.6 us
    all_gather x1, blocking collectives, on_device(): lax.all_gather(iterate.astype(jnp.bfloat16), 'coil', axis=2, tiled=True)  28.3 us
    ppermute x18, starting transfers between devices, with_halo(): lax.ppermute(head, axis, [((i + 1) % count, i) for i in range(ends)])  23.2 us
  transfers between devices with their start and end apart: 38, of which 4 were waited for; matrix products, arithmetic and copies ran while one was open for 37% of the time, Pallas kernels for 0%

commit v1 on v0

v1 whole, which is shorter than its diff:
```python
import math

import jax
import jax.numpy as jnp
import numpy as np
from jax import lax
from jax.experimental import pallas as pl
from jax.experimental.pallas import tpu as pltpu
from jax.sharding import PartitionSpec as P

STEP = 0.8
F32 = jnp.float32
BF16 = jnp.bfloat16
NZ = 128
NY = 256
NYL = 32
HALO_ROWS = 40
VMEM_BIG = 56 << 20


def whole(count):
    return [pl.BlockSpec(memory_space=pltpu.VMEM)] * count


def split_host(table):
    high = table.astype(np.float32).astype(jnp.bfloat16)
    low = (table - high.astype(np.float64)).astype(jnp.bfloat16)
    return high, low


def fourier_constants():
    def cos_sin(length):
        index = np.arange(length)
        angles = (index[:, None] * index[None, :] % length) * (2.0 * math.pi / length)
        return np.cos(angles) / math.sqrt(length), np.sin(angles) / math.sqrt(length)

    cos_y, sin_y = cos_sin(NY)
    cos_z, sin_z = cos_sin(NZ)
    along_y = np.concatenate([cos_y, sin_y], axis=0)
    along_z = np.block([[cos_z, -sin_z], [sin_z, cos_z]])
    return split_host(along_y) + split_host(along_z)


def split(values):
    high = values.astype(BF16)
    return high, (values - high.astype(F32)).astype(BF16)


def mm(left, right):
    return jnp.dot(left, right, preferred_element_type=F32)


def along_z(joined, high_ref, low_ref):
    high, low = split(joined)
    return mm(high, high_ref[...]) + (mm(high, low_ref[...]) + mm(low, high_ref[...]))


def along_y(joined, high_ref, low_ref):
    high, low = split(joined)
    return mm(high_ref[...], high) + (mm(low_ref[...], high) + mm(high_ref[...], low))


def forward(real, imag, tabs):
    y_high, y_low, z_high, z_low = tabs
    turned = along_y(along_z(jnp.concatenate([real, imag], 1), z_high, z_low), y_high, y_low)
    cos_part, sin_part = turned[:NY], turned[NY:]
    return cos_part[:, :NZ] + sin_part[:, NZ:], cos_part[:, NZ:] - sin_part[:, :NZ]


def inverse(real, imag, tabs):
    y_high, y_low, z_high, z_low = tabs
    turned = along_y(jnp.concatenate([real, imag], 1), y_high, y_low)
    cos_part, sin_part = turned[:NY], turned[NY:]
    back = cos_part[:, :NZ] - sin_part[:, NZ:], -(cos_part[:, NZ:] + sin_part[:, :NZ])
    turned = along_z(jnp.concatenate(back, 1), z_high, z_low)
    return turned[:, :NZ], -turned[:, NZ:]


def gradient_kernel(
    field_ref, maps_ref, kspace_ref, mask_ref, bits_ref, adj_ref, yh, yl, zh, zl, out_ref, pad
):
    tabs = (yh, yl, zh, zl)
    weight = mask_ref[...].astype(F32)
    map_re, map_im = maps_ref[0], maps_ref[1]
    re = field_ref[:, 0].reshape(NY, NZ)
    im = field_ref[:, 1].reshape(NY, NZ)
    f_re, f_im = forward(map_re * re - map_im * im, map_re * im + map_im * re, tabs)
    f_re = weight * (f_re - kspace_ref[0])
    f_im = weight * (f_im - kspace_ref[1])
    b_re, b_im = inverse(f_re, f_im, tabs)
    zero = jnp.zeros((4, NZ), F32)
    for ch in range(2):
        pad[ch, 0:4] = zero
        pad[ch, NY + 4 : NY + 8] = zero
    pad[0, 4 : NY + 4] = map_re * b_re + map_im * b_im
    pad[1, 4 : NY + 4] = map_re * b_im - map_im * b_re
    edges = []
    for ch in range(4):
        if ch < 2:
            rows = (2 * bits_ref[ch] - 1).astype(F32)
        else:
            rows = adj_ref[ch - 2]
        edges += [rows[0:4], rows[NYL - 4 : NYL]]
    edges = jnp.concatenate(edges + [jnp.zeros((8, NZ), F32)], 0).astype(BF16)
    for dest in range(8):
        for ch in range(2):
            out_ref[dest, ch] = pad[ch, NYL * dest : NYL * dest + HALO_ROWS].astype(BF16)
        out_ref[dest, 2] = edges


def relax_kernel(place_ref, got_ref, field_ref, bits_ref, adj_ref, out_ref, relaxed_ref, pad, qpad):
    coil = place_ref[0]
    zero = jnp.zeros((4, NZ), F32)
    first = pl.multiple_of(coil * NYL, NYL)
    for ch in range(2):
        pad[ch, 0:4] = zero
        pad[ch, NY + 4 : NY + 8] = zero
        pad[ch, 4 : NY + 4] = field_ref[:, ch].reshape(NY, NZ)
        total = got_ref[0, ch].astype(F32)
        for source in range(1, 8):
            total = total + got_ref[source, ch].astype(F32)
        relaxed = pad[ch, pl.ds(first, HALO_ROWS)] - STEP * total
        relaxed_ref[ch] = relaxed[4 : 4 + NYL]
        rows = relaxed.astype(BF16)
        for dest in range(16):
            out_ref[dest, ch] = rows
    below = got_ref[jnp.maximum(coil - 1, 0), 2].astype(F32)
    above = got_ref[jnp.minimum(coil + 1, 7), 2].astype(F32)
    below = jnp.where(coil > 0, below, 0.0)
    above = jnp.where(coil < 7, above, 0.0)
    for ch in range(4):
        if ch < 2:
            rows = (2 * bits_ref[ch] - 1).astype(F32)
        else:
            rows = adj_ref[ch - 2]
        qpad[ch, 0:3] = below[ch * 8 + 5 : ch * 8 + 8]
        qpad[ch, 3 : 3 + NYL] = rows
        qpad[ch, 3 + NYL : 7 + NYL] = above[ch * 8 : ch * 8 + 4]
        qpad[ch, 7 + NYL : HALO_ROWS] = zero[0:1]
        packed = qpad[ch].astype(BF16)
        for dest in range(16):
            out_ref[dest, 2 + ch] = packed


def dot_first(left, right):
    return lax.dot_general(left, right, (((0,), (0,)), ((), ())), preferred_element_type=F32)


def tables_kernel(k1_ref, k2_ref, k3_ref, t1_ref, t2_ref, t3_ref, t1t_ref, t2t_ref, t3t_ref):
    lane = lax.broadcasted_iota(jnp.int32, (24, 256), 1)
    row = lax.broadcasted_iota(jnp.int32, (24, 256), 0)
    tile24 = ((lane % 24 == row) & (lane < 240)).astype(BF16)
    window = jnp.where(lane < 240, lane // 24, 99)

    def tap(dx, dy, dz, flip):
        if flip:
            dx, dy, dz = 2 - dx, 2 - dy, 2 - dz
        return dx * 9 + dy * 3 + dz

    for target, flip in ((t2_ref, False), (t2t_ref, True)):
        for dz in range(3):
            for dx in range(3):
                spread = []
                for dy in range(3):
                    block = k2_ref[tap(dx, dy, dz, flip)]
                    spread.append(dot_first(block, tile24) if flip else mm(block, tile24))
                for yo in range(8):
                    value = jnp.zeros((24, 256), F32)
                    for dy in range(3):
                        value = jnp.where(window == yo + dy, spread[dy], value)
                    at = dz * 192 + yo * 24
                    target[at : at + 24, dx * 256 : dx * 256 + 256] = value.astype(BF16)

    lane96 = lax.broadcasted_iota(jnp.int32, (24, 96), 1)
    lane2 = lax.broadcasted_iota(jnp.int32, (2, 96), 1)
    row2 = lax.broadcasted_iota(jnp.int32, (2, 96), 0)
    tile2 = ((lane2 // 16) % 2 == row2).astype(BF16)
    code = (lane96 // 32) * 16 + lane96 % 16
    for target, source, flip in ((t1_ref, k1_ref, False), (t3t_ref, k3_ref, True)):
        for dz in range(3):
            spread = {}
            for dx in range(3):
                for dy in range(3):
                    spread[dx, dy] = dot_first(source[tap(dx, dy, dz, flip)], tile2)
            for yo in range(8):
                value = jnp.zeros((24, 96), F32)
                for dx in range(3):
                    for dy in range(3):
                        value = jnp.where(code == dx * 16 + yo + dy, spread[dx, dy], value)
                at = dz * 192 + yo * 24
                target[at : at + 24, :] = value.astype(BF16)

    window8 = window[0:8] - lax.broadcasted_iota(jnp.int32, (8, 256), 0)
    for target, source, flip in ((t3_ref, k3_ref, False), (t1t_ref, k1_ref, True)):
        for dz in range(3):
            for dx in range(3):
                spread = [mm(source[tap(dx, dy, dz, flip)], tile24) for dy in range(3)]
                both = []
                for ch in range(2):
                    value = jnp.zeros((8, 256), F32)
                    for dy in range(3):
                        value = jnp.where(window8 == dy, spread[dy][ch : ch + 1], value)
                    both.append(value)
                target[dz * 16 : dz * 16 + 16, dx * 256 : dx * 256 + 256] = jnp.concatenate(
                    both, 0
                ).astype(BF16)


def tables(kernel_first, kernel_second, kernel_last):
    k1 = jnp.transpose(kernel_first, (2, 3, 4, 1, 0)).reshape(27, 2, 24)
    k2 = jnp.transpose(kernel_second, (2, 3, 4, 0, 1)).reshape(27, 24, 24)
    k3 = jnp.transpose(kernel_last, (2, 3, 4, 0, 1)).reshape(27, 2, 24)
    shapes = [(576, 96), (576, 768), (48, 768), (48, 768), (576, 768), (576, 96)]
    return pl.pallas_call(
        tables_kernel,
        out_shape=[jax.ShapeDtypeStruct(s, BF16) for s in shapes],
        in_specs=whole(3),
        out_specs=whole(6),
        cost_estimate=pl.CostEstimate(flops=10**9, bytes_accessed=4 * 10**6, transcendentals=0),
    )(k1, k2, k3)


def join_z(parts, rows, half, at_low, at_high):
    lanes = slice(half * NZ, half * NZ + NZ)
    before = jnp.where(at_low, 0.0, pltpu.roll(parts[0:rows, lanes], 1, 1))
    after = jnp.where(at_high, 0.0, pltpu.roll(parts[2 * rows : 3 * rows, lanes], NZ - 1, 1))
    return parts[rows : 2 * rows, lanes] + (before + after)


def denoise_kernel(
    place_ref,
    planes_ref,
    relaxed_ref,
    bits_ref,
    adj_ref,
    t1_ref,
    t2_ref,
    t3_ref,
    t1t_ref,
    t2t_ref,
    t3t_ref,
    new_ref,
    pulled_ref,
    send_ref,
    image,
    cots,
    a1,
    s1,
    a2,
    e2,
    e1,
):
    coil, slab = place_ref[0], place_ref[1]
    tail8 = jnp.zeros((8, NZ), F32)

    def inside(plane):
        return (plane >= 0) & (plane < 16)

    for j in range(10):
        plane = slab - 4 + j
        keep = inside(plane) & (j < 9)
        source = jnp.clip(plane, 0, 15)
        for ch in range(2):
            image[j, ch, 0:HALO_ROWS] = jnp.where(keep, planes_ref[source, ch].astype(F32), 0.0)
            image[j, ch, HALO_ROWS:48] = tail8
        if 1 <= j < 9:
            for ch in range(4):
                cots[j - 1, ch, 0:HALO_ROWS] = jnp.where(
                    keep, planes_ref[source, 2 + ch].astype(F32), 0.0
                )
                cots[j - 1, ch, HALO_ROWS:48] = tail8

    def at_edges(rows):
        column = lax.broadcasted_iota(jnp.int32, (rows, NZ), 1)
        return column == 0, column == NZ - 1

    low, high = at_edges(192)
    zero64 = jnp.zeros((64, NZ), BF16)
    for j in range(8):
        a1[j, 960:1024] = zero64
        s1[j, 960:1024] = jnp.zeros((64, NZ), F32)
    for j in range(6):
        a2[j, 960:1024] = zero64
        e2[j, 960:1024] = jnp.zeros((64, 2 * NZ), BF16)
    for j in range(3):
        e1[j, 960:1024] = jnp.zeros((64, 2 * NZ), BF16)

    def first_step(step, carry):
        pair, block = 2 * (step // 5), step % 5
        at = pl.multiple_of(8 * block, 8)
        to = pl.multiple_of(192 * block, 192)
        pieces = []
        for dx in range(3):
            for ch in range(2):
                pieces.append(
                    jnp.concatenate(
                        [
                            image[pair + dx, ch, pl.ds(at, 16)],
                            image[pair + dx + 1, ch, pl.ds(at, 16)],
                        ],
                        1,
                    ).astype(BF16)
                )
        parts = mm(t1_ref[...], jnp.concatenate(pieces, 0))
        for half in range(2):
            pre = join_z(parts, 192, half, low, high)
            gate = jax.nn.sigmoid(pre)
            a1[pair + half, pl.ds(to, 192)] = (pre * gate).astype(BF16)
            s1[pair + half, pl.ds(to, 192)] = gate * (1.0 + pre * (1.0 - gate))
        return carry

    lax.fori_loop(0, 20, first_step, 0)

    def clear(ref, planes, offset, top, bottom, width):
        for j in range(planes):

            @pl.when(jnp.logical_not(inside(slab + offset + j)))
            def _():
                ref[j] = jnp.zeros((1024, width), BF16)

        @pl.when(coil == 0)
        def _():
            for j in range(planes):
                ref[j, 0:top] = jnp.zeros((top, width), BF16)

        @pl.when(coil == 7)
        def _():
            for j in range(planes):
                ref[j, bottom:1024] = jnp.zeros((1024 - bottom, width), BF16)

    clear(a1, 8, -3, 72, 840, NZ)

    def second_step(step, carry):
        pair, block = 2 * (step // 5), step % 5
        at = pl.multiple_of(8 * block, 8)
        to = pl.multiple_of(192 * block, 192)
        stacked = jnp.concatenate(
            [
                jnp.concatenate(
                    [a1[pair + dx, pl.ds(to, 256)], a1[pair + dx + 1, pl.ds(to, 256)]], 1
                )
                for dx in range(3)
            ],
            0,
        )
        parts = mm(t2_ref[...], stacked)
        for half in range(2):
            pre = join_z(parts, 192, half, low, high)
            gate = jax.nn.sigmoid(pre)
            a2[pair + half, pl.ds(to, 192)] = (pre * gate).astype(BF16)
            slope = gate * (1.0 + pre * (1.0 - gate))
            pieces = []
            for dx in range(3):
                for ch in range(2):
                    pieces.append(
                        jnp.concatenate(
                            [
                                cots[pair + half + dx, ch, pl.ds(at, 16)],
                                cots[pair + half + dx, 2 + ch, pl.ds(at, 16)],
                            ],
                            1,
                        ).astype(BF16)
                    )
            back = mm(t3t_ref[...], jnp.concatenate(pieces, 0))
            for which in range(2):
                grad = join_z(back, 192, which, low, high) * slope
                e2[pair + half, pl.ds(to, 192), which * NZ : which * NZ + NZ] = grad.astype(BF16)
        return carry

    lax.fori_loop(0, 15, second_step, 0)
    clear(a2, 6, -2, 48, 816, NZ)
    clear(e2, 6, -2, 48, 816, 2 * NZ)

    def third_step(step, carry):
        plane, block = step // 5, step % 5
        to = pl.multiple_of(192 * block, 192)
        stacked = jnp.concatenate([e2[plane + dx, pl.ds(to, 256)] for dx in range(3)], 0)
        back = mm(t2t_ref[...], stacked)
        slope = s1[plane + 2, pl.ds(to + 48, 192)]
        for which in range(2):
            grad = join_z(back, 192, which, low, high) * slope
            e1[plane, pl.ds(to, 192), which * NZ : which * NZ + NZ] = grad.astype(BF16)
        return carry

    lax.fori_loop(0, 15, third_step, 0)
    clear(e1, 3, -1, 24, 792, 2 * NZ)

    low16, high16 = at_edges(16)
    for pair in range(2):
        stacked = jnp.concatenate(
            [
                jnp.concatenate(
                    [
                        a2[1 + dx, 24 + 384 * pair : 280 + 384 * pair],
                        a2[1 + dx, 216 + 384 * pair : 472 + 384 * pair],
                    ],
                    1,
                )
                for dx in range(3)
            ],
            0,
        )
        parts = mm(t3_ref[...], stacked)
        for half in range(2):
            update = join_z(parts, 16, half, low16, high16)
            at = 16 * pair + 8 * half
            for ch in range(2):
                new_ref[ch, at : at + 8] = (
                    relaxed_ref[ch, at : at + 8] + update[8 * ch : 8 * ch + 8]
                )

    for block in range(4):
        stacked = jnp.concatenate([e1[dx, 192 * block : 192 * block + 256] for dx in range(3)], 0)
        back = mm(t1t_ref[...], stacked)
        for which in range(2):
            grad = join_z(back, 16, which, low16, high16)
            for ch in range(2):
                rows = slice(8 * block, 8 * block + 8)
                if which == 0:
                    base = (2 * bits_ref[ch, rows] - 1).astype(F32)
                else:
                    base = adj_ref[ch, rows]
                pulled_ref[2 * which + ch, rows] = base + grad[8 * ch : 8 * ch + 8]
    for ch in range(4):
        rows = pulled_ref[ch].astype(BF16)
        for dest in range(8):
            send_ref[dest, ch] = rows


def normal_kernel(field_ref, maps_ref, mask_ref, yh, yl, zh, zl, out_ref):
    tabs = (yh, yl, zh, zl)
    weight = mask_ref[...].astype(F32)
    map_re, map_im = maps_ref[0], maps_ref[1]
    for which in range(2):
        re = field_ref[:, 2 * which].reshape(NY, NZ).astype(F32)
        im = field_ref[:, 2 * which + 1].reshape(NY, NZ).astype(F32)
        f_re, f_im = forward(map_re * re - map_im * im, map_re * im + map_im * re, tabs)
        b_re, b_im = inverse(weight * f_re, weight * f_im, tabs)
        out_re = (map_re * b_re + map_im * b_im).astype(BF16)
        out_im = (map_re * b_im - map_im * b_re).astype(BF16)
        for dest in range(8):
            rows = slice(NYL * dest, NYL * dest + NYL)
            out_ref[dest, 2 * which] = out_re[rows]
            out_ref[dest, 2 * which + 1] = out_im[rows]


def final_kernel(got_ref, pulled_ref, loss_ref, probe_ref, next_ref):
    for ch in range(4):
        total = got_ref[0, ch].astype(F32)
        for source in range(1, 8):
            total = total + got_ref[source, ch].astype(F32)
        result = pulled_ref[ch] - STEP * total
        if ch < 2:
            probe_ref[ch] = result
        else:
            next_ref[ch - 2] = loss_ref[ch - 2] + result


def on_device(
    coil_maps,
    kspace,
    sample_mask,
    iterate,
    probe_bits,
    loss_gradient,
    adjoint,
    kernel_first,
    kernel_second,
    kernel_last,
):
    maps = coil_maps[0, :, 0]
    data = kspace[0, :, 0]
    iterate, bits, loss, adj = (
        a[:, 0] for a in (iterate, probe_bits, loss_gradient, adjoint)
    )
    fourier = [jnp.asarray(t) for t in fourier_constants()]
    place = jnp.stack([lax.axis_index("coil"), lax.axis_index("slab")]).astype(jnp.int32)
    smem = pl.BlockSpec(memory_space=pltpu.SMEM)

    toeplitz = tables(kernel_first, kernel_second, kernel_last)
    field = lax.all_to_all(jnp.broadcast_to(iterate[None], (8,) + iterate.shape), "coil", 0, 0)
    partial_sums = pl.pallas_call(
        gradient_kernel,
        out_shape=jax.ShapeDtypeStruct((8, 3, HALO_ROWS, NZ), BF16),
        in_specs=whole(10),
        out_specs=whole(1)[0],
        scratch_shapes=[pltpu.VMEM((2, NY + 8, NZ), F32)],
    )(field, maps, data, sample_mask, bits, adj, *fourier)
    got = lax.all_to_all(partial_sums, "coil", 0, 0)
    payload, relaxed = pl.pallas_call(
        relax_kernel,
        out_shape=[
            jax.ShapeDtypeStruct((16, 6, HALO_ROWS, NZ), BF16),
            jax.ShapeDtypeStruct((2, NYL, NZ), F32),
        ],
        in_specs=[smem] + whole(4),
        out_specs=whole(2),
        scratch_shapes=[pltpu.VMEM((2, NY + 8, NZ), F32), pltpu.VMEM((4, HALO_ROWS, NZ), F32)],
    )(place, got, field, bits, adj)
    planes = lax.all_to_all(payload, "slab", 0, 0)
    new_iterate, pulled, send = pl.pallas_call(
        denoise_kernel,
        out_shape=[
            jax.ShapeDtypeStruct((2, NYL, NZ), F32),
            jax.ShapeDtypeStruct((4, NYL, NZ), F32),
            jax.ShapeDtypeStruct((8, 4, NYL, NZ), BF16),
        ],
        in_specs=[smem] + whole(10),
        out_specs=whole(3),
        scratch_shapes=[
            pltpu.VMEM((10, 2, 48, NZ), F32),
            pltpu.VMEM((8, 4, 48, NZ), F32),
            pltpu.VMEM((8, 1024, NZ), BF16),
            pltpu.VMEM((8, 1024, NZ), F32),
            pltpu.VMEM((6, 1024, NZ), BF16),
            pltpu.VMEM((6, 1024, 2 * NZ), BF16),
            pltpu.VMEM((3, 1024, 2 * NZ), BF16),
        ],
        compiler_params=pltpu.CompilerParams(vmem_limit_bytes=VMEM_BIG),
    )(place, planes, relaxed, bits, adj, *toeplitz)
    spread = lax.all_to_all(send, "coil", 0, 0)
    back = pl.pallas_call(
        normal_kernel,
        out_shape=jax.ShapeDtypeStruct((8, 4, NYL, NZ), BF16),
        in_specs=whole(7),
        out_specs=whole(1)[0],
    )(spread, maps, sample_mask, *fourier)
    back = lax.all_to_all(back, "coil", 0, 0)
    probe, following = pl.pallas_call(
        final_kernel,
        out_shape=[jax.ShapeDtypeStruct((2, NYL, NZ), F32)] * 2,
        in_specs=whole(3),
        out_specs=whole(2),
    )(back, pulled, loss)
    return new_iterate[:, None], probe[:, None], following[:, None]


def solution(mesh):
    image = P(None, "slab", "coil", None)
    coils = P("coil", None, "slab", None, None)
    return jax.shard_map(
        on_device,
        mesh=mesh,
        in_specs=(coils, coils, P(), image, image, image, image, P(), P(), P()),
        out_specs=(image, image, image),
        check_vma=False,
    )
```

time: 687 us -> 115 us (0.17); the launches traced: 677 us -> 114 us
  matrix products: 286 us -> 0 us
  local copies, waits for them, and re-layouts: 123 us -> 2.42 us
  starting transfers between devices: 114 us -> 11 us
  waiting for transfers between devices: 68.4 us -> 20.4 us
  Pallas kernels: 0 us -> 44.2 us
  blocking collectives: 56.9 us -> 35 us
  between operations: 16.3 us -> 0.67 us
  other arithmetic: 11.2 us -> 0.65 us
    conv_general_dilated x9 -> x0, matrix products: 253 us -> none  [convolve_local(): lax.conv_general_dilated(haloed, kernel, (1, 1, 1), ((0, 0), (0, 0), (1,...]
    ppermute x36 -> x0, starting transfers between devices: 114 us -> none  [the longest x18 90.8 us: with_halo(): lax.ppermute(tail, axis, [(i, (i + 1) % count) for i in range(ends)])]
    psum x2 -> x0, waiting for transfers between devices: 66.6 us -> none  [the longest x1 59.6 us: on_device(): summed = lax.psum(partial_sum, 'coil')]
    conv_general_dilated x24 -> x0, local copies, waits for them, and re-layouts: 63.4 us -> none  [convolve_local(): lax.conv_general_dilated(haloed, kernel, (1, 1, 1), ((0, 0), (0, 0), (1,...]
    all_gather x2 -> x0, blocking collectives: 56.9 us -> none  [the longest x1 28.6 us: on_device(): lax.all_gather(pulled.astype(jnp.bfloat16), 'coil', axis=3, tiled=True)]
    pallas_call x0 -> x6, Pallas kernels: none -> 44.2 us  [the longest x1 28.6 us: on_device(): pl.pallas_call(denoise_kernel, out_shape=[jax.ShapeDtypeStruct((2, NYL, N...]
    all_to_all x0 -> x3, blocking collectives: none -> 35 us  [the longest x1 12.9 us: on_device(): lax.all_to_all(jnp.broadcast_to(iterate[None], (8,) + iterate.shape), 'co...]
    dot_general x32 -> x0, matrix products: 33.2 us -> none  [the longest x4 6.01 us: spectrum(): jnp.einsum('yv,...vz->...yz', height_cos, along_real, precision=highest)]
  transfers between devices with their start and end apart: 38 -> 2, of which waited for: 4 -> 2; matrix products, arithmetic and copies ran while one was open for 37% -> 1% of each run, Pallas kernels for 0% -> 3%
where the time goes in v1:
time: 115 us; the launch traced here: 114 us
  Pallas kernels  44.2 us (38%)
  blocking collectives  35 us (30%)
  waiting for transfers between devices  20.4 us (18%)
  starting transfers between devices  11 us (10%)
  local copies, waits for them, and re-layouts  2.42 us (2%)
    pallas_call x1, Pallas kernels, on_device(): pl.pallas_call(denoise_kernel, out_shape=[jax.ShapeDtypeStruct((2, NYL, N...  28.6 us
    all_to_all x1, waiting for transfers between devices, on_device(): planes = lax.all_to_all(payload, 'slab', 0, 0)  14.3 us
    all_to_all x1, blocking collectives, on_device(): lax.all_to_all(jnp.broadcast_to(iterate[None], (8,) + iterate.shape), 'co...  12.9 us
    all_to_all x1, blocking collectives, on_device(): spread = lax.all_to_all(send, 'coil', 0, 0)  11.2 us
    all_to_all x1, blocking collectives, on_device(): back = lax.all_to_all(back, 'coil', 0, 0)  11 us
    all_to_all x1, starting transfers between devices, on_device(): planes = lax.all_to_all(payload, 'slab', 0, 0)  7.59 us
    all_to_all x1, waiting for transfers between devices, on_device(): got = lax.all_to_all(partial_sums, 'coil', 0, 0)  6.14 us
    pallas_call x1, Pallas kernels, on_device(): pl.pallas_call(normal_kernel, out_shape=jax.ShapeDtypeStruct((8, 4, NYL,...  4.93 us
  transfers between devices with their start and end apart: 2, of which 2 were waited for; matrix products, arithmetic and copies ran while one was open for 1% of the time, Pallas kernels for 3%

profile of v1, /device:TPU:0, one launch (start us, length us, event | category | flops | bytes accessed | tf_op | source)
XLA Modules:
  0.0 114.3 jit_solution(4936327519016530316)
XLA Ops:
  0.6 0.8 broadcast_in_dim.17
  1.4 12.9 %all_to_all.25.field_ref = f32[8,2,32,128]{3,2,1,0:T(8,128)} all-to-all(f32[8,2,32,128]{3,2,1,0:T(8,128)S(1)} %broadcast_in_dim.17), channel_id=1, replica_groups=mesh['coil'=8,'slab'=16] {'coil'}, dimensions={0} | all-to-all | bytes 524288 | tf_op jit(solution)/shard_map/all_to_all | solution.py:481
  14.3 3.8 %shard_map.157 = bf16[8,3,40,128]{3,2,1,0:T(8,128)(2,1)} custom-call(f32[8,2,32,128]{3,2,1,0:T(8,128)} %all_to_all.25.field_ref, f32[2,256,128]{2,1,0:T(8,128)} %bitcast.26, f32[2,256,128]{2,1,0:T(8,128)} %bitcast.34, s32[256,128]{1,0:T(8,128)} %mask_ref.3, s32[2,32,128]{2,1,0:T(8,128)} %bitcast.28, f32[2,32,128]{2,1,0:T(8,128)} %bitcast.31, ...), custom_call_target="tpu_custom_call" | custom-call | tf_op jit(solution)/shard_map/pallas_call | solution.py:482
  18.1 3.4 %all-to-all-start.1 = ((bf16[8,3,40,128]{3,2,1,0:T(8,128)(2,1)}), bf16[8,3,40,128]{3,2,1,0:T(8,128)(2,1)S(1)}, u32[]{:S(2)}, u32[]{:S(2)}) async-start(bf16[8,3,40,128]{3,2,1,0:T(8,128)(2,1)} %shard_map.157), calls=%async_computation.1 | async-start | bytes 491520 | tf_op jit(solution)/shard_map/all_to_all | solution.py:489
  21.5 0.7 pad_add_fusion.place_ref
  22.2 6.1 %all-to-all-done.1.got_ref = bf16[8,3,40,128]{3,2,1,0:T(8,128)(2,1)S(1)} async-done(((bf16[8,3,40,128]{3,2,1,0:T(8,128)(2,1)}), bf16[8,3,40,128]{3,2,1,0:T(8,128)(2,1)S(1)}, u32[]{:S(2)}, u32[]{:S(2)}) %all-to-all-start.1) | async-done | bytes 245792 | tf_op jit(solution)/shard_map/all_to_all | solution.py:489
  28.3 0.0 copy-start.1
  28.3 0.7 copy-done.1
  29.0 2.1 %shard_map.158 = (bf16[16,6,40,128]{3,2,1,0:T(8,128)(2,1)}, f32[2,32,128]{2,1,0:T(8,128)}) custom-call(s32[2]{0:T(128)} %pad_add_fusion.place_ref, bf16[8,3,40,128]{3,2,1,0:T(8,128)(2,1)} %copy-done.1, f32[8,2,32,128]{3,2,1,0:T(8,128)} %all_to_all.25.field_ref, s32[2,32,128]{2,1,0:T(8,128)} %bitcast.29, f32[2,32,128]{2,1,0:T(8,128)} %bitcast.32), custom_call_target="tpu_custom_call" | custom-call | tf_op jit(solution)/shard_map/pallas_call | solution.py:490
  31.1 7.6 %all-to-all-start.2 = ((bf16[16,6,40,128]{3,2,1,0:T(8,128)(2,1)}), bf16[16,6,40,128]{3,2,1,0:T(8,128)(2,1)S(1)}, u32[]{:S(2)}, u32[]{:S(2)}) async-start(bf16[16,6,40,128]{3,2,1,0:T(8,128)(2,1)} %get-tuple-element.16), calls=%async_computation.2 | async-start | bytes 1966080 | tf_op jit(solution)/shard_map/all_to_all | solution.py:500
  38.7 3.0 %shard_map.159 = (bf16[576,96]{1,0:T(8,128)(2,1)}, bf16[576,768]{1,0:T(8,128)(2,1)}, bf16[48,768]{1,0:T(8,128)(2,1)}, bf16[48,768]{1,0:T(8,128)(2,1)}, bf16[576,...) custom-call(bf16[27,2,24]{2,1,0:T(2,128)(2,1)} %bitcast.41, bf16[27,24,24]{2,1,0:T(8,128)(2,1)} %bitcast.37, ...), custom_call_target="tpu_custom_call" | custom-call | flops 1000000000 | bytes 4000000 | tf_op jit(solution)/shard_map/pallas_call | solution.py:214
  41.7 14.3 %all-to-all-done.2.planes_ref = bf16[16,6,40,128]{3,2,1,0:T(8,128)(2,1)S(1)} async-done(((bf16[16,6,40,128]{3,2,1,0:T(8,128)(2,1)}), bf16[16,6,40,128]{3,2,1,0:T(8,128)(2,1)S(1)}, u32[]{:S(2)}, u32[]{:S(2)}) %all-to-all-start.2) | async-done | bytes 983072 | tf_op jit(solution)/shard_map/all_to_all | solution.py:500
  56.0 0.0 copy-start
  56.0 0.9 copy-done
  56.9 28.6 %shard_map.160 = (f32[2,32,128]{2,1,0:T(8,128)}, f32[4,32,128]{2,1,0:T(8,128)}, bf16[8,4,32,128]{3,2,1,0:T(8,128)(2,1)}) custom-call(s32[2]{0:T(128)} %pad_add_fusion.place_ref, bf16[16,6,40,128]{3,2,1,0:T(8,128)(2,1)} %copy-done, f32[2,32,128]{2,1,0:T(8,128)} %get-tuple-element.17.relaxed_ref, s32[2,32,128]{2,1,0:T(8,128)} %bitcast.30, ...), custom_call_target="tpu_custom_call" | custom-call | tf_op jit(solution)/shard_map/pallas_call | solution.py:501
  85.6 11.2 %all_to_all.26.field_ref = bf16[8,4,32,128]{3,2,1,0:T(8,128)(2,1)} all-to-all(bf16[8,4,32,128]{3,2,1,0:T(8,128)(2,1)} %get-tuple-element.25), channel_id=1, replica_groups=mesh['coil'=8,'slab'=16] {'coil'}, dimensions={0} | all-to-all | bytes 524288 | tf_op jit(solution)/shard_map/all_to_all | solution.py:521
  96.8 4.9 %shard_map.161 = bf16[8,4,32,128]{3,2,1,0:T(8,128)(2,1)} custom-call(bf16[8,4,32,128]{3,2,1,0:T(8,128)(2,1)} %all_to_all.26.field_ref, f32[2,256,128]{2,1,0:T(8,128)} %bitcast.27, s32[256,128]{1,0:T(8,128)} %mask_ref.3, bf16[512,256]{1,0:T(8,128)(2,1)} %constant.17.clone.yh, bf16[512,256]{1,0:T(8,128)(2,1)} %constant.18.clone.yl, ...), custom_call_target="tpu_custom_call" | custom-call | tf_op jit(solution)/shard_map/pallas_call | solution.py:522
  101.7 11.0 %all_to_all.27.got_ref = bf16[8,4,32,128]{3,2,1,0:T(8,128)(2,1)} all-to-all(bf16[8,4,32,128]{3,2,1,0:T(8,128)(2,1)} %shard_map.161), channel_id=1, replica_groups=mesh['coil'=8,'slab'=16] {'coil'}, dimensions={0} | all-to-all | bytes 524288 | tf_op jit(solution)/shard_map/all_to_all | solution.py:528
  112.7 1.6 %shard_map.162 = (f32[2,32,128]{2,1,0:T(8,128)}, f32[2,32,128]{2,1,0:T(8,128)}) custom-call(bf16[8,4,32,128]{3,2,1,0:T(8,128)(2,1)} %all_to_all.27.got_ref, f32[4,32,128]{2,1,0:T(8,128)} %get-tuple-element.26.pulled_ref, f32[2,32,128]{2,1,0:T(8,128)} %bitcast.36), custom_call_target="tpu_custom_call" | custom-call | tf_op jit(solution)/shard_map/pallas_call | solution.py:529
Async XLA Ops:
  18.1 10.2 %all-to-all-start.1 = ((bf16[8,3,40,128]{3,2,1,0:T(8,128)(2,1)}), bf16[8,3,40,128]{3,2,1,0:T(8,128)(2,1)S(1)}, u32[]{:S(2)}, u32[]{:S(2)}) async-start(bf16[8,3,40,128]{3,2,1,0:T(8,128)(2,1)} %shard_map.157), calls=%async_computation.1 | async-start | bytes 491520 | tf_op jit(solution)/shard_map/all_to_all | solution.py:489
  28.3 0.7 copy-start.1
  31.1 24.9 %all-to-all-start.2 = ((bf16[16,6,40,128]{3,2,1,0:T(8,128)(2,1)}), bf16[16,6,40,128]{3,2,1,0:T(8,128)(2,1)S(1)}, u32[]{:S(2)}, u32[]{:S(2)}) async-start(bf16[16,6,40,128]{3,2,1,0:T(8,128)(2,1)} %get-tuple-element.16), calls=%async_computation.2 | async-start | bytes 1966080 | tf_op jit(solution)/shard_map/all_to_all | solution.py:500
  56.0 0.9 copy-start

commit v2 on v1

--- a/solution.py
+++ b/solution.py
@@ -309,7 +309,7 @@
             s1[pair + half, pl.ds(to, 192)] = gate * (1.0 + pre * (1.0 - gate))
         return carry
 
-    lax.fori_loop(0, 20, first_step, 0)
+    lax.fori_loop(0, 20, first_step, 0, unroll=5)
 
     def clear(ref, planes, offset, top, bottom, width):
         for j in range(planes):
@@ -367,7 +367,7 @@
                 e2[pair + half, pl.ds(to, 192), which * NZ : which * NZ + NZ] = grad.astype(BF16)
         return carry
 
-    lax.fori_loop(0, 15, second_step, 0)
+    lax.fori_loop(0, 15, second_step, 0, unroll=5)
     clear(a2, 6, -2, 48, 816, NZ)
     clear(e2, 6, -2, 48, 816, 2 * NZ)
 
@@ -382,7 +382,7 @@
             e1[plane, pl.ds(to, 192), which * NZ : which * NZ + NZ] = grad.astype(BF16)
         return carry
 
-    lax.fori_loop(0, 15, third_step, 0)
+    lax.fori_loop(0, 15, third_step, 0, unroll=5)
     clear(e1, 3, -1, 24, 792, 2 * NZ)
 
     low16, high16 = at_edges(16)

time: 115 us -> 105 us (0.913)
  Pallas kernels: 44.2 us -> 34.2 us
    pallas_call x1, Pallas kernels: 28.6 us -> 18.6 us  [on_device(): pl.pallas_call(denoise_kernel, out_shape=[jax.ShapeDtypeStruct((2, NYL, N...]
where the time goes in v2:
time: 105 us; the launch traced here: 104 us
  blocking collectives  35 us (33%)
  Pallas kernels  34.2 us (33%)
  waiting for transfers between devices  20.4 us (19%)
  starting transfers between devices  11 us (10%)
  local copies, waits for them, and re-layouts  2.42 us (2%)
    pallas_call x1, Pallas kernels, on_device(): pl.pallas_call(denoise_kernel, out_shape=[jax.ShapeDtypeStruct((2, NYL, N...  18.6 us
    all_to_all x1, waiting for transfers between devices, on_device(): planes = lax.all_to_all(payload, 'slab', 0, 0)  14.3 us
    all_to_all x1, blocking collectives, on_device(): lax.all_to_all(jnp.broadcast_to(iterate[None], (8,) + iterate.shape), 'co...  12.9 us
    all_to_all x1, blocking collectives, on_device(): spread = lax.all_to_all(send, 'coil', 0, 0)  11.2 us
    all_to_all x1, blocking collectives, on_device(): back = lax.all_to_all(back, 'coil', 0, 0)  11 us
    all_to_all x1, starting transfers between devices, on_device(): planes = lax.all_to_all(payload, 'slab', 0, 0)  7.59 us
    all_to_all x1, waiting for transfers between devices, on_device(): got = lax.all_to_all(partial_sums, 'coil', 0, 0)  6.14 us
    pallas_call x1, Pallas kernels, on_device(): pl.pallas_call(normal_kernel, out_shape=jax.ShapeDtypeStruct((8, 4, NYL,...  4.93 us
  transfers between devices with their start and end apart: 2, of which 2 were waited for; matrix products, arithmetic and copies ran while one was open for 1% of the time, Pallas kernels for 3%

profile of v2, /device:TPU:0, one launch (start us, length us, event | category | flops | bytes accessed | tf_op | source)
XLA Modules:
  0.0 104.3 jit_solution(163944505598546418)
XLA Ops:
  0.6 0.8 broadcast_in_dim.17
  1.4 12.9 %all_to_all.25.field_ref = f32[8,2,32,128]{3,2,1,0:T(8,128)} all-to-all(f32[8,2,32,128]{3,2,1,0:T(8,128)S(1)} %broadcast_in_dim.17), channel_id=1, replica_groups=mesh['coil'=8,'slab'=16] {'coil'}, dimensions={0} | all-to-all | bytes 524288 | tf_op jit(solution)/shard_map/all_to_all | solution.py:481
  14.3 3.8 %shard_map.157 = bf16[8,3,40,128]{3,2,1,0:T(8,128)(2,1)} custom-call(f32[8,2,32,128]{3,2,1,0:T(8,128)} %all_to_all.25.field_ref, f32[2,256,128]{2,1,0:T(8,128)} %bitcast.26, f32[2,256,128]{2,1,0:T(8,128)} %bitcast.34, s32[256,128]{1,0:T(8,128)} %mask_ref.3, s32[2,32,128]{2,1,0:T(8,128)} %bitcast.28, f32[2,32,128]{2,1,0:T(8,128)} %bitcast.31, ...), custom_call_target="tpu_custom_call" | custom-call | tf_op jit(solution)/shard_map/pallas_call | solution.py:482
  18.1 3.4 %all-to-all-start.1 = ((bf16[8,3,40,128]{3,2,1,0:T(8,128)(2,1)}), bf16[8,3,40,128]{3,2,1,0:T(8,128)(2,1)S(1)}, u32[]{:S(2)}, u32[]{:S(2)}) async-start(bf16[8,3,40,128]{3,2,1,0:T(8,128)(2,1)} %shard_map.157), calls=%async_computation.1 | async-start | bytes 491520 | tf_op jit(solution)/shard_map/all_to_all | solution.py:489
  21.5 0.7 pad_add_fusion.place_ref
  22.2 6.1 %all-to-all-done.1.got_ref = bf16[8,3,40,128]{3,2,1,0:T(8,128)(2,1)S(1)} async-done(((bf16[8,3,40,128]{3,2,1,0:T(8,128)(2,1)}), bf16[8,3,40,128]{3,2,1,0:T(8,128)(2,1)S(1)}, u32[]{:S(2)}, u32[]{:S(2)}) %all-to-all-start.1) | async-done | bytes 245792 | tf_op jit(solution)/shard_map/all_to_all | solution.py:489
  28.3 0.0 copy-start.1
  28.3 0.7 copy-done.1
  29.0 2.1 %shard_map.158 = (bf16[16,6,40,128]{3,2,1,0:T(8,128)(2,1)}, f32[2,32,128]{2,1,0:T(8,128)}) custom-call(s32[2]{0:T(128)} %pad_add_fusion.place_ref, bf16[8,3,40,128]{3,2,1,0:T(8,128)(2,1)} %copy-done.1, f32[8,2,32,128]{3,2,1,0:T(8,128)} %all_to_all.25.field_ref, s32[2,32,128]{2,1,0:T(8,128)} %bitcast.29, f32[2,32,128]{2,1,0:T(8,128)} %bitcast.32), custom_call_target="tpu_custom_call" | custom-call | tf_op jit(solution)/shard_map/pallas_call | solution.py:490
  31.1 7.6 %all-to-all-start.2 = ((bf16[16,6,40,128]{3,2,1,0:T(8,128)(2,1)}), bf16[16,6,40,128]{3,2,1,0:T(8,128)(2,1)S(1)}, u32[]{:S(2)}, u32[]{:S(2)}) async-start(bf16[16,6,40,128]{3,2,1,0:T(8,128)(2,1)} %get-tuple-element.16), calls=%async_computation.2 | async-start | bytes 1966080 | tf_op jit(solution)/shard_map/all_to_all | solution.py:500
  38.7 3.0 %shard_map.159 = (bf16[576,96]{1,0:T(8,128)(2,1)}, bf16[576,768]{1,0:T(8,128)(2,1)}, bf16[48,768]{1,0:T(8,128)(2,1)}, bf16[48,768]{1,0:T(8,128)(2,1)}, bf16[576,...) custom-call(bf16[27,2,24]{2,1,0:T(2,128)(2,1)} %bitcast.41, bf16[27,24,24]{2,1,0:T(8,128)(2,1)} %bitcast.37, ...), custom_call_target="tpu_custom_call" | custom-call | flops 1000000000 | bytes 4000000 | tf_op jit(solution)/shard_map/pallas_call | solution.py:214
  41.7 14.3 %all-to-all-done.2.planes_ref = bf16[16,6,40,128]{3,2,1,0:T(8,128)(2,1)S(1)} async-done(((bf16[16,6,40,128]{3,2,1,0:T(8,128)(2,1)}), bf16[16,6,40,128]{3,2,1,0:T(8,128)(2,1)S(1)}, u32[]{:S(2)}, u32[]{:S(2)}) %all-to-all-start.2) | async-done | bytes 983072 | tf_op jit(solution)/shard_map/all_to_all | solution.py:500
  56.0 0.0 copy-start
  56.0 0.9 copy-done
  56.9 18.6 %shard_map.160 = (f32[2,32,128]{2,1,0:T(8,128)}, f32[4,32,128]{2,1,0:T(8,128)}, bf16[8,4,32,128]{3,2,1,0:T(8,128)(2,1)}) custom-call(s32[2]{0:T(128)} %pad_add_fusion.place_ref, bf16[16,6,40,128]{3,2,1,0:T(8,128)(2,1)} %copy-done, f32[2,32,128]{2,1,0:T(8,128)} %get-tuple-element.17.relaxed_ref, s32[2,32,128]{2,1,0:T(8,128)} %bitcast.30, ...), custom_call_target="tpu_custom_call" | custom-call | tf_op jit(solution)/shard_map/pallas_call | solution.py:501
  75.6 11.2 %all_to_all.26.field_ref = bf16[8,4,32,128]{3,2,1,0:T(8,128)(2,1)} all-to-all(bf16[8,4,32,128]{3,2,1,0:T(8,128)(2,1)} %get-tuple-element.25), channel_id=1, replica_groups=mesh['coil'=8,'slab'=16] {'coil'}, dimensions={0} | all-to-all | bytes 524288 | tf_op jit(solution)/shard_map/all_to_all | solution.py:521
  86.8 4.9 %shard_map.161 = bf16[8,4,32,128]{3,2,1,0:T(8,128)(2,1)} custom-call(bf16[8,4,32,128]{3,2,1,0:T(8,128)(2,1)} %all_to_all.26.field_ref, f32[2,256,128]{2,1,0:T(8,128)} %bitcast.27, s32[256,128]{1,0:T(8,128)} %mask_ref.3, bf16[512,256]{1,0:T(8,128)(2,1)} %constant.17.clone.yh, bf16[512,256]{1,0:T(8,128)(2,1)} %constant.18.clone.yl, ...), custom_call_target="tpu_custom_call" | custom-call | tf_op jit(solution)/shard_map/pallas_call | solution.py:522
  91.7 11.0 %all_to_all.27.got_ref = bf16[8,4,32,128]{3,2,1,0:T(8,128)(2,1)} all-to-all(bf16[8,4,32,128]{3,2,1,0:T(8,128)(2,1)} %shard_map.161), channel_id=1, replica_groups=mesh['coil'=8,'slab'=16] {'coil'}, dimensions={0} | all-to-all | bytes 524288 | tf_op jit(solution)/shard_map/all_to_all | solution.py:528
  102.7 1.6 %shard_map.162 = (f32[2,32,128]{2,1,0:T(8,128)}, f32[2,32,128]{2,1,0:T(8,128)}) custom-call(bf16[8,4,32,128]{3,2,1,0:T(8,128)(2,1)} %all_to_all.27.got_ref, f32[4,32,128]{2,1,0:T(8,128)} %get-tuple-element.26.pulled_ref, f32[2,32,128]{2,1,0:T(8,128)} %bitcast.36), custom_call_target="tpu_custom_call" | custom-call | tf_op jit(solution)/shard_map/pallas_call | solution.py:529
Async XLA Ops:
  18.1 10.2 %all-to-all-start.1 = ((bf16[8,3,40,128]{3,2,1,0:T(8,128)(2,1)}), bf16[8,3,40,128]{3,2,1,0:T(8,128)(2,1)S(1)}, u32[]{:S(2)}, u32[]{:S(2)}) async-start(bf16[8,3,40,128]{3,2,1,0:T(8,128)(2,1)} %shard_map.157), calls=%async_computation.1 | async-start | bytes 491520 | tf_op jit(solution)/shard_map/all_to_all | solution.py:489
  28.3 0.7 copy-start.1
  31.1 24.9 %all-to-all-start.2 = ((bf16[16,6,40,128]{3,2,1,0:T(8,128)(2,1)}), bf16[16,6,40,128]{3,2,1,0:T(8,128)(2,1)S(1)}, u32[]{:S(2)}, u32[]{:S(2)}) async-start(bf16[16,6,40,128]{3,2,1,0:T(8,128)(2,1)} %get-tuple-element.16), calls=%async_computation.2 | async-start | bytes 1966080 | tf_op jit(solution)/shard_map/all_to_all | solution.py:500
  56.0 0.9 copy-start

commit v3 on v2

v3 whole, which is shorter than its diff:
```python
import math

import jax
import jax.numpy as jnp
import numpy as np
from jax import lax
from jax.experimental import pallas as pl
from jax.experimental.pallas import tpu as pltpu
from jax.sharding import PartitionSpec as P

STEP = 0.8
F32 = jnp.float32
BF16 = jnp.bfloat16
NZ = 128
NY = 256
NYL = 32
HALO_ROWS = 40
HALF = 16
PART_ROWS = 24
GRANT = pltpu.CompilerParams(vmem_limit_bytes=24 << 20)


def whole(count):
    return [pl.BlockSpec(memory_space=pltpu.VMEM)] * count


def split_host(table):
    high = table.astype(np.float32).astype(jnp.bfloat16)
    low = (table - high.astype(np.float64)).astype(jnp.bfloat16)
    return high, low


def fourier_constants():
    def cos_sin(length):
        index = np.arange(length)
        angles = (index[:, None] * index[None, :] % length) * (2.0 * math.pi / length)
        return np.cos(angles) / math.sqrt(length), np.sin(angles) / math.sqrt(length)

    cos_y, sin_y = cos_sin(NY)
    cos_z, sin_z = cos_sin(NZ)
    along_y = np.concatenate([cos_y, sin_y], axis=0)
    along_z = np.block([[cos_z, -sin_z], [sin_z, cos_z]])
    return split_host(along_y) + split_host(along_z)


def split(values):
    high = values.astype(BF16)
    return high, (values - high.astype(F32)).astype(BF16)


def mm(left, right):
    return jnp.dot(left, right, preferred_element_type=F32)


def along_z(joined, high_ref, low_ref):
    high, low = split(joined)
    return mm(high, high_ref[...]) + (mm(high, low_ref[...]) + mm(low, high_ref[...]))


def along_y(joined, high_ref, low_ref):
    high, low = split(joined)
    return mm(high_ref[...], high) + (mm(low_ref[...], high) + mm(high_ref[...], low))


def forward(real, imag, tabs):
    y_high, y_low, z_high, z_low = tabs
    turned = along_y(along_z(jnp.concatenate([real, imag], 1), z_high, z_low), y_high, y_low)
    cos_part, sin_part = turned[:NY], turned[NY:]
    return cos_part[:, :NZ] + sin_part[:, NZ:], cos_part[:, NZ:] - sin_part[:, :NZ]


def inverse(real, imag, tabs):
    y_high, y_low, z_high, z_low = tabs
    turned = along_y(jnp.concatenate([real, imag], 1), y_high, y_low)
    cos_part, sin_part = turned[:NY], turned[NY:]
    back = cos_part[:, :NZ] - sin_part[:, NZ:], -(cos_part[:, NZ:] + sin_part[:, :NZ])
    turned = along_z(jnp.concatenate(back, 1), z_high, z_low)
    return turned[:, :NZ], -turned[:, NZ:]


def gradient_kernel(
    field_ref,
    maps_ref,
    kspace_ref,
    mask_ref,
    iterate_ref,
    bits_ref,
    adj_ref,
    yh,
    yl,
    zh,
    zl,
    out_ref,
    pad,
):
    tabs = (yh, yl, zh, zl)
    weight = mask_ref[...].astype(F32)
    map_re, map_im = maps_ref[0], maps_ref[1]
    re = field_ref[:, 0].astype(F32).reshape(NY, NZ)
    im = field_ref[:, 1].astype(F32).reshape(NY, NZ)
    f_re, f_im = forward(map_re * re - map_im * im, map_re * im + map_im * re, tabs)
    f_re = weight * (f_re - kspace_ref[0])
    f_im = weight * (f_im - kspace_ref[1])
    b_re, b_im = inverse(f_re, f_im, tabs)
    zero = jnp.zeros((4, NZ), F32)
    for ch in range(2):
        pad[ch, 0:4] = zero
        pad[ch, NY + 4 : NY + 8] = zero
    pad[0, 4 : NY + 4] = map_re * b_re + map_im * b_im
    pad[1, 4 : NY + 4] = map_re * b_im - map_im * b_re
    edges = []
    for ch in range(6):
        if ch < 2:
            rows = (2 * bits_ref[ch] - 1).astype(F32)
        elif ch < 4:
            rows = adj_ref[ch - 2]
        else:
            rows = split(iterate_ref[ch - 4])[1].astype(F32)
        edges += [rows[0:4], rows[NYL - 4 : NYL]]
    edges = jnp.concatenate(edges, 0).astype(BF16)
    for dest in range(8):
        for ch in range(2):
            out_ref[dest, HALO_ROWS * ch : HALO_ROWS * ch + HALO_ROWS] = pad[
                ch, NYL * dest : NYL * dest + HALO_ROWS
            ].astype(BF16)
        out_ref[dest, 80:128] = edges


def relax_kernel(
    got_ref, field_ref, iterate_ref, bits_ref, adj_ref, out_ref, relaxed_ref, pad, qpad
):
    coil = lax.axis_index("coil")
    lower, upper = jnp.maximum(coil - 1, 0), jnp.minimum(coil + 1, 7)
    below = jnp.where(coil > 0, got_ref[lower, 80:128].astype(F32), 0.0)
    above = jnp.where(coil < 7, got_ref[upper, 80:128].astype(F32), 0.0)
    for ch in range(2):
        under = jnp.where(coil > 0, field_ref[lower, ch].astype(F32), 0.0)
        over = jnp.where(coil < 7, field_ref[upper, ch].astype(F32), 0.0)
        at = 32 + 8 * ch
        pad[ch, 0:4] = under[NYL - 4 : NYL] + below[at + 4 : at + 8]
        pad[ch, 4 : 4 + NYL] = iterate_ref[ch]
        pad[ch, 4 + NYL : HALO_ROWS] = over[0:4] + above[at : at + 4]
        rows = slice(HALO_ROWS * ch, HALO_ROWS * ch + HALO_ROWS)
        total = got_ref[0, rows].astype(F32)
        for source in range(1, 8):
            total = total + got_ref[source, rows].astype(F32)
        relaxed = pad[ch] - STEP * total
        relaxed_ref[ch] = relaxed[4 : 4 + NYL]
        rows = relaxed.astype(BF16)
        for dest in range(16):
            first = HALF * (dest % 2)
            out_ref[dest, ch] = rows[first : first + PART_ROWS]
    for ch in range(4):
        if ch < 2:
            rows = (2 * bits_ref[ch] - 1).astype(F32)
        else:
            rows = adj_ref[ch - 2]
        qpad[ch, 0:3] = below[ch * 8 + 5 : ch * 8 + 8]
        qpad[ch, 3 : 3 + NYL] = rows
        qpad[ch, 3 + NYL : 7 + NYL] = above[ch * 8 : ch * 8 + 4]
        qpad[ch, 7 + NYL : HALO_ROWS] = jnp.zeros((1, NZ), F32)
        rows = qpad[ch].astype(BF16)
        for dest in range(16):
            first = HALF * (dest % 2)
            out_ref[dest, 2 + ch] = rows[first : first + PART_ROWS]


def dot_first(left, right):
    return lax.dot_general(left, right, (((0,), (0,)), ((), ())), preferred_element_type=F32)


def tables_kernel(k1_ref, k2_ref, k3_ref, t1_ref, t2_ref, t3_ref, t1t_ref, t2t_ref, t3t_ref):
    lane = lax.broadcasted_iota(jnp.int32, (24, 256), 1)
    row = lax.broadcasted_iota(jnp.int32, (24, 256), 0)
    tile24 = ((lane % 24 == row) & (lane < 240)).astype(BF16)
    window = jnp.where(lane < 240, lane // 24, 99)

    def tap(dx, dy, dz, flip):
        if flip:
            dx, dy, dz = 2 - dx, 2 - dy, 2 - dz
        return dx * 9 + dy * 3 + dz

    for target, flip in ((t2_ref, False), (t2t_ref, True)):
        for dz in range(3):
            for dx in range(3):
                spread = []
                for dy in range(3):
                    block = k2_ref[tap(dx, dy, dz, flip)]
                    spread.append(dot_first(block, tile24) if flip else mm(block, tile24))
                for yo in range(8):
                    value = jnp.zeros((24, 256), F32)
                    for dy in range(3):
                        value = jnp.where(window == yo + dy, spread[dy], value)
                    at = dz * 192 + yo * 24
                    target[at : at + 24, dx * 256 : dx * 256 + 256] = value.astype(BF16)

    lane96 = lax.broadcasted_iota(jnp.int32, (24, 96), 1)
    lane2 = lax.broadcasted_iota(jnp.int32, (2, 96), 1)
    row2 = lax.broadcasted_iota(jnp.int32, (2, 96), 0)
    tile2 = ((lane2 // 16) % 2 == row2).astype(BF16)
    code = (lane96 // 32) * 16 + lane96 % 16
    for target, source, flip in ((t1_ref, k1_ref, False), (t3t_ref, k3_ref, True)):
        for dz in range(3):
            spread = {}
            for dx in range(3):
                for dy in range(3):
                    spread[dx, dy] = dot_first(source[tap(dx, dy, dz, flip)], tile2)
            for yo in range(8):
                value = jnp.zeros((24, 96), F32)
                for dx in range(3):
                    for dy in range(3):
                        value = jnp.where(code == dx * 16 + yo + dy, spread[dx, dy], value)
                at = dz * 192 + yo * 24
                target[at : at + 24, :] = value.astype(BF16)

    window8 = window[0:8] - lax.broadcasted_iota(jnp.int32, (8, 256), 0)
    for target, source, flip in ((t3_ref, k3_ref, False), (t1t_ref, k1_ref, True)):
        for dz in range(3):
            for dx in range(3):
                spread = [mm(source[tap(dx, dy, dz, flip)], tile24) for dy in range(3)]
                both = []
                for ch in range(2):
                    value = jnp.zeros((8, 256), F32)
                    for dy in range(3):
                        value = jnp.where(window8 == dy, spread[dy][ch : ch + 1], value)
                    both.append(value)
                target[dz * 16 : dz * 16 + 16, dx * 256 : dx * 256 + 256] = jnp.concatenate(
                    both, 0
                ).astype(BF16)


def tables(kernel_first, kernel_second, kernel_last):
    k1 = jnp.transpose(kernel_first, (2, 3, 4, 1, 0)).reshape(27, 2, 24)
    k2 = jnp.transpose(kernel_second, (2, 3, 4, 0, 1)).reshape(27, 24, 24)
    k3 = jnp.transpose(kernel_last, (2, 3, 4, 0, 1)).reshape(27, 2, 24)
    shapes = [(576, 96), (576, 768), (48, 768), (48, 768), (576, 768), (576, 96)]
    return pl.pallas_call(
        tables_kernel,
        compiler_params=GRANT,
        out_shape=[jax.ShapeDtypeStruct(s, BF16) for s in shapes],
        in_specs=whole(3),
        out_specs=whole(6),
        cost_estimate=pl.CostEstimate(flops=10**9, bytes_accessed=4 * 10**6, transcendentals=0),
    )(k1, k2, k3)


def join_z(parts, rows, half, at_low, at_high):
    lanes = slice(half * NZ, half * NZ + NZ)
    before = jnp.where(at_low, 0.0, pltpu.roll(parts[0:rows, lanes], 1, 1))
    after = jnp.where(at_high, 0.0, pltpu.roll(parts[2 * rows : 3 * rows, lanes], NZ - 1, 1))
    return parts[rows : 2 * rows, lanes] + (before + after)


def denoise_kernel(
    planes_ref,
    t1_ref,
    t2_ref,
    t3_ref,
    t1t_ref,
    t2t_ref,
    t3t_ref,
    send_ref,
    pair_ref,
    image,
    cots,
    a1,
    s1,
    a2,
    e2,
    e1,
):
    coil, slab = lax.axis_index("coil"), lax.axis_index("slab")
    base, side = 2 * (slab // 2), slab % 2

    def inside(plane):
        return (plane >= 0) & (plane < 16)

    for j in range(10):
        plane = base - 4 + j
        keep = inside(plane)
        source = jnp.clip(plane, 0, 15)
        for ch in range(2):
            image[j, ch, 0:PART_ROWS] = jnp.where(keep, planes_ref[source, ch].astype(F32), 0.0)
            image[j, ch, PART_ROWS:32] = jnp.zeros((8, NZ), F32)
        if 1 <= j < 9:
            for ch in range(4):
                cots[j - 1, ch, 0:PART_ROWS] = jnp.where(
                    keep, planes_ref[source, 2 + ch].astype(F32), 0.0
                )
                cots[j - 1, ch, PART_ROWS:32] = jnp.zeros((8, NZ), F32)

    def at_edges(rows):
        column = lax.broadcasted_iota(jnp.int32, (rows, NZ), 1)
        return column == 0, column == NZ - 1

    for j in range(8):
        a1[j, 576:640] = jnp.zeros((64, NZ), BF16)
        s1[j, 576:640] = jnp.zeros((64, NZ), F32)
    for j in range(6):
        e2[j, 480:640] = jnp.zeros((160, 2 * NZ), BF16)

    def rows_of(table_ref, rows):
        if rows == 192:
            return table_ref[...]
        return jnp.concatenate([table_ref[192 * dz : 192 * dz + rows] for dz in range(3)], 0)

    def first_step(step, carry):
        pair, block = 2 * (step // 3), step % 3
        at = pl.multiple_of(8 * block, 8)
        to = pl.multiple_of(192 * block, 192)
        pieces = []
        for dx in range(3):
            for ch in range(2):
                pieces.append(
                    jnp.concatenate(
                        [
                            image[pair + dx, ch, pl.ds(at, 16)],
                            image[pair + dx + 1, ch, pl.ds(at, 16)],
                        ],
                        1,
                    ).astype(BF16)
                )
        parts = mm(t1_ref[...], jnp.concatenate(pieces, 0))
        low, high = at_edges(192)
        for half in range(2):
            pre = join_z(parts, 192, half, low, high)
            gate = jax.nn.sigmoid(pre)
            a1[pair + half, pl.ds(to, 192)] = (pre * gate).astype(BF16)
            s1[pair + half, pl.ds(to, 192)] = gate * (1.0 + pre * (1.0 - gate))
        return carry

    lax.fori_loop(0, 12, first_step, 0, unroll=6)

    def clear(ref, planes, offset, top, bottom):
        rows, width = ref.shape[1], ref.shape[2]
        for j in range(planes):

            @pl.when(jnp.logical_not(inside(base + offset + j)))
            def _():
                ref[j] = jnp.zeros((rows, width), BF16)

        @pl.when((coil == 0) & (side == 0))
        def _():
            for j in range(planes):
                ref[j, 0:top] = jnp.zeros((top, width), BF16)

        @pl.when((coil == 7) & (side == 1))
        def _():
            for j in range(planes):
                ref[j, bottom:rows] = jnp.zeros((rows - bottom, width), BF16)

    clear(a1, 8, -3, 72, 456)

    def second_block(pair, at, to, rows):
        stacked = jnp.concatenate(
            [
                jnp.concatenate(
                    [a1[pair + dx, pl.ds(to, 256)], a1[pair + dx + 1, pl.ds(to, 256)]], 1
                )
                for dx in range(3)
            ],
            0,
        )
        parts = mm(rows_of(t2_ref, rows), stacked)
        low, high = at_edges(rows)
        for half in range(2):
            pre = join_z(parts, rows, half, low, high)
            gate = jax.nn.sigmoid(pre)
            a2[pair + half, pl.ds(to, rows)] = (pre * gate).astype(BF16)
            slope = gate * (1.0 + pre * (1.0 - gate))
            pieces = []
            for dx in range(3):
                for ch in range(2):
                    pieces.append(
                        jnp.concatenate(
                            [
                                cots[pair + half + dx, ch, pl.ds(at, 16)],
                                cots[pair + half + dx, 2 + ch, pl.ds(at, 16)],
                            ],
                            1,
                        ).astype(BF16)
                    )
            back = mm(rows_of(t3t_ref, rows), jnp.concatenate(pieces, 0))
            for which in range(2):
                grad = join_z(back, rows, which, low, high) * slope
                e2[pair + half, pl.ds(to, rows), which * NZ : which * NZ + NZ] = grad.astype(BF16)

    def second_step(step, carry):
        pair = 2 * step
        second_block(pair, 0, 0, 192)
        second_block(pair, 8, 192, 192)
        second_block(pair, 16, 384, 96)
        return carry

    lax.fori_loop(0, 3, second_step, 0)
    clear(a2, 6, -2, 48, 432)
    clear(e2, 6, -2, 48, 432)

    def third_block(plane, to, rows):
        stacked = jnp.concatenate([e2[plane + dx, pl.ds(to, 256)] for dx in range(3)], 0)
        back = mm(rows_of(t2t_ref, rows), stacked)
        low, high = at_edges(rows)
        slope = s1[plane + 2, pl.ds(to + 48, rows)]
        for which in range(2):
            grad = join_z(back, rows, which, low, high) * slope
            e1[plane, pl.ds(to, rows), which * NZ : which * NZ + NZ] = grad.astype(BF16)

    def third_step(step, carry):
        for plane in (2 * step, 2 * step + 1):
            third_block(plane, 0, 192)
            third_block(plane, 192, 192)
            third_block(plane, 384, 48)
        return carry

    lax.fori_loop(0, 2, third_step, 0)
    for j in range(4):
        e1[j, 432:448] = jnp.zeros((16, 2 * NZ), BF16)
    clear(e1, 4, -1, 24, 408)

    low, high = at_edges(16)
    for block in range(2):
        rows = slice(8 * block, 8 * block + 8)
        window = slice(24 + 192 * block, 280 + 192 * block)
        stacked = jnp.concatenate(
            [jnp.concatenate([a2[1 + dx, window], a2[2 + dx, window]], 1) for dx in range(3)], 0
        )
        parts = mm(t3_ref[...], stacked)
        for p in range(2):
            update = join_z(parts, 16, p, low, high)
            for ch in range(2):
                pair_ref[p, 4 + ch, rows] = update[8 * ch : 8 * ch + 8]

    for p in range(2):
        for block in range(2):
            rows = slice(8 * block, 8 * block + 8)
            shifted = slice(3 + 8 * block, 11 + 8 * block)
            window = slice(192 * block, 192 * block + 256)
            stacked = jnp.concatenate([e1[p + dx, window] for dx in range(3)], 0)
            back = mm(t1t_ref[...], stacked)
            for which in range(2):
                grad = join_z(back, 16, which, low, high)
                for ch in range(2):
                    pair_ref[p, 2 * which + ch, rows] = grad[8 * ch : 8 * ch + 8]
        for ch in range(4):
            pulled = cots[3 + p, ch, 3 : 3 + HALF] + pair_ref[p, ch]
            pulled = pulled.astype(BF16)
            for dest in range(8):
                send_ref[2 * dest + p, ch] = pulled


def normal_kernel(field_ref, maps_ref, mask_ref, yh, yl, zh, zl, out_ref):
    tabs = (yh, yl, zh, zl)
    weight = mask_ref[...].astype(F32)
    map_re, map_im = maps_ref[0], maps_ref[1]
    for which in range(2):
        re = field_ref[:, 2 * which].reshape(NY, NZ).astype(F32)
        im = field_ref[:, 2 * which + 1].reshape(NY, NZ).astype(F32)
        f_re, f_im = forward(map_re * re - map_im * im, map_re * im + map_im * re, tabs)
        b_re, b_im = inverse(weight * f_re, weight * f_im, tabs)
        out_re = (map_re * b_re + map_im * b_im).astype(BF16)
        out_im = (map_re * b_im - map_im * b_re).astype(BF16)
        for dest in range(8):
            rows = slice(NYL * dest, NYL * dest + NYL)
            out_ref[dest, 2 * which] = out_re[rows]
            out_ref[dest, 2 * which + 1] = out_im[rows]


def final_kernel(
    got_ref, pair_ref, relaxed_ref, bits_ref, adj_ref, loss_ref, new_ref, probe_ref, next_ref
):
    for ch in range(2):
        for side in range(2):
            rows = slice(HALF * side, HALF * side + HALF)
            new_ref[ch, rows] = relaxed_ref[ch, rows] + pair_ref[side, 4 + ch]
    for ch in range(4):
        total = got_ref[0, ch].astype(F32)
        for source in range(1, 8):
            total = total + got_ref[source, ch].astype(F32)
        total = STEP * total
        for side in range(2):
            rows = slice(HALF * side, HALF * side + HALF)
            if ch < 2:
                base = (2 * bits_ref[ch, rows] - 1).astype(F32)
                probe_ref[ch, rows] = base + pair_ref[side, ch] - total[rows]
            else:
                base = adj_ref[ch - 2, rows]
                result = base + pair_ref[side, ch] - total[rows]
                next_ref[ch - 2, rows] = loss_ref[ch - 2, rows] + result


def on_device(
    coil_maps,
    kspace,
    sample_mask,
    iterate,
    probe_bits,
    loss_gradient,
    adjoint,
    kernel_first,
    kernel_second,
    kernel_last,
):
    maps = coil_maps[0, :, 0]
    data = kspace[0, :, 0]
    iterate, bits, loss, adj = (a[:, 0] for a in (iterate, probe_bits, loss_gradient, adjoint))
    fourier = [jnp.asarray(t) for t in fourier_constants()]
    slabs = lax.axis_size("slab")
    coils = lax.axis_size("coil")
    twins = [[2 * j, 2 * j + 1] for j in range(slabs // 2)]
    families = [
        [c * slabs + 2 * j + h for c in range(coils) for h in range(2)] for j in range(slabs // 2)
    ]

    toeplitz = tables(kernel_first, kernel_second, kernel_last)
    field = lax.all_to_all(
        jnp.broadcast_to(iterate.astype(BF16)[None], (coils,) + iterate.shape), "coil", 0, 0
    )
    partial_sums = pl.pallas_call(
        gradient_kernel,
        compiler_params=GRANT,
        out_shape=jax.ShapeDtypeStruct((8, 128, NZ), BF16),
        in_specs=whole(11),
        out_specs=whole(1)[0],
        scratch_shapes=[pltpu.VMEM((2, NY + 8, NZ), F32)],
    )(field, maps, data, sample_mask, iterate, bits, adj, *fourier)
    got = lax.all_to_all(partial_sums, "coil", 0, 0)
    payload, relaxed = pl.pallas_call(
        relax_kernel,
        compiler_params=GRANT,
        out_shape=[
            jax.ShapeDtypeStruct((16, 6, PART_ROWS, NZ), BF16),
            jax.ShapeDtypeStruct((2, NYL, NZ), F32),
        ],
        in_specs=whole(5),
        out_specs=whole(2),
        scratch_shapes=[
            pltpu.VMEM((2, HALO_ROWS, NZ), F32),
            pltpu.VMEM((4, HALO_ROWS, NZ), F32),
        ],
    )(got, field, iterate, bits, adj)
    planes = lax.all_to_all(payload, "slab", 0, 0)
    send, pair = pl.pallas_call(
        denoise_kernel,
        compiler_params=GRANT,
        out_shape=[
            jax.ShapeDtypeStruct((16, 4, HALF, NZ), BF16),
            jax.ShapeDtypeStruct((2, 6, HALF, NZ), F32),
        ],
        in_specs=whole(7),
        out_specs=whole(2),
        scratch_shapes=[
            pltpu.VMEM((10, 2, 32, NZ), F32),
            pltpu.VMEM((8, 4, 32, NZ), F32),
            pltpu.VMEM((8, 640, NZ), BF16),
            pltpu.VMEM((8, 640, NZ), F32),
            pltpu.VMEM((6, 480, NZ), BF16),
            pltpu.VMEM((6, 640, 2 * NZ), BF16),
            pltpu.VMEM((4, 448, 2 * NZ), BF16),
        ],
    )(planes, *toeplitz)
    spread = lax.all_to_all(send, ("coil", "slab"), 0, 0, axis_index_groups=families)
    pair = lax.all_to_all(pair, "slab", 0, 0, axis_index_groups=twins)
    back = pl.pallas_call(
        normal_kernel,
        compiler_params=GRANT,
        out_shape=jax.ShapeDtypeStruct((8, 4, NYL, NZ), BF16),
        in_specs=whole(7),
        out_specs=whole(1)[0],
    )(spread, maps, sample_mask, *fourier)
    back = lax.all_to_all(back, "coil", 0, 0)
    new_iterate, probe, following = pl.pallas_call(
        final_kernel,
        compiler_params=GRANT,
        out_shape=[jax.ShapeDtypeStruct((2, NYL, NZ), F32)] * 3,
        in_specs=whole(6),
        out_specs=whole(3),
    )(back, pair, relaxed, bits, adj, loss)
    return new_iterate[:, None], probe[:, None], following[:, None]


def solution(mesh):
    image = P(None, "slab", "coil", None)
    coils = P("coil", None, "slab", None, None)
    return jax.shard_map(
        on_device,
        mesh=mesh,
        in_specs=(coils, coils, P(), image, image, image, image, P(), P(), P()),
        out_specs=(image, image, image),
        check_vma=False,
    )
```

time: 105 us -> 91.2 us (0.87)
  Pallas kernels: 34.2 us -> 17.4 us
  waiting for transfers between devices: 20.4 us -> 11 us
  blocking collectives: 35 us -> 42.2 us
  local copies, waits for them, and re-layouts: 2.42 us -> 6.4 us
    pallas_call x6, Pallas kernels: 34.2 us -> 17.4 us  [the longest x1 10 us: on_device(): pl.pallas_call(denoise_kernel, compiler_params=GRANT, out_shape=[jax.Shap...]
    all_to_all x2 -> x3, blocking collectives: 24 us -> 32.2 us  [the longest x1 12.1 us: on_device(): lax.all_to_all(jnp.broadcast_to(iterate.astype(BF16)[None], (coils,) + it...]
    all_to_all x1, waiting for transfers between devices: 6.14 us -> 0.01 us  [on_device(): pair = lax.all_to_all(pair, 'slab', 0, 0, axis_index_groups=twins)]
    unnamed x4 -> x38, local copies, waits for them, and re-layouts: 1.65 us -> 6.38 us
    all_to_all x1, waiting for transfers between devices: 14.3 us -> 11 us  [on_device(): planes = lax.all_to_all(payload, 'slab', 0, 0)]
  transfers between devices with their start and end apart: 2 -> 2, of which waited for: 2 -> 1; matrix products, arithmetic and copies ran while one was open for 1% -> 0% of each run, Pallas kernels for 3% -> 5%
where the time goes in v3:
time: 91.2 us; the launch traced here: 89.8 us
  blocking collectives  42.2 us (46%)
  Pallas kernels  17.4 us (19%)
  starting transfers between devices  11.2 us (12%)
  waiting for transfers between devices  11 us (12%)
  local copies, waits for them, and re-layouts  6.4 us (7%)
    all_to_all x1, blocking collectives, on_device(): lax.all_to_all(jnp.broadcast_to(iterate.astype(BF16)[None], (coils,) + it...  12.1 us
    all_to_all x1, waiting for transfers between devices, on_device(): planes = lax.all_to_all(payload, 'slab', 0, 0)  11 us
    all_to_all x1, blocking collectives, on_device(): lax.all_to_all(send, ('coil', 'slab'), 0, 0, axis_index_groups=families)  10.4 us
    all_to_all x1, blocking collectives, on_device(): back = lax.all_to_all(back, 'coil', 0, 0)  10.1 us
    pallas_call x1, Pallas kernels, on_device(): pl.pallas_call(denoise_kernel, compiler_params=GRANT, out_shape=[jax.Shap...  10 us
    all_to_all x1, blocking collectives, on_device(): got = lax.all_to_all(partial_sums, 'coil', 0, 0)  9.64 us
    all_to_all x1, starting transfers between devices, on_device(): planes = lax.all_to_all(payload, 'slab', 0, 0)  7.73 us
    unnamed x38, local copies, waits for them, and re-layouts  6.38 us
  transfers between devices with their start and end apart: 2, of which 1 were waited for; matrix products, arithmetic and copies ran while one was open for 0% of the time, Pallas kernels for 5%

profile of v3, /device:TPU:0, one launch (start us, length us, event | category | flops | bytes accessed | tf_op | source)
XLA Modules:
  0.0 89.8 jit_solution(3612167187735091732)
XLA Ops:
  0.6 0.0 copy-start
  0.6 0.8 bitcast_convert_fusion
  1.5 0.0 copy-start.5
  1.5 0.0 copy-start.10
  1.5 0.0 copy-start.11
  1.5 12.1 %all_to_all.30.field_ref = bf16[8,2,32,128]{3,2,1,0:T(8,128)(2,1)S(1)} all-to-all(bf16[8,2,32,128]{3,2,1,0:T(8,128)(2,1)S(1)} %broadcast_in_dim.15), channel_id=1, replica_groups=mesh['coil'=8,'slab'=16] {'coil'}, dimensions={0} | all-to-all | bytes 262144 | tf_op jit(solution)/shard_map/all_to_all | solution.py:515
  13.6 0.0 copy-done
  13.6 0.0 copy-done.5
  13.6 0.0 copy-done.10
  13.6 0.0 copy-done.11
  13.6 0.0 copy-start.1
  13.6 0.9 %copy-done.1 = bf16[512,256]{1,0:T(8,128)(2,1)S(1)} copy-done((bf16[512,256]{1,0:T(8,128)(2,1)S(1)}, bf16[512,256]{1,0:T(8,128)(2,1)}, u32[]{:S(2)}) %copy-start.1) | copy-done | bytes 262168
  14.6 0.0 copy-start.3
  14.6 0.9 %copy-done.3 = bf16[512,256]{1,0:T(8,128)(2,1)S(1)} copy-done((bf16[512,256]{1,0:T(8,128)(2,1)S(1)}, bf16[512,256]{1,0:T(8,128)(2,1)}, u32[]{:S(2)}) %copy-start.3) | copy-done | bytes 262168
  15.5 0.0 copy-start.6
  15.5 0.9 %copy-done.6 = bf16[256,256]{1,0:T(8,128)(2,1)S(1)} copy-done((bf16[256,256]{1,0:T(8,128)(2,1)S(1)}, bf16[256,256]{1,0:T(8,128)(2,1)}, u32[]{:S(2)}) %copy-start.6) | copy-done | bytes 131096
  16.4 0.0 copy-start.8
  16.4 0.9 %copy-done.8 = bf16[256,256]{1,0:T(8,128)(2,1)S(1)} copy-done((bf16[256,256]{1,0:T(8,128)(2,1)S(1)}, bf16[256,256]{1,0:T(8,128)(2,1)}, u32[]{:S(2)}) %copy-start.8) | copy-done | bytes 131096
  17.3 0.0 copy-start.12
  17.3 0.8 copy-done.12
  18.1 0.0 copy-start.14
  18.1 0.9 %copy-done.14 = f32[1,2,1,256,128]{4,3,2,1,0:T(8,128)S(1)} copy-done((f32[1,2,1,256,128]{4,3,2,1,0:T(8,128)S(1)}, f32[1,2,1,256,128]{4,3,2,1,0:T(8,128)}, u32[]{:S(2)}) %copy-start.14) | copy-done | bytes 262168
  19.0 1.7 %shard_map.157 = bf16[8,128,128]{2,1,0:T(8,128)(2,1)S(1)} custom-call(bf16[8,2,32,128]{3,2,1,0:T(8,128)(2,1)S(1)} %all_to_all.30.field_ref, f32[2,256,128]{2,1,0:T(8,128)S(1)} %bitcast.25, f32[2,256,128]{2,1,0:T(8,128)S(1)} %bitcast.35, s32[256,128]{1,0:T(8,128)S(1)} %copy-done.5, f32[2,32,128]{2,1,0:T(8,128)S(1)} %bitcast.27, s32[2,32,128]{2,1,0:T(8,128)S(1)} %bitcast.29, ...), custom_call_target="tpu_custom_call" | custom-call | tf_op jit(solution)/shard_map/pallas_call | solution.py:518
  20.7 0.0 copy-start.13
  20.7 9.6 %all_to_all.31.got_ref = bf16[8,128,128]{2,1,0:T(8,128)(2,1)S(1)} all-to-all(bf16[8,128,128]{2,1,0:T(8,128)(2,1)S(1)} %shard_map.157), channel_id=1, replica_groups=mesh['coil'=8,'slab'=16] {'coil'}, dimensions={0} | all-to-all | bytes 524288 | tf_op jit(solution)/shard_map/all_to_all | solution.py:526
  30.4 0.0 copy-done.13
  30.4 0.9 %shard_map.158 = (bf16[16,6,24,128]{3,2,1,0:T(8,128)(2,1)}, f32[2,32,128]{2,1,0:T(8,128)S(1)}) custom-call(bf16[8,128,128]{2,1,0:T(8,128)(2,1)S(1)} %all_to_all.31.got_ref, bf16[8,2,32,128]{3,2,1,0:T(8,128)(2,1)S(1)} %all_to_all.30.field_ref, f32[2,32,128]{2,1,0:T(8,128)S(1)} %bitcast.28, s32[2,32,128]{2,1,0:T(8,128)S(1)} %bitcast.30, f32[2,32,128]{2,1,0:T(8,128)S(1)} %bitcast.33), custom_call_target="tpu_custom_call" | custom-call | tf_op jit(solution)/shard_map/pallas_call | solution.py:527
  31.3 0.0 copy-start.17
  31.3 0.0 copy-start.18
  31.3 7.7 %all-to-all-start.2 = ((bf16[16,6,24,128]{3,2,1,0:T(8,128)(2,1)}), bf16[16,6,24,128]{3,2,1,0:T(8,128)(2,1)S(1)}, u32[]{:S(2)}, u32[]{:S(2)}) async-start(bf16[16,6,24,128]{3,2,1,0:T(8,128)(2,1)} %get-tuple-element.16), calls=%async_computation.2 | async-start | bytes 1179648 | tf_op jit(solution)/shard_map/all_to_all | solution.py:541
  39.1 0.0 copy-done.17
  39.1 0.0 copy-done.18
  39.1 0.0 copy-start.16
  39.1 0.9 %copy-done.16 = bf16[24,24,3,3,3]{1,0,4,3,2:T(8,128)(2,1)S(1)} copy-done((bf16[24,24,3,3,3]{1,0,4,3,2:T(8,128)(2,1)S(1)}, bf16[24,24,3,3,3]{1,0,4,3,2:T(8,128)(2,1)}, u32[]{:S(2)}) %copy-start.16) | copy-done | bytes 31128
  40.0 1.1 %shard_map.159 = (bf16[576,96]{1,0:T(8,128)(2,1)S(1)}, bf16[576,768]{1,0:T(8,128)(2,1)S(1)}, bf16[48,768]{1,0:T(8,128)(2,1)S(1)}, bf16[48,768]{1,0:T(8,128)(2,1)...) custom-call(bf16[27,2,24]{2,1,0:T(2,128)(2,1)S(1)} %bitcast.38, bf16[27,24,24]{2,1,0:T(8,128)(2,1)S(1)} %bitcast.37, ...), custom_call_target="tpu_custom_call" | custom-call | flops 1000000000 | bytes 4000000 | tf_op jit(solution)/shard_map/pallas_call | solution.py:237
  41.1 11.0 %all-to-all-done.2.planes_ref = bf16[16,6,24,128]{3,2,1,0:T(8,128)(2,1)S(1)} async-done(((bf16[16,6,24,128]{3,2,1,0:T(8,128)(2,1)}), bf16[16,6,24,128]{3,2,1,0:T(8,128)(2,1)S(1)}, u32[]{:S(2)}, u32[]{:S(2)}) %all-to-all-start.2) | async-done | bytes 589856 | tf_op jit(solution)/shard_map/all_to_all | solution.py:541
  52.1 0.0 copy-start.9
  52.1 10.0 %shard_map.160 = (bf16[16,4,16,128]{3,2,1,0:T(8,128)(2,1)S(1)}, f32[2,6,16,128]{3,2,1,0:T(8,128)}) custom-call(bf16[16,6,24,128]{3,2,1,0:T(8,128)(2,1)S(1)} %all-to-all-done.2.planes_ref, bf16[576,96]{1,0:T(8,128)(2,1)S(1)} %get-tuple-element.17.t1_ref, bf16[576,768]{1,0:T(8,128)(2,1)S(1)} %get-tuple-element.18.t2_ref, ...), custom_call_target="tpu_custom_call" | custom-call | tf_op jit(solution)/shard_map/pallas_call | solution.py:542
  62.1 0.0 copy-start.2
  62.1 0.0 copy-start.4
  62.1 10.4 %all_to_all.32.field_ref = bf16[16,4,16,128]{3,2,1,0:T(8,128)(2,1)S(1)} all-to-all(bf16[16,4,16,128]{3,2,1,0:T(8,128)(2,1)S(1)} %get-tuple-element.23), channel_id=1, replica_groups={{0,1,16,17,32,33,48,49,64,65,80,81,96,97,112,113},{2,3,18,19,34,35,50,5..., dimensions={0} | all-to-all | bytes 524288 | tf_op jit(solution)/shard_map/all_to_all | solution.py:561
  72.6 0.0 copy-start.7
  72.6 3.5 %all-to-all-start.5 = ((f32[2,6,16,128]{3,2,1,0:T(8,128)}), f32[2,6,16,128]{3,2,1,0:T(8,128)S(1)}, u32[]{:S(2)}, u32[]{:S(2)}) async-start(f32[2,6,16,128]{3,2,1,0:T(8,128)} %get-tuple-element.24), calls=%async_computation.5 | async-start | bytes 196608 | tf_op jit(solution)/shard_map/all_to_all | solution.py:562
  76.1 0.0 copy-done.9
  76.1 0.0 copy-done.2
  76.1 0.0 copy-done.4
  76.1 0.0 copy-done.7
  76.1 2.9 %shard_map.161 = bf16[8,4,32,128]{3,2,1,0:T(8,128)(2,1)S(1)} custom-call(bf16[16,4,16,128]{3,2,1,0:T(8,128)(2,1)S(1)} %all_to_all.32.field_ref, f32[2,256,128]{2,1,0:T(8,128)S(1)} %bitcast.26, s32[256,128]{1,0:T(8,128)S(1)} %copy-done.5, bf16[512,256]{1,0:T(8,128)(2,1)S(1)} %copy-done.4, bf16[512,256]{1,0:T(8,128)(2,1)S(1)} %copy-done.2, ...), custom_call_target="tpu_custom_call" | custom-call | tf_op jit(solution)/shard_map/pallas_call | solution.py:563
  79.0 0.0 copy-start.15
  79.0 0.0 all-to-all-done.5.pair_ref
  79.1 10.1 %all_to_all.33.got_ref = bf16[8,4,32,128]{3,2,1,0:T(8,128)(2,1)S(1)} all-to-all(bf16[8,4,32,128]{3,2,1,0:T(8,128)(2,1)S(1)} %shard_map.161), channel_id=1, replica_groups=mesh['coil'=8,'slab'=16] {'coil'}, dimensions={0} | all-to-all | bytes 524288 | tf_op jit(solution)/shard_map/all_to_all | solution.py:570
  89.1 0.0 copy-done.15
  89.1 0.7 shard_map.162
  (1 shorter events, 0.0 us)
Async XLA Ops:
  0.6 13.0 %copy-start = (f32[1,2,1,256,128]{4,3,2,1,0:T(8,128)S(1)}, f32[1,2,1,256,128]{4,3,2,1,0:T(8,128)}, u32[]{:S(2)}) copy-start(f32[1,2,1,256,128]{4,3,2,1,0:T(8,128)} %param.14) | copy-start | bytes 786436
  1.5 12.1 %copy-start.5 = (s32[256,128]{1,0:T(8,128)S(1)}, s32[256,128]{1,0:T(8,128)}, u32[]{:S(2)}) copy-start(s32[256,128]{1,0:T(8,128)} %mask_ref.3) | copy-start | bytes 393220
  1.5 12.1 %copy-start.10 = (f32[2,1,32,128]{3,2,1,0:T(8,128)S(1)}, f32[2,1,32,128]{3,2,1,0:T(8,128)}, u32[]{:S(2)}) copy-start(f32[2,1,32,128]{3,2,1,0:T(8,128)} %param.17) | copy-start | bytes 98308
  1.5 12.1 %copy-start.11 = (s32[2,1,32,128]{3,2,1,0:T(8,128)S(1)}, s32[2,1,32,128]{3,2,1,0:T(8,128)}, u32[]{:S(2)}) copy-start(s32[2,1,32,128]{3,2,1,0:T(8,128)} %param.18) | copy-start | bytes 98308
  13.6 1.0 %copy-start.1 = (bf16[512,256]{1,0:T(8,128)(2,1)S(1)}, bf16[512,256]{1,0:T(8,128)(2,1)}, u32[]{:S(2)}) copy-start(bf16[512,256]{1,0:T(8,128)(2,1)} %constant.9.clone.yl) | copy-start | bytes 786436
  14.6 0.9 %copy-start.3 = (bf16[512,256]{1,0:T(8,128)(2,1)S(1)}, bf16[512,256]{1,0:T(8,128)(2,1)}, u32[]{:S(2)}) copy-start(bf16[512,256]{1,0:T(8,128)(2,1)} %constant.8.clone.yh) | copy-start | bytes 786436
  15.5 0.9 %copy-start.6 = (bf16[256,256]{1,0:T(8,128)(2,1)S(1)}, bf16[256,256]{1,0:T(8,128)(2,1)}, u32[]{:S(2)}) copy-start(bf16[256,256]{1,0:T(8,128)(2,1)} %constant.11.clone.zl) | copy-start | bytes 393220
  16.4 0.9 %copy-start.8 = (bf16[256,256]{1,0:T(8,128)(2,1)S(1)}, bf16[256,256]{1,0:T(8,128)(2,1)}, u32[]{:S(2)}) copy-start(bf16[256,256]{1,0:T(8,128)(2,1)} %constant.10.clone.zh) | copy-start | bytes 393220
  17.3 0.8 copy-start.12
  18.1 0.9 %copy-start.14 = (f32[1,2,1,256,128]{4,3,2,1,0:T(8,128)S(1)}, f32[1,2,1,256,128]{4,3,2,1,0:T(8,128)}, u32[]{:S(2)}) copy-start(f32[1,2,1,256,128]{4,3,2,1,0:T(8,128)} %param.15) | copy-start | bytes 786436
  20.7 9.7 %copy-start.13 = (f32[2,1,32,128]{3,2,1,0:T(8,128)S(1)}, f32[2,1,32,128]{3,2,1,0:T(8,128)}, u32[]{:S(2)}) copy-start(f32[2,1,32,128]{3,2,1,0:T(8,128)} %param.20) | copy-start | bytes 98308
  31.3 7.7 %copy-start.17 = (bf16[24,2,3,3,3]{0,1,4,3,2:T(2,128)(2,1)S(1)}, bf16[24,2,3,3,3]{0,1,4,3,2:T(2,128)(2,1)}, u32[]{:S(2)}) copy-start(bf16[24,2,3,3,3]{0,1,4,3,2:T(2,128)(2,1)} %param.21) | copy-start | bytes 7780
  31.3 7.7 %copy-start.18 = (bf16[2,24,3,3,3]{1,0,4,3,2:T(2,128)(2,1)S(1)}, bf16[2,24,3,3,3]{1,0,4,3,2:T(2,128)(2,1)}, u32[]{:S(2)}) copy-start(bf16[2,24,3,3,3]{1,0,4,3,2:T(2,128)(2,1)} %param.23) | copy-start | bytes 7780
  31.3 20.8 %all-to-all-start.2 = ((bf16[16,6,24,128]{3,2,1,0:T(8,128)(2,1)}), bf16[16,6,24,128]{3,2,1,0:T(8,128)(2,1)S(1)}, u32[]{:S(2)}, u32[]{:S(2)}) async-start(bf16[16,6,24,128]{3,2,1,0:T(8,128)(2,1)} %get-tuple-element.16), calls=%async_computation.2 | async-start | bytes 1179648 | tf_op jit(solution)/shard_map/all_to_all | solution.py:541
  39.1 0.9 %copy-start.16 = (bf16[24,24,3,3,3]{1,0,4,3,2:T(8,128)(2,1)S(1)}, bf16[24,24,3,3,3]{1,0,4,3,2:T(8,128)(2,1)}, u32[]{:S(2)}) copy-start(bf16[24,24,3,3,3]{1,0,4,3,2:T(8,128)(2,1)} %param.22) | copy-start | bytes 93316
  52.1 23.9 %copy-start.9 = (bf16[256,256]{1,0:T(8,128)(2,1)S(1)}, bf16[256,256]{1,0:T(8,128)(2,1)}, u32[]{:S(2)}) copy-start(bf16[256,256]{1,0:T(8,128)(2,1)} %constant.10.clone.zh) | copy-start | bytes 393220
  62.1 13.9 %copy-start.2 = (bf16[512,256]{1,0:T(8,128)(2,1)S(1)}, bf16[512,256]{1,0:T(8,128)(2,1)}, u32[]{:S(2)}) copy-start(bf16[512,256]{1,0:T(8,128)(2,1)} %constant.9.clone.yl) | copy-start | bytes 786436
  62.1 13.9 %copy-start.4 = (bf16[512,256]{1,0:T(8,128)(2,1)S(1)}, bf16[512,256]{1,0:T(8,128)(2,1)}, u32[]{:S(2)}) copy-start(bf16[512,256]{1,0:T(8,128)(2,1)} %constant.8.clone.yh) | copy-start | bytes 786436
  72.6 3.5 %copy-start.7 = (bf16[256,256]{1,0:T(8,128)(2,1)S(1)}, bf16[256,256]{1,0:T(8,128)(2,1)}, u32[]{:S(2)}) copy-start(bf16[256,256]{1,0:T(8,128)(2,1)} %constant.11.clone.zl) | copy-start | bytes 393220
  72.6 6.5 %all-to-all-start.5 = ((f32[2,6,16,128]{3,2,1,0:T(8,128)}), f32[2,6,16,128]{3,2,1,0:T(8,128)S(1)}, u32[]{:S(2)}, u32[]{:S(2)}) async-start(f32[2,6,16,128]{3,2,1,0:T(8,128)} %get-tuple-element.24), calls=%async_computation.5 | async-start | bytes 196608 | tf_op jit(solution)/shard_map/all_to_all | solution.py:562
  79.0 10.1 %copy-start.15 = (f32[2,1,32,128]{3,2,1,0:T(8,128)S(1)}, f32[2,1,32,128]{3,2,1,0:T(8,128)}, u32[]{:S(2)}) copy-start(f32[2,1,32,128]{3,2,1,0:T(8,128)} %param.19) | copy-start | bytes 98308

commit v4 on v3

--- a/solution.py
+++ b/solution.py
@@ -40,7 +40,7 @@
     cos_z, sin_z = cos_sin(NZ)
     along_y = np.concatenate([cos_y, sin_y], axis=0)
     along_z = np.block([[cos_z, -sin_z], [sin_z, cos_z]])
-    return split_host(along_y) + split_host(along_z)
+    return jnp.asarray(np.concatenate(split_host(along_y) + split_host(along_z), axis=0))
 
 
 def split(values):
@@ -52,72 +52,114 @@
     return jnp.dot(left, right, preferred_element_type=F32)
 
 
-def along_z(joined, high_ref, low_ref):
+def along_z(joined, tab_ref):
     high, low = split(joined)
-    return mm(high, high_ref[...]) + (mm(high, low_ref[...]) + mm(low, high_ref[...]))
-
-
-def along_y(joined, high_ref, low_ref):
+    z_high, z_low = tab_ref[1024:1280], tab_ref[1280:1536]
+    return mm(high, z_high) + (mm(high, z_low) + mm(low, z_high))
+
+
+def along_y(joined, tab_ref):
     high, low = split(joined)
-    return mm(high_ref[...], high) + (mm(low_ref[...], high) + mm(high_ref[...], low))
-
-
-def forward(real, imag, tabs):
-    y_high, y_low, z_high, z_low = tabs
-    turned = along_y(along_z(jnp.concatenate([real, imag], 1), z_high, z_low), y_high, y_low)
+    y_high, y_low = tab_ref[0:512], tab_ref[512:1024]
+    return mm(y_high, high) + (mm(y_low, high) + mm(y_high, low))
+
+
+def forward(real, imag, tab_ref):
+    turned = along_y(along_z(jnp.concatenate([real, imag], 1), tab_ref), tab_ref)
     cos_part, sin_part = turned[:NY], turned[NY:]
     return cos_part[:, :NZ] + sin_part[:, NZ:], cos_part[:, NZ:] - sin_part[:, :NZ]
 
 
-def inverse(real, imag, tabs):
-    y_high, y_low, z_high, z_low = tabs
-    turned = along_y(jnp.concatenate([real, imag], 1), y_high, y_low)
+def inverse(real, imag, tab_ref):
+    turned = along_y(jnp.concatenate([real, imag], 1), tab_ref)
     cos_part, sin_part = turned[:NY], turned[NY:]
     back = cos_part[:, :NZ] - sin_part[:, NZ:], -(cos_part[:, NZ:] + sin_part[:, :NZ])
-    turned = along_z(jnp.concatenate(back, 1), z_high, z_low)
+    turned = along_z(jnp.concatenate(back, 1), tab_ref)
     return turned[:, :NZ], -turned[:, NZ:]
 
 
+def stage_kernel(
+    maps_in,
+    kspace_in,
+    mask_in,
+    iterate_in,
+    bits_in,
+    adj_in,
+    tab_in,
+    k1_in,
+    k2_in,
+    k3_in,
+    maps_ref,
+    masked_ref,
+    weight_ref,
+    own_ref,
+    edges_ref,
+    tab_ref,
+    first_ref,
+    all_ref,
+    mask_ref,
+    bits_ref,
+    k1_ref,
+    k2_ref,
+    k3_ref,
+    sems,
+):
+    moves = (
+        (k1_in, k1_ref),
+        (k2_in, k2_ref),
+        (k3_in, k3_ref),
+        (iterate_in, own_ref.at[0:2]),
+        (bits_in, bits_ref),
+        (adj_in, own_ref.at[4:6]),
+        (mask_in, mask_ref),
+        (kspace_in, masked_ref),
+        (maps_in, maps_ref),
+        (tab_in, tab_ref),
+    )
+    copies = [pltpu.make_async_copy(s, d, sems.at[i]) for i, (s, d) in enumerate(moves)]
+    for copy in copies:
+        copy.start()
+    for copy in copies[0:3]:
+        copy.wait()
+    build_tables(k1_ref, k2_ref, k3_ref, all_ref)
+    for copy in copies[3:]:
+        copy.wait()
+    for ch in range(2):
+        rows = own_ref[ch].astype(BF16)
+        for dest in range(8):
+            first_ref[dest, ch] = rows
+    weight = mask_ref[...].astype(F32)
+    weight_ref[...] = weight
+    for ch in range(2):
+        masked_ref[ch] = weight * masked_ref[ch]
+        own_ref[2 + ch] = (2 * bits_ref[ch] - 1).astype(F32)
+    edges = []
+    for ch in (2, 3, 4, 5, 0, 1):
+        rows = own_ref[ch]
+        if ch < 2:
+            rows = split(rows)[1].astype(F32)
+        edges += [rows[0:4], rows[NYL - 4 : NYL]]
+    edges_ref[...] = jnp.concatenate(edges, 0).astype(BF16)
+
+
 def gradient_kernel(
-    field_ref,
-    maps_ref,
-    kspace_ref,
-    mask_ref,
-    iterate_ref,
-    bits_ref,
-    adj_ref,
-    yh,
-    yl,
-    zh,
-    zl,
-    out_ref,
-    pad,
+    field_ref, maps_ref, masked_ref, weight_ref, edges_ref, tab_ref, out_ref, pad
 ):
-    tabs = (yh, yl, zh, zl)
-    weight = mask_ref[...].astype(F32)
+    weight = weight_ref[...]
     map_re, map_im = maps_ref[0], maps_ref[1]
     re = field_ref[:, 0].astype(F32).reshape(NY, NZ)
     im = field_ref[:, 1].astype(F32).reshape(NY, NZ)
-    f_re, f_im = forward(map_re * re - map_im * im, map_re * im + map_im * re, tabs)
-    f_re = weight * (f_re - kspace_ref[0])
-    f_im = weight * (f_im - kspace_ref[1])
-    b_re, b_im = inverse(f_re, f_im, tabs)
+    f_re, f_im = forward(map_re * re - map_im * im, map_re * im + map_im * re, tab_ref)
+    f_re = weight * f_re - masked_ref[0]
+    f_im = weight * f_im - masked_ref[1]
+    b_re, b_im = inverse(f_re, f_im, tab_ref)
     zero = jnp.zeros((4, NZ), F32)
     for ch in range(2):
         pad[ch, 0:4] = zero
         pad[ch, NY + 4 : NY + 8] = zero
     pad[0, 4 : NY + 4] = map_re * b_re + map_im * b_im
     pad[1, 4 : NY + 4] = map_re * b_im - map_im * b_re
-    edges = []
-    for ch in range(6):
-        if ch < 2:
-            rows = (2 * bits_ref[ch] - 1).astype(F32)
-        elif ch < 4:
-            rows = adj_ref[ch - 2]
-        else:
-            rows = split(iterate_ref[ch - 4])[1].astype(F32)
-        edges += [rows[0:4], rows[NYL - 4 : NYL]]
-    edges = jnp.concatenate(edges, 0).astype(BF16)
+    edges = edges_ref[...]
     for dest in range(8):
         for ch in range(2):
             out_ref[dest, HALO_ROWS * ch : HALO_ROWS * ch + HALO_ROWS] = pad[
@@ -126,9 +168,7 @@
         out_ref[dest, 80:128] = edges
 
 
-def relax_kernel(
-    got_ref, field_ref, iterate_ref, bits_ref, adj_ref, out_ref, relaxed_ref, pad, qpad
-):
+def relax_kernel(got_ref, field_ref, own_ref, out_ref, relaxed_ref, pad, qpad):
     coil = lax.axis_index("coil")
     lower, upper = jnp.maximum(coil - 1, 0), jnp.minimum(coil + 1, 7)
     below = jnp.where(coil > 0, got_ref[lower, 80:128].astype(F32), 0.0)
@@ -138,7 +178,7 @@
         over = jnp.where(coil < 7, field_ref[upper, ch].astype(F32), 0.0)
         at = 32 + 8 * ch
         pad[ch, 0:4] = under[NYL - 4 : NYL] + below[at + 4 : at + 8]
-        pad[ch, 4 : 4 + NYL] = iterate_ref[ch]
+        pad[ch, 4 : 4 + NYL] = own_ref[ch]
         pad[ch, 4 + NYL : HALO_ROWS] = over[0:4] + above[at : at + 4]
         rows = slice(HALO_ROWS * ch, HALO_ROWS * ch + HALO_ROWS)
         total = got_ref[0, rows].astype(F32)
@@ -151,12 +191,8 @@
             first = HALF * (dest % 2)
             out_ref[dest, ch] = rows[first : first + PART_ROWS]
     for ch in range(4):
-        if ch < 2:
-            rows = (2 * bits_ref[ch] - 1).astype(F32)
-        else:
-            rows = adj_ref[ch - 2]
         qpad[ch, 0:3] = below[ch * 8 + 5 : ch * 8 + 8]
-        qpad[ch, 3 : 3 + NYL] = rows
+        qpad[ch, 3 : 3 + NYL] = own_ref[2 + ch]
         qpad[ch, 3 + NYL : 7 + NYL] = above[ch * 8 : ch * 8 + 4]
         qpad[ch, 7 + NYL : HALO_ROWS] = jnp.zeros((1, NZ), F32)
         rows = qpad[ch].astype(BF16)
@@ -169,7 +205,10 @@
     return lax.dot_general(left, right, (((0,), (0,)), ((), ())), preferred_element_type=F32)
 
 
-def tables_kernel(k1_ref, k2_ref, k3_ref, t1_ref, t2_ref, t3_ref, t1t_ref, t2t_ref, t3t_ref):
+def build_tables(k1_ref, k2_ref, k3_ref, all_ref):
+    t2_ref, t2t_ref = all_ref.at[0:576, 0:768], all_ref.at[576:1152, 0:768]
+    t1_ref, t3t_ref = all_ref.at[0:576, 768:896], all_ref.at[576:1152, 768:896]
+    t3_ref, t1t_ref = all_ref.at[1152:1200, 0:768], all_ref.at[1200:1248, 0:768]
     lane = lax.broadcasted_iota(jnp.int32, (24, 256), 1)
     row = lax.broadcasted_iota(jnp.int32, (24, 256), 0)
     tile24 = ((lane % 24 == row) & (lane < 240)).astype(BF16)
@@ -194,9 +233,9 @@
                     at = dz * 192 + yo * 24
                     target[at : at + 24, dx * 256 : dx * 256 + 256] = value.astype(BF16)
 
-    lane96 = lax.broadcasted_iota(jnp.int32, (24, 96), 1)
-    lane2 = lax.broadcasted_iota(jnp.int32, (2, 96), 1)
-    row2 = lax.broadcasted_iota(jnp.int32, (2, 96), 0)
+    lane96 = lax.broadcasted_iota(jnp.int32, (24, 128), 1)
+    lane2 = lax.broadcasted_iota(jnp.int32, (2, 128), 1)
+    row2 = lax.broadcasted_iota(jnp.int32, (2, 128), 0)
     tile2 = ((lane2 // 16) % 2 == row2).astype(BF16)
     code = (lane96 // 32) * 16 + lane96 % 16
     for target, source, flip in ((t1_ref, k1_ref, False), (t3t_ref, k3_ref, True)):
@@ -206,7 +245,7 @@
                 for dy in range(3):
                     spread[dx, dy] = dot_first(source[tap(dx, dy, dz, flip)], tile2)
             for yo in range(8):
-                value = jnp.zeros((24, 96), F32)
+                value = jnp.zeros((24, 128), F32)
                 for dx in range(3):
                     for dy in range(3):
                         value = jnp.where(code == dx * 16 + yo + dy, spread[dx, dy], value)
@@ -229,21 +268,6 @@
                 ).astype(BF16)
 
 
-def tables(kernel_first, kernel_second, kernel_last):
-    k1 = jnp.transpose(kernel_first, (2, 3, 4, 1, 0)).reshape(27, 2, 24)
-    k2 = jnp.transpose(kernel_second, (2, 3, 4, 0, 1)).reshape(27, 24, 24)
-    k3 = jnp.transpose(kernel_last, (2, 3, 4, 0, 1)).reshape(27, 2, 24)
-    shapes = [(576, 96), (576, 768), (48, 768), (48, 768), (576, 768), (576, 96)]
-    return pl.pallas_call(
-        tables_kernel,
-        compiler_params=GRANT,
-        out_shape=[jax.ShapeDtypeStruct(s, BF16) for s in shapes],
-        in_specs=whole(3),
-        out_specs=whole(6),
-        cost_estimate=pl.CostEstimate(flops=10**9, bytes_accessed=4 * 10**6, transcendentals=0),
-    )(k1, k2, k3)
-
-
 def join_z(parts, rows, half, at_low, at_high):
     lanes = slice(half * NZ, half * NZ + NZ)
     before = jnp.where(at_low, 0.0, pltpu.roll(parts[0:rows, lanes], 1, 1))
@@ -253,13 +277,10 @@
 
 def denoise_kernel(
     planes_ref,
-    t1_ref,
-    t2_ref,
-    t3_ref,
-    t1t_ref,
-    t2t_ref,
-    t3t_ref,
+    all_ref,
     send_ref,
+    mine_ref,
+    theirs_ref,
     pair_ref,
     image,
     cots,
@@ -269,6 +290,9 @@
     e2,
     e1,
 ):
+    t2_ref, t2t_ref = all_ref.at[0:576, 0:768], all_ref.at[576:1152, 0:768]
+    t1_ref, t3t_ref = all_ref.at[0:576, 768:896], all_ref.at[576:1152, 768:896]
+    t3_ref, t1t_ref = all_ref.at[1152:1200, 0:768], all_ref.at[1200:1248, 0:768]
     coil, slab = lax.axis_index("coil"), lax.axis_index("slab")
     base, side = 2 * (slab // 2), slab % 2
 
@@ -299,10 +323,12 @@
     for j in range(6):
         e2[j, 480:640] = jnp.zeros((160, 2 * NZ), BF16)
 
-    def rows_of(table_ref, rows):
+    def rows_of(table_ref, rows, depth=768):
         if rows == 192:
-            return table_ref[...]
-        return jnp.concatenate([table_ref[192 * dz : 192 * dz + rows] for dz in range(3)], 0)
+            return table_ref[:, 0:depth]
+        return jnp.concatenate(
+            [table_ref[192 * dz : 192 * dz + rows, 0:depth] for dz in range(3)], 0
+        )
 
     def first_step(step, carry):
         pair, block = 2 * (step // 3), step % 3
@@ -320,7 +346,7 @@
                         1,
                     ).astype(BF16)
                 )
-        parts = mm(t1_ref[...], jnp.concatenate(pieces, 0))
+        parts = mm(t1_ref[:, 0:96], jnp.concatenate(pieces, 0))
         low, high = at_edges(192)
         for half in range(2):
             pre = join_z(parts, 192, half, low, high)
@@ -380,7 +406,7 @@
                             1,
                         ).astype(BF16)
                     )
-            back = mm(rows_of(t3t_ref, rows), jnp.concatenate(pieces, 0))
+            back = mm(rows_of(t3t_ref, rows, 96), jnp.concatenate(pieces, 0))
             for which in range(2):
                 grad = join_z(back, rows, which, low, high) * slope
                 e2[pair + half, pl.ds(to, rows), which * NZ : which * NZ + NZ] = grad.astype(BF16)
@@ -446,17 +472,18 @@
             pulled = pulled.astype(BF16)
             for dest in range(8):
                 send_ref[2 * dest + p, ch] = pulled
-
-
-def normal_kernel(field_ref, maps_ref, mask_ref, yh, yl, zh, zl, out_ref):
-    tabs = (yh, yl, zh, zl)
-    weight = mask_ref[...].astype(F32)
+    mine_ref[...] = pair_ref[side]
+    theirs_ref[...] = pair_ref[1 - side]
+
+
+def normal_kernel(field_ref, maps_ref, weight_ref, tab_ref, out_ref):
+    weight = weight_ref[...]
     map_re, map_im = maps_ref[0], maps_ref[1]
     for which in range(2):
         re = field_ref[:, 2 * which].reshape(NY, NZ).astype(F32)
         im = field_ref[:, 2 * which + 1].reshape(NY, NZ).astype(F32)
-        f_re, f_im = forward(map_re * re - map_im * im, map_re * im + map_im * re, tabs)
-        b_re, b_im = inverse(weight * f_re, weight * f_im, tabs)
+        f_re, f_im = forward(map_re * re - map_im * im, map_re * im + map_im * re, tab_ref)
+        b_re, b_im = inverse(weight * f_re, weight * f_im, tab_ref)
         out_re = (map_re * b_re + map_im * b_im).astype(BF16)
         out_im = (map_re * b_im - map_im * b_re).astype(BF16)
         for dest in range(8):
@@ -466,26 +493,33 @@
 
 
 def final_kernel(
-    got_ref, pair_ref, relaxed_ref, bits_ref, adj_ref, loss_ref, new_ref, probe_ref, next_ref
+    got_ref, mine_ref, theirs_ref, relaxed_ref, own_ref, loss_ref, new_ref, probe_ref, next_ref
 ):
-    for ch in range(2):
-        for side in range(2):
-            rows = slice(HALF * side, HALF * side + HALF)
-            new_ref[ch, rows] = relaxed_ref[ch, rows] + pair_ref[side, 4 + ch]
+    side = lax.axis_index("slab") % 2
+    sums = []
     for ch in range(4):
         total = got_ref[0, ch].astype(F32)
         for source in range(1, 8):
             total = total + got_ref[source, ch].astype(F32)
-        total = STEP * total
-        for side in range(2):
-            rows = slice(HALF * side, HALF * side + HALF)
-            if ch < 2:
-                base = (2 * bits_ref[ch, rows] - 1).astype(F32)
-                probe_ref[ch, rows] = base + pair_ref[side, ch] - total[rows]
-            else:
-                base = adj_ref[ch - 2, rows]
-                result = base + pair_ref[side, ch] - total[rows]
-                next_ref[ch - 2, rows] = loss_ref[ch - 2, rows] + result
+        sums.append(STEP * total)
+
+    def put(first, part_ref):
+        rows = slice(first, first + HALF)
+        for ch in range(2):
+            new_ref[ch, rows] = relaxed_ref[ch, rows] + part_ref[4 + ch]
+            probe_ref[ch, rows] = own_ref[2 + ch, rows] + part_ref[ch] - sums[ch][rows]
+            pulled = own_ref[4 + ch, rows] + part_ref[2 + ch]
+            next_ref[ch, rows] = loss_ref[ch, rows] + (pulled - sums[2 + ch][rows])
+
+    @pl.when(side == 0)
+    def _():
+        put(0, mine_ref)
+        put(HALF, theirs_ref)
+
+    @pl.when(side == 1)
+    def _():
+        put(0, theirs_ref)
+        put(HALF, mine_ref)
 
 
 def on_device(
@@ -503,26 +537,56 @@
     maps = coil_maps[0, :, 0]
     data = kspace[0, :, 0]
     iterate, bits, loss, adj = (a[:, 0] for a in (iterate, probe_bits, loss_gradient, adjoint))
-    fourier = [jnp.asarray(t) for t in fourier_constants()]
     slabs = lax.axis_size("slab")
     coils = lax.axis_size("coil")
-    twins = [[2 * j, 2 * j + 1] for j in range(slabs // 2)]
     families = [
         [c * slabs + 2 * j + h for c in range(coils) for h in range(2)] for j in range(slabs // 2)
     ]
 
-    toeplitz = tables(kernel_first, kernel_second, kernel_last)
-    field = lax.all_to_all(
-        jnp.broadcast_to(iterate.astype(BF16)[None], (coils,) + iterate.shape), "coil", 0, 0
+    k1 = jnp.transpose(kernel_first, (2, 3, 4, 1, 0)).reshape(27, 2, 24)
+    k2 = jnp.transpose(kernel_second, (2, 3, 4, 0, 1)).reshape(27, 24, 24)
+    k3 = jnp.transpose(kernel_last, (2, 3, 4, 0, 1)).reshape(27, 2, 24)
+    staged = pl.pallas_call(
+        stage_kernel,
+        compiler_params=GRANT,
+        out_shape=[
+            jax.ShapeDtypeStruct((2, NY, NZ), F32),
+            jax.ShapeDtypeStruct((2, NY, NZ), F32),
+            jax.ShapeDtypeStruct((NY, NZ), F32),
+            jax.ShapeDtypeStruct((6, NYL, NZ), F32),
+            jax.ShapeDtypeStruct((48, NZ), BF16),
+            jax.ShapeDtypeStruct((1536, 256), BF16),
+            jax.ShapeDtypeStruct((8, 2, NYL, NZ), BF16),
+            jax.ShapeDtypeStruct((1248, 896), BF16),
+        ],
+        in_specs=[pl.BlockSpec(memory_space=pltpu.HBM)] * 10,
+        out_specs=whole(8),
+        scratch_shapes=[
+            pltpu.VMEM((NY, NZ), jnp.int32),
+            pltpu.VMEM((2, NYL, NZ), jnp.int32),
+            pltpu.VMEM((27, 2, 24), BF16),
+            pltpu.VMEM((27, 24, 24), BF16),
+            pltpu.VMEM((27, 2, 24), BF16),
+            pltpu.SemaphoreType.DMA((10,)),
+        ],
+    )(
+        *(
+            pltpu.with_memory_space_constraint(x, pltpu.HBM)
+            for x in (
+                maps, data, sample_mask, iterate, bits, adj, fourier_constants(), k1, k2, k3
+            )
+        )
     )
+    maps, masked, weight, own, edges, fourier, first, toeplitz = staged
+    field = lax.all_to_all(first, "coil", 0, 0)
     partial_sums = pl.pallas_call(
         gradient_kernel,
         compiler_params=GRANT,
         out_shape=jax.ShapeDtypeStruct((8, 128, NZ), BF16),
-        in_specs=whole(11),
+        in_specs=whole(6),
         out_specs=whole(1)[0],
         scratch_shapes=[pltpu.VMEM((2, NY + 8, NZ), F32)],
-    )(field, maps, data, sample_mask, iterate, bits, adj, *fourier)
+    )(field, maps, masked, weight, edges, fourier)
     got = lax.all_to_all(partial_sums, "coil", 0, 0)
     payload, relaxed = pl.pallas_call(
         relax_kernel,
@@ -531,24 +595,26 @@
             jax.ShapeDtypeStruct((16, 6, PART_ROWS, NZ), BF16),
             jax.ShapeDtypeStruct((2, NYL, NZ), F32),
         ],
-        in_specs=whole(5),
+        in_specs=whole(3),
         out_specs=whole(2),
         scratch_shapes=[
             pltpu.VMEM((2, HALO_ROWS, NZ), F32),
             pltpu.VMEM((4, HALO_ROWS, NZ), F32),
         ],
-    )(got, field, iterate, bits, adj)
+    )(got, field, own)
     planes = lax.all_to_all(payload, "slab", 0, 0)
-    send, pair = pl.pallas_call(
+    send, mine, theirs = pl.pallas_call(
         denoise_kernel,
         compiler_params=GRANT,
         out_shape=[
             jax.ShapeDtypeStruct((16, 4, HALF, NZ), BF16),
-            jax.ShapeDtypeStruct((2, 6, HALF, NZ), F32),
+            jax.ShapeDtypeStruct((6, HALF, NZ), F32),
+            jax.ShapeDtypeStruct((6, HALF, NZ), F32),
         ],
-        in_specs=whole(7),
-        out_specs=whole(2),
+        in_specs=whole(2),
+        out_specs=whole(3),
         scratch_shapes=[
+            pltpu.VMEM((2, 6, HALF, NZ), F32),
             pltpu.VMEM((10, 2, 32, NZ), F32),
             pltpu.VMEM((8, 4, 32, NZ), F32),
             pltpu.VMEM((8, 640, NZ), BF16),
@@ -557,16 +623,16 @@
             pltpu.VMEM((6, 640, 2 * NZ), BF16),
             pltpu.VMEM((4, 448, 2 * NZ), BF16),
         ],
-    )(planes, *toeplitz)
+    )(planes, toeplitz)
     spread = lax.all_to_all(send, ("coil", "slab"), 0, 0, axis_index_groups=families)
-    pair = lax.all_to_all(pair, "slab", 0, 0, axis_index_groups=twins)
+    theirs = lax.ppermute(theirs, "slab", [(i, i + 1 - 2 * (i % 2)) for i in range(slabs)])
     back = pl.pallas_call(
         normal_kernel,
         compiler_params=GRANT,
         out_shape=jax.ShapeDtypeStruct((8, 4, NYL, NZ), BF16),
-        in_specs=whole(7),
+        in_specs=whole(4),
         out_specs=whole(1)[0],
-    )(spread, maps, sample_mask, *fourier)
+    )(spread, maps, weight, fourier)
     back = lax.all_to_all(back, "coil", 0, 0)
     new_iterate, probe, following = pl.pallas_call(
         final_kernel,
@@ -574,7 +640,7 @@
         out_shape=[jax.ShapeDtypeStruct((2, NYL, NZ), F32)] * 3,
         in_specs=whole(6),
         out_specs=whole(3),
-    )(back, pair, relaxed, bits, adj, loss)
+    )(back, mine, theirs, relaxed, own, loss)
     return new_iterate[:, None], probe[:, None], following[:, None]
 
 

time: 91.2 us -> 82.2 us (0.901); the launches traced: 89.8 us -> 81.8 us
  blocking collectives: 42.2 us -> 52.4 us
  starting transfers between devices: 11.2 us -> 3.6 us
  local copies, waits for them, and re-layouts: 6.4 us -> 0.01 us
  waiting for transfers between devices: 11 us -> 7.22 us
    all_to_all x2, blocking collectives: 22.2 us -> 32.4 us  [the longest x1 20.5 us: on_device(): planes = lax.all_to_all(payload, 'slab', 0, 0)]
    all_to_all x2 -> x1, starting transfers between devices: 11.2 us -> 3.41 us  [on_device(): back = lax.all_to_all(back, 'coil', 0, 0)]
    unnamed x38 -> x2, local copies, waits for them, and re-layouts: 6.38 us -> 0.01 us
    all_to_all x2 -> x1, waiting for transfers between devices: 11 us -> 6.11 us  [on_device(): back = lax.all_to_all(back, 'coil', 0, 0)]
    ppermute x0 -> x1, waiting for transfers between devices: none -> 1.12 us  [on_device(): lax.ppermute(theirs, 'slab', [(i, i + 1 - 2 * (i % 2)) for i in range(sla...]
    pallas_call x1, Pallas kernels: 1.14 us -> 2.21 us  [on_device(): pl.pallas_call(stage_kernel, compiler_params=GRANT, out_shape=[jax.ShapeD...]
  transfers between devices with their start and end apart: 2 -> 2, of which waited for: 1 -> 2; matrix products, arithmetic and copies ran while one was open for 0% -> 0% of each run, Pallas kernels for 5% -> 0%
where the time goes in v4:
time: 82.2 us; the launch traced here: 81.8 us
  blocking collectives  52.4 us (64%)
  Pallas kernels  17.9 us (22%)
  waiting for transfers between devices  7.22 us (9%)
  starting transfers between devices  3.6 us (4%)
    all_to_all x1, blocking collectives, on_device(): planes = lax.all_to_all(payload, 'slab', 0, 0)  20.5 us
    all_to_all x1, blocking collectives, on_device(): field = lax.all_to_all(first, 'coil', 0, 0)  11.9 us
    all_to_all x1, blocking collectives, on_device(): lax.all_to_all(send, ('coil', 'slab'), 0, 0, axis_index_groups=families)  10.3 us
    all_to_all x1, blocking collectives, on_device(): got = lax.all_to_all(partial_sums, 'coil', 0, 0)  9.64 us
    pallas_call x1, Pallas kernels, on_device(): pl.pallas_call(denoise_kernel, compiler_params=GRANT, out_shape=[jax.Shap...  9.6 us
    all_to_all x1, waiting for transfers between devices, on_device(): back = lax.all_to_all(back, 'coil', 0, 0)  6.11 us
    pallas_call x1, Pallas kernels, on_device(): pl.pallas_call(normal_kernel, compiler_params=GRANT, out_shape=jax.ShapeD...  3.64 us
    all_to_all x1, starting transfers between devices, on_device(): back = lax.all_to_all(back, 'coil', 0, 0)  3.41 us
  transfers between devices with their start and end apart: 2, of which 2 were waited for; matrix products, arithmetic and copies ran while one was open for 0% of the time, Pallas kernels for 0%

profile of v4, /device:TPU:0, one launch (start us, length us, event | category | flops | bytes accessed | tf_op | source)
XLA Modules:
  0.0 81.8 jit_solution(4383944385097889488)
XLA Ops:
  0.6 2.2 %shard_map.130 = (f32[2,256,128]{2,1,0:T(8,128)S(1)}, f32[2,256,128]{2,1,0:T(8,128)S(1)}, f32[256,128]{1,0:T(8,128)S(1)}, f32[6,32,128]{2,1,0:T(8,128)S(1)}, bf1...) custom-call(f32[2,256,128]{2,1,0:T(8,128)} %bitcast.25, ...), custom_call_target="tpu_custom_call" | custom-call | tf_op jit(solution)/shard_map/pallas_call | solution.py:549
  2.8 11.9 %all_to_all.25.field_ref = bf16[8,2,32,128]{3,2,1,0:T(8,128)(2,1)S(1)} all-to-all(bf16[8,2,32,128]{3,2,1,0:T(8,128)(2,1)S(1)} %get-tuple-element.19), channel_id=1, replica_groups=mesh['coil'=8,'slab'=16] {'coil'}, dimensions={0} | all-to-all | bytes 262144 | tf_op jit(solution)/shard_map/all_to_all | solution.py:581
  14.8 1.7 %shard_map.131 = bf16[8,128,128]{2,1,0:T(8,128)(2,1)S(1)} custom-call(bf16[8,2,32,128]{3,2,1,0:T(8,128)(2,1)S(1)} %all_to_all.25.field_ref, f32[2,256,128]{2,1,0:T(8,128)S(1)} %get-tuple-element.20.maps_ref, f32[2,256,128]{2,1,0:T(8,128)S(1)} %get-tuple-element.21.masked_ref, f32[256,128]{1,0:T(8,128)S(1)} %get-tuple-element.22.weight_ref, ...), custom_call_target="tpu_custom_call" | custom-call | tf_op jit(solution)/shard_map/pallas_call | solution.py:582
  16.5 9.6 %all_to_all.26.got_ref = bf16[8,128,128]{2,1,0:T(8,128)(2,1)S(1)} all-to-all(bf16[8,128,128]{2,1,0:T(8,128)(2,1)S(1)} %shard_map.131), channel_id=1, replica_groups=mesh['coil'=8,'slab'=16] {'coil'}, dimensions={0} | all-to-all | bytes 524288 | tf_op jit(solution)/shard_map/all_to_all | solution.py:590
  26.1 0.1 shard_map.132
  26.2 20.5 %all_to_all.27.planes_ref = bf16[16,6,24,128]{3,2,1,0:T(8,128)(2,1)S(1)} all-to-all(bf16[16,6,24,128]{3,2,1,0:T(8,128)(2,1)S(1)} %get-tuple-element.26), channel_id=1, replica_groups=mesh['coil'=8,'slab'=16] {'slab'}, dimensions={0} | all-to-all | bytes 1179648 | tf_op jit(solution)/shard_map/all_to_all | solution.py:605
  46.7 0.0 copy-start
  46.7 9.6 %shard_map.133 = (bf16[16,4,16,128]{3,2,1,0:T(8,128)(2,1)S(1)}, f32[6,16,128]{2,1,0:T(8,128)S(1)}, f32[6,16,128]{2,1,0:T(8,128)S(1)}) custom-call(bf16[16,6,24,128]{3,2,1,0:T(8,128)(2,1)S(1)} %all_to_all.27.planes_ref, bf16[1248,896]{1,0:T(8,128)(2,1)S(1)} %get-tuple-element.27.all_ref), custom_call_target="tpu_custom_call" | custom-call | tf_op jit(solution)/shard_map/pallas_call | solution.py:606
  56.3 10.3 %all_to_all.28.field_ref = bf16[16,4,16,128]{3,2,1,0:T(8,128)(2,1)S(1)} all-to-all(bf16[16,4,16,128]{3,2,1,0:T(8,128)(2,1)S(1)} %get-tuple-element.28), channel_id=1, replica_groups={{0,1,16,17,32,33,48,49,64,65,80,81,96,97,112,113},{2,3,18,19,34,35,50,5..., dimensions={0} | all-to-all | bytes 524288 | tf_op jit(solution)/shard_map/all_to_all | solution.py:627
  66.6 3.6 %shard_map.134 = bf16[8,4,32,128]{3,2,1,0:T(8,128)(2,1)} custom-call(bf16[16,4,16,128]{3,2,1,0:T(8,128)(2,1)S(1)} %all_to_all.28.field_ref, f32[2,256,128]{2,1,0:T(8,128)S(1)} %get-tuple-element.20.maps_ref, f32[256,128]{1,0:T(8,128)S(1)} %get-tuple-element.22.weight_ref, bf16[1536,256]{1,0:T(8,128)(2,1)S(1)} %get-tuple-element.24.tab_ref), custom_call_target="tpu_custom_call" | custom-call | tf_op jit(solution)/shard_map/pallas_call | solution.py:629
  70.3 3.4 %all-to-all-start.4 = ((bf16[8,4,32,128]{3,2,1,0:T(8,128)(2,1)}), bf16[8,4,32,128]{3,2,1,0:T(8,128)(2,1)S(1)}, u32[]{:S(2)}, u32[]{:S(2)}) async-start(bf16[8,4,32,128]{3,2,1,0:T(8,128)(2,1)} %shard_map.134), calls=%async_computation.4 | async-start | bytes 524288 | tf_op jit(solution)/shard_map/all_to_all | solution.py:636
  73.7 0.2 collective-permute-start
  73.9 1.1 %collective-permute-done.theirs_ref = f32[6,16,128]{2,1,0:T(8,128)S(1)} collective-permute-done((f32[6,16,128]{2,1,0:T(8,128)S(1)}, f32[6,16,128]{2,1,0:T(8,128)S(1)}, u32[]{:S(2)}, u32[]{:S(2)}) %collective-permute-start) | collective-permute-done | bytes 49184 | tf_op jit(solution)/shard_map/ppermute | solution.py:628
  75.0 6.1 %all-to-all-done.4.got_ref = bf16[8,4,32,128]{3,2,1,0:T(8,128)(2,1)S(1)} async-done(((bf16[8,4,32,128]{3,2,1,0:T(8,128)(2,1)}), bf16[8,4,32,128]{3,2,1,0:T(8,128)(2,1)S(1)}, u32[]{:S(2)}, u32[]{:S(2)}) %all-to-all-start.4) | async-done | bytes 262176 | tf_op jit(solution)/shard_map/all_to_all | solution.py:636
  81.1 0.0 copy-done
  81.1 0.7 shard_map.135
Async XLA Ops:
  46.7 34.4 %copy-start = (f32[2,1,32,128]{3,2,1,0:T(8,128)S(1)}, f32[2,1,32,128]{3,2,1,0:T(8,128)}, u32[]{:S(2)}) copy-start(f32[2,1,32,128]{3,2,1,0:T(8,128)} %param.16) | copy-start | bytes 98308
  70.3 10.8 %all-to-all-start.4 = ((bf16[8,4,32,128]{3,2,1,0:T(8,128)(2,1)}), bf16[8,4,32,128]{3,2,1,0:T(8,128)(2,1)S(1)}, u32[]{:S(2)}, u32[]{:S(2)}) async-start(bf16[8,4,32,128]{3,2,1,0:T(8,128)(2,1)} %shard_map.134), calls=%async_computation.4 | async-start | bytes 524288 | tf_op jit(solution)/shard_map/all_to_all | solution.py:636
  73.7 1.3 %collective-permute-start = (f32[6,16,128]{2,1,0:T(8,128)S(1)}, f32[6,16,128]{2,1,0:T(8,128)S(1)}, u32[]{:S(2)}, u32[]{:S(2)}) collective-permute-start(f32[6,16,128]{2,1,0:T(8,128)S(1)} %get-tuple-element.30), channel_id=1, source_target_pairs={{0,1},{1,0},{2,3},{3,2},{4,5},{5,4},{6,7},{7,6},{8,9},{9,8},{10,11... | collective-permute-start | bytes 147464 | tf_op jit(solution)/shard_map/ppermute | solution.py:628

commit v5 on v4

--- a/solution.py
+++ b/solution.py
@@ -207,7 +207,7 @@
 
 def build_tables(k1_ref, k2_ref, k3_ref, all_ref):
     t2_ref, t2t_ref = all_ref.at[0:576, 0:768], all_ref.at[576:1152, 0:768]
-    t1_ref, t3t_ref = all_ref.at[0:576, 768:896], all_ref.at[576:1152, 768:896]
+    t1_ref, t3t_ref = all_ref.at[0:192, 768:1152], all_ref.at[192:384, 768:1152]
     t3_ref, t1t_ref = all_ref.at[1152:1200, 0:768], all_ref.at[1200:1248, 0:768]
     lane = lax.broadcasted_iota(jnp.int32, (24, 256), 1)
     row = lax.broadcasted_iota(jnp.int32, (24, 256), 0)
@@ -233,24 +233,25 @@
                     at = dz * 192 + yo * 24
                     target[at : at + 24, dx * 256 : dx * 256 + 256] = value.astype(BF16)
 
-    lane96 = lax.broadcasted_iota(jnp.int32, (24, 128), 1)
-    lane2 = lax.broadcasted_iota(jnp.int32, (2, 128), 1)
-    row2 = lax.broadcasted_iota(jnp.int32, (2, 128), 0)
+    lane = lax.broadcasted_iota(jnp.int32, (24, 384), 1)
+    lane2 = lax.broadcasted_iota(jnp.int32, (2, 384), 1)
+    row2 = lax.broadcasted_iota(jnp.int32, (2, 384), 0)
     tile2 = ((lane2 // 16) % 2 == row2).astype(BF16)
-    code = (lane96 // 32) * 16 + lane96 % 16
+    group, offset = lane // 32, lane % 16
     for target, source, flip in ((t1_ref, k1_ref, False), (t3t_ref, k3_ref, True)):
-        for dz in range(3):
-            spread = {}
+        spread = []
+        for dy in range(3):
+            value = jnp.zeros((24, 384), F32)
             for dx in range(3):
-                for dy in range(3):
-                    spread[dx, dy] = dot_first(source[tap(dx, dy, dz, flip)], tile2)
-            for yo in range(8):
-                value = jnp.zeros((24, 128), F32)
-                for dx in range(3):
-                    for dy in range(3):
-                        value = jnp.where(code == dx * 16 + yo + dy, spread[dx, dy], value)
-                at = dz * 192 + yo * 24
-                target[at : at + 24, :] = value.astype(BF16)
+                for dz in range(3):
+                    block = dot_first(source[tap(dx, dy, dz, flip)], tile2)
+                    value = jnp.where(group == dx * 3 + dz, block, value)
+            spread.append(value)
+        for yo in range(8):
+            value = jnp.zeros((24, 384), F32)
+            for dy in range(3):
+                value = jnp.where(offset == yo + dy, spread[dy], value)
+            target[yo * 24 : yo * 24 + 24, :] = value.astype(BF16)
 
     window8 = window[0:8] - lax.broadcasted_iota(jnp.int32, (8, 256), 0)
     for target, source, flip in ((t3_ref, k3_ref, False), (t1t_ref, k1_ref, True)):
@@ -291,31 +292,40 @@
     e1,
 ):
     t2_ref, t2t_ref = all_ref.at[0:576, 0:768], all_ref.at[576:1152, 0:768]
-    t1_ref, t3t_ref = all_ref.at[0:576, 768:896], all_ref.at[576:1152, 768:896]
+    t1_ref, t3t_ref = all_ref.at[0:192, 768:1152], all_ref.at[192:384, 768:1152]
     t3_ref, t1t_ref = all_ref.at[1152:1200, 0:768], all_ref.at[1200:1248, 0:768]
     coil, slab = lax.axis_index("coil"), lax.axis_index("slab")
     base, side = 2 * (slab // 2), slab % 2
 
     def inside(plane):
         return (plane >= 0) & (plane < 16)
+
+    def at_edges(rows):
+        column = lax.broadcasted_iota(jnp.int32, (rows, NZ), 1)
+        return column == 0, column == NZ - 1
+
+    low, high = at_edges(PART_ROWS)
+
+    def stage(ref, j, ch, rows):
+        ref[0, j, ch, 0:PART_ROWS] = jnp.where(low, 0.0, pltpu.roll(rows, 1, 1))
+        ref[1, j, ch, 0:PART_ROWS] = rows
+        ref[2, j, ch, 0:PART_ROWS] = jnp.where(high, 0.0, pltpu.roll(rows, NZ - 1, 1))
+        for dz in range(3):
+            ref[dz, j, ch, PART_ROWS:32] = jnp.zeros((8, NZ), F32)
 
     for j in range(10):
         plane = base - 4 + j
         keep = inside(plane)
         source = jnp.clip(plane, 0, 15)
         for ch in range(2):
-            image[j, ch, 0:PART_ROWS] = jnp.where(keep, planes_ref[source, ch].astype(F32), 0.0)
-            image[j, ch, PART_ROWS:32] = jnp.zeros((8, NZ), F32)
+            stage(image, j, ch, jnp.where(keep, planes_ref[source, ch].astype(F32), 0.0))
         if 1 <= j < 9:
             for ch in range(4):
-                cots[j - 1, ch, 0:PART_ROWS] = jnp.where(
-                    keep, planes_ref[source, 2 + ch].astype(F32), 0.0
-                )
-                cots[j - 1, ch, PART_ROWS:32] = jnp.zeros((8, NZ), F32)
-
-    def at_edges(rows):
-        column = lax.broadcasted_iota(jnp.int32, (rows, NZ), 1)
-        return column == 0, column == NZ - 1
+                rows = jnp.where(keep, planes_ref[source, 2 + ch].astype(F32), 0.0)
+                stage(cots, j - 1, ch, rows)
+
+    def usable(plane):
+        return jnp.where(inside(plane), 1.0, 0.0)
 
     for j in range(8):
         a1[j, 576:640] = jnp.zeros((64, NZ), BF16)
@@ -323,12 +333,10 @@
     for j in range(6):
         e2[j, 480:640] = jnp.zeros((160, 2 * NZ), BF16)
 
-    def rows_of(table_ref, rows, depth=768):
+    def rows_of(table_ref, rows):
         if rows == 192:
-            return table_ref[:, 0:depth]
-        return jnp.concatenate(
-            [table_ref[192 * dz : 192 * dz + rows, 0:depth] for dz in range(3)], 0
-        )
+            return table_ref[...]
+        return jnp.concatenate([table_ref[192 * dz : 192 * dz + rows] for dz in range(3)], 0)
 
     def first_step(step, carry):
         pair, block = 2 * (step // 3), step % 3
@@ -336,46 +344,38 @@
         to = pl.multiple_of(192 * block, 192)
         pieces = []
         for dx in range(3):
-            for ch in range(2):
-                pieces.append(
-                    jnp.concatenate(
-                        [
-                            image[pair + dx, ch, pl.ds(at, 16)],
-                            image[pair + dx + 1, ch, pl.ds(at, 16)],
-                        ],
-                        1,
-                    ).astype(BF16)
-                )
-        parts = mm(t1_ref[:, 0:96], jnp.concatenate(pieces, 0))
-        low, high = at_edges(192)
+            for dz in range(3):
+                for ch in range(2):
+                    pieces.append(
+                        jnp.concatenate(
+                            [
+                                image[dz, pair + dx, ch, pl.ds(at, 16)],
+                                image[dz, pair + dx + 1, ch, pl.ds(at, 16)],
+                            ],
+                            1,
+                        ).astype(BF16)
+                    )
+        both = mm(t1_ref[:, 0:288], jnp.concatenate(pieces, 0))
         for half in range(2):
-            pre = join_z(parts, 192, half, low, high)
+            pre = both[:, half * NZ : half * NZ + NZ]
             gate = jax.nn.sigmoid(pre)
-            a1[pair + half, pl.ds(to, 192)] = (pre * gate).astype(BF16)
-            s1[pair + half, pl.ds(to, 192)] = gate * (1.0 + pre * (1.0 - gate))
+            keep = usable(base - 3 + pair + half)
+            a1[pair + half, pl.ds(to, 192)] = (pre * gate * keep).astype(BF16)
+            s1[pair + half, pl.ds(to, 192)] = gate * (1.0 + pre * (1.0 - gate)) * keep
         return carry
 
-    lax.fori_loop(0, 12, first_step, 0, unroll=6)
-
-    def clear(ref, planes, offset, top, bottom):
-        rows, width = ref.shape[1], ref.shape[2]
+    lax.fori_loop(0, 12, first_step, 0, unroll=12)
+
+    def clear(ref, planes, top, bottom):
+        rows = ref.shape[1]
+        first, last = (coil == 0) & (side == 0), (coil == 7) & (side == 1)
         for j in range(planes):
-
-            @pl.when(jnp.logical_not(inside(base + offset + j)))
-            def _():
-                ref[j] = jnp.zeros((rows, width), BF16)
-
-        @pl.when((coil == 0) & (side == 0))
-        def _():
-            for j in range(planes):
-                ref[j, 0:top] = jnp.zeros((top, width), BF16)
-
-        @pl.when((coil == 7) & (side == 1))
-        def _():
-            for j in range(planes):
-                ref[j, bottom:rows] = jnp.zeros((rows - bottom, width), BF16)
-
-    clear(a1, 8, -3, 72, 456)
+            value = ref[j, 0:top]
+            ref[j, 0:top] = jnp.where(first, jnp.zeros_like(value), value)
+            value = ref[j, bottom:rows]
+            ref[j, bottom:rows] = jnp.where(last, jnp.zeros_like(value), value)
+
+    clear(a1, 8, 72, 456)
 
     def second_block(pair, at, to, rows):
         stacked = jnp.concatenate(
@@ -392,24 +392,26 @@
         for half in range(2):
             pre = join_z(parts, rows, half, low, high)
             gate = jax.nn.sigmoid(pre)
-            a2[pair + half, pl.ds(to, rows)] = (pre * gate).astype(BF16)
-            slope = gate * (1.0 + pre * (1.0 - gate))
+            keep = usable(base - 2 + pair + half)
+            a2[pair + half, pl.ds(to, rows)] = (pre * gate * keep).astype(BF16)
+            slope = gate * (1.0 + pre * (1.0 - gate)) * keep
             pieces = []
             for dx in range(3):
-                for ch in range(2):
-                    pieces.append(
-                        jnp.concatenate(
-                            [
-                                cots[pair + half + dx, ch, pl.ds(at, 16)],
-                                cots[pair + half + dx, 2 + ch, pl.ds(at, 16)],
-                            ],
-                            1,
-                        ).astype(BF16)
-                    )
-            back = mm(rows_of(t3t_ref, rows, 96), jnp.concatenate(pieces, 0))
+                for dz in range(3):
+                    for ch in range(2):
+                        pieces.append(
+                            jnp.concatenate(
+                                [
+                                    cots[dz, pair + half + dx, ch, pl.ds(at, 16)],
+                                    cots[dz, pair + half + dx, 2 + ch, pl.ds(at, 16)],
+                                ],
+                                1,
+                            ).astype(BF16)
+                        )
+            back = mm(t3t_ref[0:rows, 0:288], jnp.concatenate(pieces, 0))
             for which in range(2):
-                grad = join_z(back, rows, which, low, high) * slope
-                e2[pair + half, pl.ds(to, rows), which * NZ : which * NZ + NZ] = grad.astype(BF16)
+                lanes = slice(which * NZ, which * NZ + NZ)
+                e2[pair + half, pl.ds(to, rows), lanes] = (back[:, lanes] * slope).astype(BF16)
 
     def second_step(step, carry):
         pair = 2 * step
@@ -418,9 +420,9 @@
         second_block(pair, 16, 384, 96)
         return carry
 
-    lax.fori_loop(0, 3, second_step, 0)
-    clear(a2, 6, -2, 48, 432)
-    clear(e2, 6, -2, 48, 432)
+    lax.fori_loop(0, 3, second_step, 0, unroll=3)
+    clear(a2, 6, 48, 432)
+    clear(e2, 6, 48, 432)
 
     def third_block(plane, to, rows):
         stacked = jnp.concatenate([e2[plane + dx, pl.ds(to, 256)] for dx in range(3)], 0)
@@ -438,10 +440,10 @@
             third_block(plane, 384, 48)
         return carry
 
-    lax.fori_loop(0, 2, third_step, 0)
+    lax.fori_loop(0, 2, third_step, 0, unroll=2)
     for j in range(4):
         e1[j, 432:448] = jnp.zeros((16, 2 * NZ), BF16)
-    clear(e1, 4, -1, 24, 408)
+    clear(e1, 4, 24, 408)
 
     low, high = at_edges(16)
     for block in range(2):
@@ -468,7 +470,7 @@
                 for ch in range(2):
                     pair_ref[p, 2 * which + ch, rows] = grad[8 * ch : 8 * ch + 8]
         for ch in range(4):
-            pulled = cots[3 + p, ch, 3 : 3 + HALF] + pair_ref[p, ch]
+            pulled = cots[1, 3 + p, ch, 3 : 3 + HALF] + pair_ref[p, ch]
             pulled = pulled.astype(BF16)
             for dest in range(8):
                 send_ref[2 * dest + p, ch] = pulled
@@ -557,7 +559,7 @@
             jax.ShapeDtypeStruct((48, NZ), BF16),
             jax.ShapeDtypeStruct((1536, 256), BF16),
             jax.ShapeDtypeStruct((8, 2, NYL, NZ), BF16),
-            jax.ShapeDtypeStruct((1248, 896), BF16),
+            jax.ShapeDtypeStruct((1248, 1152), BF16),
         ],
         in_specs=[pl.BlockSpec(memory_space=pltpu.HBM)] * 10,
         out_specs=whole(8),
@@ -615,8 +617,8 @@
         out_specs=whole(3),
         scratch_shapes=[
             pltpu.VMEM((2, 6, HALF, NZ), F32),
-            pltpu.VMEM((10, 2, 32, NZ), F32),
-            pltpu.VMEM((8, 4, 32, NZ), F32),
+            pltpu.VMEM((3, 10, 2, 32, NZ), F32),
+            pltpu.VMEM((3, 8, 4, 32, NZ), F32),
             pltpu.VMEM((8, 640, NZ), BF16),
             pltpu.VMEM((8, 640, NZ), F32),
             pltpu.VMEM((6, 480, NZ), BF16),

time: 82.2 us -> 79.1 us (0.962)
  Pallas kernels: 17.9 us -> 14.8 us
    pallas_call x1, Pallas kernels: 9.6 us -> 6.4 us  [on_device(): pl.pallas_call(denoise_kernel, compiler_params=GRANT, out_shape=[jax.Shap...]
where the time goes in v5:
time: 79.1 us; the launch traced here: 78.7 us
  blocking collectives  52.4 us (66%)
  Pallas kernels  14.8 us (19%)
  waiting for transfers between devices  7.22 us (9%)
  starting transfers between devices  3.6 us (5%)
    all_to_all x1, blocking collectives, on_device(): planes = lax.all_to_all(payload, 'slab', 0, 0)  20.5 us
    all_to_all x1, blocking collectives, on_device(): field = lax.all_to_all(first, 'coil', 0, 0)  11.9 us
    all_to_all x1, blocking collectives, on_device(): lax.all_to_all(send, ('coil', 'slab'), 0, 0, axis_index_groups=families)  10.4 us
    all_to_all x1, blocking collectives, on_device(): got = lax.all_to_all(partial_sums, 'coil', 0, 0)  9.64 us
    pallas_call x1, Pallas kernels, on_device(): pl.pallas_call(denoise_kernel, compiler_params=GRANT, out_shape=[jax.Shap...  6.4 us
    all_to_all x1, waiting for transfers between devices, on_device(): back = lax.all_to_all(back, 'coil', 0, 0)  6.11 us
    pallas_call x1, Pallas kernels, on_device(): pl.pallas_call(normal_kernel, compiler_params=GRANT, out_shape=jax.ShapeD...  3.64 us
    all_to_all x1, starting transfers between devices, on_device(): back = lax.all_to_all(back, 'coil', 0, 0)  3.41 us
  transfers between devices with their start and end apart: 2, of which 2 were waited for; matrix products, arithmetic and copies ran while one was open for 0% of the time, Pallas kernels for 0%

profile of v5, /device:TPU:0, one launch (start us, length us, event | category | flops | bytes accessed | tf_op | source)
XLA Modules:
  0.0 78.7 jit_solution(6674352656446835185)
XLA Ops:
  0.6 2.3 %shard_map.130 = (f32[2,256,128]{2,1,0:T(8,128)S(1)}, f32[2,256,128]{2,1,0:T(8,128)S(1)}, f32[256,128]{1,0:T(8,128)S(1)}, f32[6,32,128]{2,1,0:T(8,128)S(1)}, bf1...) custom-call(f32[2,256,128]{2,1,0:T(8,128)} %bitcast.25, ...), custom_call_target="tpu_custom_call" | custom-call | tf_op jit(solution)/shard_map/pallas_call | solution.py:551
  2.9 11.9 %all_to_all.25.field_ref = bf16[8,2,32,128]{3,2,1,0:T(8,128)(2,1)S(1)} all-to-all(bf16[8,2,32,128]{3,2,1,0:T(8,128)(2,1)S(1)} %get-tuple-element.19), channel_id=1, replica_groups=mesh['coil'=8,'slab'=16] {'coil'}, dimensions={0} | all-to-all | bytes 262144 | tf_op jit(solution)/shard_map/all_to_all | solution.py:583
  14.8 1.7 %shard_map.131 = bf16[8,128,128]{2,1,0:T(8,128)(2,1)S(1)} custom-call(bf16[8,2,32,128]{3,2,1,0:T(8,128)(2,1)S(1)} %all_to_all.25.field_ref, f32[2,256,128]{2,1,0:T(8,128)S(1)} %get-tuple-element.20.maps_ref, f32[2,256,128]{2,1,0:T(8,128)S(1)} %get-tuple-element.21.masked_ref, f32[256,128]{1,0:T(8,128)S(1)} %get-tuple-element.22.weight_ref, ...), custom_call_target="tpu_custom_call" | custom-call | tf_op jit(solution)/shard_map/pallas_call | solution.py:584
  16.5 9.6 %all_to_all.26.got_ref = bf16[8,128,128]{2,1,0:T(8,128)(2,1)S(1)} all-to-all(bf16[8,128,128]{2,1,0:T(8,128)(2,1)S(1)} %shard_map.131), channel_id=1, replica_groups=mesh['coil'=8,'slab'=16] {'coil'}, dimensions={0} | all-to-all | bytes 524288 | tf_op jit(solution)/shard_map/all_to_all | solution.py:592
  26.2 0.1 shard_map.132
  26.3 20.5 %all_to_all.27.planes_ref = bf16[16,6,24,128]{3,2,1,0:T(8,128)(2,1)S(1)} all-to-all(bf16[16,6,24,128]{3,2,1,0:T(8,128)(2,1)S(1)} %get-tuple-element.26), channel_id=1, replica_groups=mesh['coil'=8,'slab'=16] {'slab'}, dimensions={0} | all-to-all | bytes 1179648 | tf_op jit(solution)/shard_map/all_to_all | solution.py:607
  46.7 0.0 copy-start
  46.8 6.4 %shard_map.133 = (bf16[16,4,16,128]{3,2,1,0:T(8,128)(2,1)S(1)}, f32[6,16,128]{2,1,0:T(8,128)S(1)}, f32[6,16,128]{2,1,0:T(8,128)S(1)}) custom-call(bf16[16,6,24,128]{3,2,1,0:T(8,128)(2,1)S(1)} %all_to_all.27.planes_ref, bf16[1248,1152]{1,0:T(8,128)(2,1)S(1)} %get-tuple-element.27.all_ref), custom_call_target="tpu_custom_call" | custom-call | tf_op jit(solution)/shard_map/pallas_call | solution.py:608
  53.2 10.4 %all_to_all.28.field_ref = bf16[16,4,16,128]{3,2,1,0:T(8,128)(2,1)S(1)} all-to-all(bf16[16,4,16,128]{3,2,1,0:T(8,128)(2,1)S(1)} %get-tuple-element.28), channel_id=1, replica_groups={{0,1,16,17,32,33,48,49,64,65,80,81,96,97,112,113},{2,3,18,19,34,35,50,5..., dimensions={0} | all-to-all | bytes 524288 | tf_op jit(solution)/shard_map/all_to_all | solution.py:629
  63.5 3.6 %shard_map.134 = bf16[8,4,32,128]{3,2,1,0:T(8,128)(2,1)} custom-call(bf16[16,4,16,128]{3,2,1,0:T(8,128)(2,1)S(1)} %all_to_all.28.field_ref, f32[2,256,128]{2,1,0:T(8,128)S(1)} %get-tuple-element.20.maps_ref, f32[256,128]{1,0:T(8,128)S(1)} %get-tuple-element.22.weight_ref, bf16[1536,256]{1,0:T(8,128)(2,1)S(1)} %get-tuple-element.24.tab_ref), custom_call_target="tpu_custom_call" | custom-call | tf_op jit(solution)/shard_map/pallas_call | solution.py:631
  67.2 3.4 %all-to-all-start.4 = ((bf16[8,4,32,128]{3,2,1,0:T(8,128)(2,1)}), bf16[8,4,32,128]{3,2,1,0:T(8,128)(2,1)S(1)}, u32[]{:S(2)}, u32[]{:S(2)}) async-start(bf16[8,4,32,128]{3,2,1,0:T(8,128)(2,1)} %shard_map.134), calls=%async_computation.4 | async-start | bytes 524288 | tf_op jit(solution)/shard_map/all_to_all | solution.py:638
  70.6 0.2 collective-permute-start
  70.8 1.1 %collective-permute-done.theirs_ref = f32[6,16,128]{2,1,0:T(8,128)S(1)} collective-permute-done((f32[6,16,128]{2,1,0:T(8,128)S(1)}, f32[6,16,128]{2,1,0:T(8,128)S(1)}, u32[]{:S(2)}, u32[]{:S(2)}) %collective-permute-start) | collective-permute-done | bytes 49184 | tf_op jit(solution)/shard_map/ppermute | solution.py:630
  71.9 6.1 %all-to-all-done.4.got_ref = bf16[8,4,32,128]{3,2,1,0:T(8,128)(2,1)S(1)} async-done(((bf16[8,4,32,128]{3,2,1,0:T(8,128)(2,1)}), bf16[8,4,32,128]{3,2,1,0:T(8,128)(2,1)S(1)}, u32[]{:S(2)}, u32[]{:S(2)}) %all-to-all-start.4) | async-done | bytes 262176 | tf_op jit(solution)/shard_map/all_to_all | solution.py:638
  78.0 0.0 copy-done
  78.0 0.7 shard_map.135
Async XLA Ops:
  46.7 31.3 %copy-start = (f32[2,1,32,128]{3,2,1,0:T(8,128)S(1)}, f32[2,1,32,128]{3,2,1,0:T(8,128)}, u32[]{:S(2)}) copy-start(f32[2,1,32,128]{3,2,1,0:T(8,128)} %param.16) | copy-start | bytes 98308
  67.2 10.8 %all-to-all-start.4 = ((bf16[8,4,32,128]{3,2,1,0:T(8,128)(2,1)}), bf16[8,4,32,128]{3,2,1,0:T(8,128)(2,1)S(1)}, u32[]{:S(2)}, u32[]{:S(2)}) async-start(bf16[8,4,32,128]{3,2,1,0:T(8,128)(2,1)} %shard_map.134), calls=%async_computation.4 | async-start | bytes 524288 | tf_op jit(solution)/shard_map/all_to_all | solution.py:638
  70.6 1.3 %collective-permute-start = (f32[6,16,128]{2,1,0:T(8,128)S(1)}, f32[6,16,128]{2,1,0:T(8,128)S(1)}, u32[]{:S(2)}, u32[]{:S(2)}) collective-permute-start(f32[6,16,128]{2,1,0:T(8,128)S(1)} %get-tuple-element.30), channel_id=1, source_target_pairs={{0,1},{1,0},{2,3},{3,2},{4,5},{5,4},{6,7},{7,6},{8,9},{9,8},{10,11... | collective-permute-start | bytes 147464 | tf_op jit(solution)/shard_map/ppermute | solution.py:630

commit v6 on v5

--- a/solution.py
+++ b/solution.py
@@ -17,6 +17,7 @@
 HALO_ROWS = 40
 HALF = 16
 PART_ROWS = 24
+MESSAGE = 136
 GRANT = pltpu.CompilerParams(vmem_limit_bytes=24 << 20)
 
 
@@ -168,7 +169,7 @@
         out_ref[dest, 80:128] = edges
 
 
-def relax_kernel(got_ref, field_ref, own_ref, out_ref, relaxed_ref, pad, qpad):
+def relax_kernel(got_ref, field_ref, own_ref, out_ref, relaxed_ref, pad, qpad, message):
     coil = lax.axis_index("coil")
     lower, upper = jnp.maximum(coil - 1, 0), jnp.minimum(coil + 1, 7)
     below = jnp.where(coil > 0, got_ref[lower, 80:128].astype(F32), 0.0)
@@ -186,19 +187,23 @@
             total = total + got_ref[source, rows].astype(F32)
         relaxed = pad[ch] - STEP * total
         relaxed_ref[ch] = relaxed[4 : 4 + NYL]
-        rows = relaxed.astype(BF16)
-        for dest in range(16):
-            first = HALF * (dest % 2)
-            out_ref[dest, ch] = rows[first : first + PART_ROWS]
+        for side in range(2):
+            first = HALF * side
+            message[side, PART_ROWS * ch : PART_ROWS * ch + PART_ROWS] = relaxed[
+                first : first + PART_ROWS
+            ]
     for ch in range(4):
         qpad[ch, 0:3] = below[ch * 8 + 5 : ch * 8 + 8]
         qpad[ch, 3 : 3 + NYL] = own_ref[2 + ch]
         qpad[ch, 3 + NYL : 7 + NYL] = above[ch * 8 : ch * 8 + 4]
-        qpad[ch, 7 + NYL : HALO_ROWS] = jnp.zeros((1, NZ), F32)
-        rows = qpad[ch].astype(BF16)
-        for dest in range(16):
-            first = HALF * (dest % 2)
-            out_ref[dest, 2 + ch] = rows[first : first + PART_ROWS]
+        for side in range(2):
+            first = HALF * side
+            at = 2 * PART_ROWS + 22 * ch
+            message[side, at : at + 22] = qpad[ch, first : first + 22]
+    for side in range(2):
+        rows = message[side].astype(BF16)
+        for dest in range(8):
+            out_ref[2 * dest + side] = rows
 
 
 def dot_first(left, right):
@@ -307,9 +312,10 @@
     low, high = at_edges(PART_ROWS)
 
     def stage(ref, j, ch, rows):
-        ref[0, j, ch, 0:PART_ROWS] = jnp.where(low, 0.0, pltpu.roll(rows, 1, 1))
-        ref[1, j, ch, 0:PART_ROWS] = rows
-        ref[2, j, ch, 0:PART_ROWS] = jnp.where(high, 0.0, pltpu.roll(rows, NZ - 1, 1))
+        count = rows.shape[0]
+        ref[0, j, ch, 0:count] = jnp.where(low[:count], 0.0, pltpu.roll(rows, 1, 1))
+        ref[1, j, ch, 0:count] = rows
+        ref[2, j, ch, 0:count] = jnp.where(high[:count], 0.0, pltpu.roll(rows, NZ - 1, 1))
         for dz in range(3):
             ref[dz, j, ch, PART_ROWS:32] = jnp.zeros((8, NZ), F32)
 
@@ -318,11 +324,15 @@
         keep = inside(plane)
         source = jnp.clip(plane, 0, 15)
         for ch in range(2):
-            stage(image, j, ch, jnp.where(keep, planes_ref[source, ch].astype(F32), 0.0))
+            rows = planes_ref[source, PART_ROWS * ch : PART_ROWS * ch + PART_ROWS].astype(F32)
+            stage(image, j, ch, jnp.where(keep, rows, 0.0))
         if 1 <= j < 9:
             for ch in range(4):
-                rows = jnp.where(keep, planes_ref[source, 2 + ch].astype(F32), 0.0)
-                stage(cots, j - 1, ch, rows)
+                at = 2 * PART_ROWS + 22 * ch
+                rows = planes_ref[source, at : at + 22].astype(F32)
+                for dz in range(3):
+                    cots[dz, j - 1, ch, 16:24] = jnp.zeros((8, NZ), F32)
+                stage(cots, j - 1, ch, jnp.where(keep, rows, 0.0))
 
     def usable(plane):
         return jnp.where(inside(plane), 1.0, 0.0)
@@ -481,11 +491,44 @@
 def normal_kernel(field_ref, maps_ref, weight_ref, tab_ref, out_ref):
     weight = weight_ref[...]
     map_re, map_im = maps_ref[0], maps_ref[1]
+
+    def over_z(rows):
+        rows = rows.astype(BF16)
+        return mm(rows, tab_ref[1024:1280]) + mm(rows, tab_ref[1280:1536])
+
+    def over_y(columns):
+        columns = columns.astype(BF16)
+        return mm(tab_ref[0:512], columns) + mm(tab_ref[512:1024], columns)
+
+    rows = []
     for which in range(2):
         re = field_ref[:, 2 * which].reshape(NY, NZ).astype(F32)
         im = field_ref[:, 2 * which + 1].reshape(NY, NZ).astype(F32)
-        f_re, f_im = forward(map_re * re - map_im * im, map_re * im + map_im * re, tab_ref)
-        b_re, b_im = inverse(weight * f_re, weight * f_im, tab_ref)
+        rows.append(
+            jnp.concatenate([map_re * re - map_im * im, map_re * im + map_im * re], 1)
+        )
+    turned = over_z(jnp.concatenate(rows, 0))
+    turned = over_y(jnp.concatenate([turned[:NY], turned[NY:]], 1))
+    columns = []
+    for which in range(2):
+        at = 2 * NZ * which
+        cos_part, sin_part = turned[:NY, at : at + 2 * NZ], turned[NY:, at : at + 2 * NZ]
+        columns.append(weight * (cos_part[:, :NZ] + sin_part[:, NZ:]))
+        columns.append(weight * (cos_part[:, NZ:] - sin_part[:, :NZ]))
+    turned = over_y(jnp.concatenate(columns, 1))
+    rows = []
+    for which in range(2):
+        at = 2 * NZ * which
+        cos_part, sin_part = turned[:NY, at : at + 2 * NZ], turned[NY:, at : at + 2 * NZ]
+        rows.append(
+            jnp.concatenate(
+                [cos_part[:, :NZ] - sin_part[:, NZ:], -(cos_part[:, NZ:] + sin_part[:, :NZ])], 1
+            )
+        )
+    turned = over_z(jnp.concatenate(rows, 0))
+    for which in range(2):
+        back = turned[NY * which : NY * which + NY]
+        b_re, b_im = back[:, :NZ], -back[:, NZ:]
         out_re = (map_re * b_re + map_im * b_im).astype(BF16)
         out_im = (map_re * b_im - map_im * b_re).astype(BF16)
         for dest in range(8):
@@ -594,7 +637,7 @@
         relax_kernel,
         compiler_params=GRANT,
         out_shape=[
-            jax.ShapeDtypeStruct((16, 6, PART_ROWS, NZ), BF16),
+            jax.ShapeDtypeStruct((16, MESSAGE, NZ), BF16),
             jax.ShapeDtypeStruct((2, NYL, NZ), F32),
         ],
         in_specs=whole(3),
@@ -602,6 +645,7 @@
         scratch_shapes=[
             pltpu.VMEM((2, HALO_ROWS, NZ), F32),
             pltpu.VMEM((4, HALO_ROWS, NZ), F32),
+            pltpu.VMEM((2, MESSAGE, NZ), F32),
         ],
     )(got, field, own)
     planes = lax.all_to_all(payload, "slab", 0, 0)

time: 79.1 us -> 77.8 us (0.984)
  Pallas kernels: 14.8 us -> 13.7 us
    pallas_call x1, Pallas kernels: 3.64 us -> 2.5 us  [on_device(): pl.pallas_call(normal_kernel, compiler_params=GRANT, out_shape=jax.ShapeD...]
where the time goes in v6:
time: 77.8 us; the launch traced here: 77.4 us
  blocking collectives  52.2 us (67%)
  Pallas kernels  13.7 us (18%)
  waiting for transfers between devices  7.22 us (9%)
  starting transfers between devices  3.6 us (5%)
    all_to_all x1, blocking collectives, on_device(): planes = lax.all_to_all(payload, 'slab', 0, 0)  20.3 us
    all_to_all x1, blocking collectives, on_device(): field = lax.all_to_all(first, 'coil', 0, 0)  11.9 us
    all_to_all x1, blocking collectives, on_device(): lax.all_to_all(send, ('coil', 'slab'), 0, 0, axis_index_groups=families)  10.4 us
    all_to_all x1, blocking collectives, on_device(): got = lax.all_to_all(partial_sums, 'coil', 0, 0)  9.64 us
    pallas_call x1, Pallas kernels, on_device(): pl.pallas_call(denoise_kernel, compiler_params=GRANT, out_shape=[jax.Shap...  6.46 us
    all_to_all x1, waiting for transfers between devices, on_device(): back = lax.all_to_all(back, 'coil', 0, 0)  6.11 us
    all_to_all x1, starting transfers between devices, on_device(): back = lax.all_to_all(back, 'coil', 0, 0)  3.41 us
    pallas_call x1, Pallas kernels, on_device(): pl.pallas_call(normal_kernel, compiler_params=GRANT, out_shape=jax.ShapeD...  2.5 us
  transfers between devices with their start and end apart: 2, of which 2 were waited for; matrix products, arithmetic and copies ran while one was open for 0% of the time, Pallas kernels for 0%

profile of v6, /device:TPU:0, one launch (start us, length us, event | category | flops | bytes accessed | tf_op | source)
XLA Modules:
  0.0 77.4 jit_solution(11270271474031759958)
XLA Ops:
  0.6 2.3 %shard_map.130 = (f32[2,256,128]{2,1,0:T(8,128)S(1)}, f32[2,256,128]{2,1,0:T(8,128)S(1)}, f32[256,128]{1,0:T(8,128)S(1)}, f32[6,32,128]{2,1,0:T(8,128)S(1)}, bf1...) custom-call(f32[2,256,128]{2,1,0:T(8,128)} %bitcast.25, ...), custom_call_target="tpu_custom_call" | custom-call | tf_op jit(solution)/shard_map/pallas_call | solution.py:594
  2.9 11.9 %all_to_all.25.field_ref = bf16[8,2,32,128]{3,2,1,0:T(8,128)(2,1)S(1)} all-to-all(bf16[8,2,32,128]{3,2,1,0:T(8,128)(2,1)S(1)} %get-tuple-element.19), channel_id=1, replica_groups=mesh['coil'=8,'slab'=16] {'coil'}, dimensions={0} | all-to-all | bytes 262144 | tf_op jit(solution)/shard_map/all_to_all | solution.py:626
  14.8 1.7 %shard_map.131 = bf16[8,128,128]{2,1,0:T(8,128)(2,1)S(1)} custom-call(bf16[8,2,32,128]{3,2,1,0:T(8,128)(2,1)S(1)} %all_to_all.25.field_ref, f32[2,256,128]{2,1,0:T(8,128)S(1)} %get-tuple-element.20.maps_ref, f32[2,256,128]{2,1,0:T(8,128)S(1)} %get-tuple-element.21.masked_ref, f32[256,128]{1,0:T(8,128)S(1)} %get-tuple-element.22.weight_ref, ...), custom_call_target="tpu_custom_call" | custom-call | tf_op jit(solution)/shard_map/pallas_call | solution.py:627
  16.5 9.6 %all_to_all.26.got_ref = bf16[8,128,128]{2,1,0:T(8,128)(2,1)S(1)} all-to-all(bf16[8,128,128]{2,1,0:T(8,128)(2,1)S(1)} %shard_map.131), channel_id=1, replica_groups=mesh['coil'=8,'slab'=16] {'coil'}, dimensions={0} | all-to-all | bytes 524288 | tf_op jit(solution)/shard_map/all_to_all | solution.py:635
  26.2 0.1 shard_map.132
  26.3 20.3 %all_to_all.27.planes_ref = bf16[16,136,128]{2,1,0:T(8,128)(2,1)S(1)} all-to-all(bf16[16,136,128]{2,1,0:T(8,128)(2,1)S(1)} %get-tuple-element.26), channel_id=1, replica_groups=mesh['coil'=8,'slab'=16] {'slab'}, dimensions={0} | all-to-all | bytes 1114112 | tf_op jit(solution)/shard_map/all_to_all | solution.py:651
  46.5 0.0 copy-start
  46.5 6.5 %shard_map.133 = (bf16[16,4,16,128]{3,2,1,0:T(8,128)(2,1)S(1)}, f32[6,16,128]{2,1,0:T(8,128)S(1)}, f32[6,16,128]{2,1,0:T(8,128)S(1)}) custom-call(bf16[16,136,128]{2,1,0:T(8,128)(2,1)S(1)} %all_to_all.27.planes_ref, bf16[1248,1152]{1,0:T(8,128)(2,1)S(1)} %get-tuple-element.27.all_ref), custom_call_target="tpu_custom_call" | custom-call | tf_op jit(solution)/shard_map/pallas_call | solution.py:652
  53.0 10.4 %all_to_all.28.field_ref = bf16[16,4,16,128]{3,2,1,0:T(8,128)(2,1)S(1)} all-to-all(bf16[16,4,16,128]{3,2,1,0:T(8,128)(2,1)S(1)} %get-tuple-element.28), channel_id=1, replica_groups={{0,1,16,17,32,33,48,49,64,65,80,81,96,97,112,113},{2,3,18,19,34,35,50,5..., dimensions={0} | all-to-all | bytes 524288 | tf_op jit(solution)/shard_map/all_to_all | solution.py:673
  63.4 2.5 %shard_map.134 = bf16[8,4,32,128]{3,2,1,0:T(8,128)(2,1)} custom-call(bf16[16,4,16,128]{3,2,1,0:T(8,128)(2,1)S(1)} %all_to_all.28.field_ref, f32[2,256,128]{2,1,0:T(8,128)S(1)} %get-tuple-element.20.maps_ref, f32[256,128]{1,0:T(8,128)S(1)} %get-tuple-element.22.weight_ref, bf16[1536,256]{1,0:T(8,128)(2,1)S(1)} %get-tuple-element.24.tab_ref), custom_call_target="tpu_custom_call" | custom-call | tf_op jit(solution)/shard_map/pallas_call | solution.py:675
  65.9 3.4 %all-to-all-start.4 = ((bf16[8,4,32,128]{3,2,1,0:T(8,128)(2,1)}), bf16[8,4,32,128]{3,2,1,0:T(8,128)(2,1)S(1)}, u32[]{:S(2)}, u32[]{:S(2)}) async-start(bf16[8,4,32,128]{3,2,1,0:T(8,128)(2,1)} %shard_map.134), calls=%async_computation.4 | async-start | bytes 524288 | tf_op jit(solution)/shard_map/all_to_all | solution.py:682
  69.3 0.2 collective-permute-start
  69.5 1.1 %collective-permute-done.theirs_ref = f32[6,16,128]{2,1,0:T(8,128)S(1)} collective-permute-done((f32[6,16,128]{2,1,0:T(8,128)S(1)}, f32[6,16,128]{2,1,0:T(8,128)S(1)}, u32[]{:S(2)}, u32[]{:S(2)}) %collective-permute-start) | collective-permute-done | bytes 49184 | tf_op jit(solution)/shard_map/ppermute | solution.py:674
  70.6 6.1 %all-to-all-done.4.got_ref = bf16[8,4,32,128]{3,2,1,0:T(8,128)(2,1)S(1)} async-done(((bf16[8,4,32,128]{3,2,1,0:T(8,128)(2,1)}), bf16[8,4,32,128]{3,2,1,0:T(8,128)(2,1)S(1)}, u32[]{:S(2)}, u32[]{:S(2)}) %all-to-all-start.4) | async-done | bytes 262176 | tf_op jit(solution)/shard_map/all_to_all | solution.py:682
  76.7 0.0 copy-done
  76.7 0.7 shard_map.135
Async XLA Ops:
  46.5 30.2 %copy-start = (f32[2,1,32,128]{3,2,1,0:T(8,128)S(1)}, f32[2,1,32,128]{3,2,1,0:T(8,128)}, u32[]{:S(2)}) copy-start(f32[2,1,32,128]{3,2,1,0:T(8,128)} %param.16) | copy-start | bytes 98308
  65.9 10.8 %all-to-all-start.4 = ((bf16[8,4,32,128]{3,2,1,0:T(8,128)(2,1)}), bf16[8,4,32,128]{3,2,1,0:T(8,128)(2,1)S(1)}, u32[]{:S(2)}, u32[]{:S(2)}) async-start(bf16[8,4,32,128]{3,2,1,0:T(8,128)(2,1)} %shard_map.134), calls=%async_computation.4 | async-start | bytes 524288 | tf_op jit(solution)/shard_map/all_to_all | solution.py:682
  69.3 1.3 %collective-permute-start = (f32[6,16,128]{2,1,0:T(8,128)S(1)}, f32[6,16,128]{2,1,0:T(8,128)S(1)}, u32[]{:S(2)}, u32[]{:S(2)}) collective-permute-start(f32[6,16,128]{2,1,0:T(8,128)S(1)} %get-tuple-element.30), channel_id=1, source_target_pairs={{0,1},{1,0},{2,3},{3,2},{4,5},{5,4},{6,7},{7,6},{8,9},{9,8},{10,11... | collective-permute-start | bytes 147464 | tf_op jit(solution)/shard_map/ppermute | solution.py:674
